TPU v7x, 32 devices: a whole 2x2x4 slice. The times are simulated.
32 devices in a mesh: dp: 16 (over z, y, x), seq: 2 (over core).
Axes of the slice: x: 2, y: 2, z: 4, core: 2. Of those that a mesh axis runs over, the one named last changes fastest.
Arguments:
- tokens: bfloat16 [64, 256, 384], P('dp', 'seq'), may hold values from -6 to 6
- cotangent: bfloat16 [64, 256, 384], P('dp', 'seq'), may hold values from -6 to 6
- cond: bfloat16 [32, 384], P('dp'), may hold values from -6 to 6
- group_ids: int32 [64], P('dp'), may hold values from 0 to 31
- image_counts: int32 [16], P('dp'), may hold values from 1 to 4, as said below
- patch_mask: int32 [64, 256], P('dp'), may hold values 0 or 1
- qkv_weight: bfloat16 [384, 1152], replicated, may hold values from -0.3125 to 0.3125
- qv_bias: bfloat16 [2, 384], replicated, may hold values from -1.796875 to 1.796875
- out_weight: bfloat16 [384, 384], replicated, may hold values from -1.75 to 1.75
- out_bias: bfloat16 [384], replicated, may hold values from -1.796875 to 1.796875
- up_weight: bfloat16 [384, 1536], replicated, may hold values from -0.3125 to 0.3125
- up_bias: bfloat16 [1536], replicated, may hold values from -1.796875 to 1.796875
- down_weight: bfloat16 [1536, 384], replicated, may hold values from -0.15625 to 0.15625
- down_bias: bfloat16 [384], replicated, may hold values from -1.796875 to 1.796875
- ada_weight: bfloat16 [384, 2304], replicated, may hold values from -0.3125 to 0.3125
- ada_bias: bfloat16 [2304], replicated, may hold values from -1.796875 to 1.796875
Outputs:
- output: bfloat16 [64, 256, 384], P('dp', 'seq')
- grad_tokens: bfloat16 [64, 256, 384], P('dp', 'seq')
- grad_cond: float32 [32, 384], P('dp', 'seq')
- grad_qkv_weight: float32 [384, 1152], P('dp', 'seq')
- grad_qv_bias: float32 [2, 384], replicated
- grad_out_weight: float32 [384, 384], P('dp', 'seq')
- grad_out_bias: float32 [384], replicated
- grad_up_weight: float32 [384, 1536], P('dp', 'seq')
- grad_up_bias: float32 [1536], replicated
- grad_down_weight: float32 [1536, 384], P('dp', 'seq')
- grad_down_bias: float32 [384], replicated
- grad_ada_weight: float32 [384, 2304], P('dp', 'seq')
- grad_ada_bias: float32 [2304], replicated
Inputs may be any that keep to these rules, and one draw needn't show every extreme that they name: `image_counts`: some index of dp holds 4 images and another holds one.
All inputs are finite; a program needn't handle non-finite values. No bound on the sum of `patch_mask` on one device may be relied on, other than what follows from the above.
Results may differ from a plain program's by a relative error of at most 0.012.
The roundings to bfloat16 on the way count: a program that leaves them out, or rounds other values in their place, can miss the bound.
Values may be sent and summed in bfloat16 or wider, within the bound.
No kernel may reach another device: no remote copies, remote signals or barrier semaphores. Data moves between devices by JAX's collectives and lax.ppermute only.
A program may use at most 320 MiB of HBM per device.

v0:
```python
from functools import partial

import jax
import jax.numpy as jnp
from jax import lax
from jax.sharding import PartitionSpec as P

HEADS = 6
HEAD_DIM = 64


def layer_norm(values):
    center = values - jnp.mean(values, axis=-1, keepdims=True)
    spread = jnp.mean(center * center, axis=-1, keepdims=True)
    return center * lax.rsqrt(spread + 1e-06)


def modulate(values, scale_part, shift_part):
    return layer_norm(values) * (1.0 + scale_part) + shift_part


def silu_slope(values):
    sigmoid_val = jax.nn.sigmoid(values)
    return sigmoid_val * (1.0 + values * (1.0 - sigmoid_val))


def blocked(local_term, dp_count, seq_count):
    row_count, col_count = local_term.shape
    blocks_view = local_term.reshape(
        dp_count, row_count // dp_count, seq_count, col_count // seq_count
    )
    return blocks_view.transpose(0, 2, 1, 3).reshape(
        dp_count * seq_count * (row_count // dp_count), col_count // seq_count
    )


def by_owner(group_table, dp_count, seq_count):
    group_count, col_count = group_table.shape
    per_rank = group_count // dp_count
    blocks_view = group_table.reshape(dp_count, per_rank, seq_count, col_count // seq_count)
    return blocks_view.transpose(1, 0, 2, 3).reshape(
        per_rank, dp_count * seq_count * (col_count // seq_count)
    )


def body(
    tokens,
    cotangent,
    cond,
    group_ids,
    image_counts,
    patch_mask,
    qkv_weight,
    qv_bias,
    out_weight,
    out_bias,
    up_weight,
    up_bias,
    down_weight,
    down_bias,
    ada_weight,
    ada_bias,
):
    highest = lax.Precision.HIGHEST
    slot_count, half_len, feat_width = tokens.shape
    dp_count = lax.axis_size("dp")
    seq_count = lax.axis_size("seq")
    seq_rank = lax.axis_index("seq")
    full_len = half_len * seq_count
    local_heads = HEADS // seq_count
    group_count = cond.shape[0] * dp_count
    inv_root = HEAD_DIM ** (-0.5)
    live_slots = (jnp.arange(slot_count, dtype=jnp.int32) < image_counts[0]).astype(jnp.float32)
    valid_full = patch_mask.astype(jnp.float32) * live_slots[:, None]
    valid_rows = lax.dynamic_slice_in_dim(valid_full, seq_rank * half_len, half_len, 1)[:, :, None]
    key_penalty = ((valid_full - 1.0) * 30000.0)[:, None, None, :]
    one_hot = (group_ids[:, None] == jnp.arange(group_count, dtype=jnp.int32)[None, :]).astype(
        jnp.float32
    )
    own_cond = cond.astype(jnp.float32)
    own_silu = jax.nn.silu(own_cond).astype(jnp.bfloat16)
    own_mod = (
        jnp.dot(own_silu, ada_weight, preferred_element_type=jnp.float32)
        + ada_bias.astype(jnp.float32)
    ).astype(jnp.bfloat16)
    mod_rows = lax.all_gather(own_mod, "dp", axis=0, tiled=True)
    image_mod = jnp.take(mod_rows, group_ids, axis=0)
    pieces = image_mod.astype(jnp.float32).reshape(slot_count, 6, 1, feat_width)
    shift_one, scale_one, gate_one = (pieces[:, 0], pieces[:, 1], pieces[:, 2])
    shift_two, scale_two, gate_two = (pieces[:, 3], pieces[:, 4], pieces[:, 5])
    residual_in = tokens.astype(jnp.float32)
    normed_one = modulate(residual_in, scale_one, shift_one).astype(jnp.bfloat16)
    proj_bias = jnp.concatenate([qv_bias[0], jnp.zeros_like(qv_bias[0]), qv_bias[1]]).astype(
        jnp.float32
    )
    projected = (
        jnp.einsum("tpd,de->tpe", normed_one, qkv_weight, preferred_element_type=jnp.float32)
        + proj_bias
    ).astype(jnp.bfloat16)
    head_major = lax.all_to_all(
        projected.reshape(slot_count, half_len, 3, seq_count, -1),
        "seq",
        split_axis=3,
        concat_axis=1,
        tiled=True,
    )
    head_major = head_major.reshape(slot_count, full_len, 3, local_heads, HEAD_DIM)
    queries = head_major[:, :, 0]
    keys_all = head_major[:, :, 1]
    values_all = head_major[:, :, 2]

    def scores_of():
        return (
            jnp.einsum("bqhd,bkhd->bhqk", queries, keys_all, preferred_element_type=jnp.float32)
            * inv_root
            + key_penalty
        )

    scores = scores_of()
    row_max = jnp.max(scores, axis=-1, keepdims=True)
    exp_scores = jnp.exp(scores - row_max)
    exp_total = jnp.sum(exp_scores, axis=-1, keepdims=True)
    probs = exp_scores / exp_total
    log_total = row_max + jnp.log(exp_total)
    attended = jnp.einsum(
        "bhqk,bkhd->bqhd",
        probs.astype(jnp.bfloat16),
        values_all,
        preferred_element_type=jnp.float32,
    ).astype(jnp.bfloat16)
    token_major = lax.all_to_all(
        attended.reshape(slot_count, full_len, 1, -1),
        "seq",
        split_axis=1,
        concat_axis=2,
        tiled=True,
    )
    attended_tok = token_major.reshape(slot_count, half_len, feat_width)
    attn_out = jnp.einsum(
        "tpd,de->tpe", attended_tok, out_weight, preferred_element_type=jnp.float32
    ) + out_bias.astype(jnp.float32)
    middle = residual_in + valid_rows * gate_one * attn_out
    normed_two = modulate(middle, scale_two, shift_two).astype(jnp.bfloat16)
    pre_act = jnp.einsum(
        "tpd,df->tpf", normed_two, up_weight, preferred_element_type=jnp.float32
    ) + up_bias.astype(jnp.float32)
    hidden = jax.nn.gelu(pre_act, approximate=True).astype(jnp.bfloat16)
    ffn_out = jnp.einsum(
        "tpf,fd->tpd", hidden, down_weight, preferred_element_type=jnp.float32
    ) + down_bias.astype(jnp.float32)
    output = (middle + valid_rows * gate_two * ffn_out).astype(jnp.bfloat16)
    upstream = cotangent.astype(jnp.float32)
    grad_ffn = (valid_rows * gate_two * upstream).astype(jnp.bfloat16)
    gate_two_grad = jnp.sum(valid_rows * ffn_out * upstream, axis=1)
    down_term = jnp.einsum("tpf,tpd->fd", hidden, grad_ffn, preferred_element_type=jnp.float32)
    down_bias_grad = jnp.sum(grad_ffn.astype(jnp.float32), axis=(0, 1))
    grad_hidden = jnp.einsum(
        "tpd,fd->tpf", grad_ffn, down_weight, preferred_element_type=jnp.float32
    )
    gelu_pull = jax.vjp(partial(jax.nn.gelu, approximate=True), pre_act)[1]
    grad_pre = gelu_pull(grad_hidden)[0].astype(jnp.bfloat16)
    up_term = jnp.einsum("tpd,tpf->df", normed_two, grad_pre, preferred_element_type=jnp.float32)
    up_bias_grad = jnp.sum(grad_pre.astype(jnp.float32), axis=(0, 1))
    grad_normed_two = jnp.einsum(
        "tpf,df->tpd", grad_pre, up_weight, preferred_element_type=jnp.float32
    )
    mod_pull_two = jax.vjp(modulate, middle, scale_two, shift_two)[1]
    grad_middle_part, scale_two_grad, shift_two_grad = mod_pull_two(grad_normed_two)
    grad_middle = upstream + grad_middle_part
    grad_attn = (valid_rows * gate_one * grad_middle).astype(jnp.bfloat16)
    gate_one_grad = jnp.sum(valid_rows * attn_out * grad_middle, axis=1)
    out_term = jnp.einsum(
        "tpd,tpe->de", attended_tok, grad_attn, preferred_element_type=jnp.float32
    )
    out_bias_grad = jnp.sum(grad_attn.astype(jnp.float32), axis=(0, 1))
    grad_attended = jnp.einsum(
        "tpe,de->tpd", grad_attn, out_weight, preferred_element_type=jnp.float32
    ).astype(jnp.bfloat16)
    grad_heads = lax.all_to_all(
        grad_attended.reshape(slot_count, half_len, seq_count, -1),
        "seq",
        split_axis=2,
        concat_axis=1,
        tiled=True,
    )
    grad_heads = grad_heads.reshape(slot_count, full_len, local_heads, HEAD_DIM)
    probs_again = jnp.exp(scores_of() - log_total)
    probs_low = probs_again.astype(jnp.bfloat16)
    grad_values = jnp.einsum(
        "bhqk,bqhd->bkhd", probs_low, grad_heads, preferred_element_type=jnp.float32
    )
    grad_probs = jnp.einsum(
        "bqhd,bkhd->bhqk", grad_heads, values_all, preferred_element_type=jnp.float32
    )
    grad_scores = (
        probs_again * (grad_probs - jnp.sum(probs_again * grad_probs, axis=-1, keepdims=True))
    ).astype(jnp.bfloat16)
    grad_queries = (
        jnp.einsum("bhqk,bkhd->bqhd", grad_scores, keys_all, preferred_element_type=jnp.float32)
        * inv_root
    )
    grad_keys = (
        jnp.einsum("bhqk,bqhd->bkhd", grad_scores, queries, preferred_element_type=jnp.float32)
        * inv_root
    )
    grad_stack = jnp.stack([grad_queries, grad_keys, grad_values], axis=2).astype(jnp.bfloat16)
    grad_stack = grad_stack.reshape(slot_count, full_len, 3, 1, -1)
    grad_proj = lax.all_to_all(grad_stack, "seq", split_axis=1, concat_axis=3, tiled=True).reshape(
        slot_count, half_len, 3 * feat_width
    )
    qkv_term = jnp.einsum("tpd,tpe->de", normed_one, grad_proj, preferred_element_type=jnp.float32)
    proj_sums = jnp.sum(grad_proj.astype(jnp.float32), axis=(0, 1))
    qv_bias_grad = jnp.stack([proj_sums[:feat_width], proj_sums[2 * feat_width :]])
    grad_normed_one = jnp.einsum(
        "tpe,de->tpd", grad_proj, qkv_weight, preferred_element_type=jnp.float32
    )
    mod_pull_one = jax.vjp(modulate, residual_in, scale_one, shift_one)[1]
    grad_input_part, scale_one_grad, shift_one_grad = mod_pull_one(grad_normed_one)
    grad_tokens = (grad_middle + grad_input_part).astype(jnp.bfloat16)
    image_grad = jnp.concatenate(
        [
            shift_one_grad[:, 0],
            scale_one_grad[:, 0],
            gate_one_grad,
            shift_two_grad[:, 0],
            scale_two_grad[:, 0],
            gate_two_grad,
        ],
        axis=1,
    )
    group_grad = jnp.dot(one_hot.T, image_grad, precision=highest)
    own_grad = lax.psum_scatter(
        by_owner(group_grad, dp_count, seq_count), ("dp", "seq"), scatter_dimension=1, tiled=True
    )
    col_share = own_grad.shape[1]
    col_start = seq_rank * col_share
    ada_half = lax.dynamic_slice_in_dim(ada_weight, col_start, col_share, 1).astype(jnp.float32)
    own_term = jnp.dot(own_silu.astype(jnp.float32).T, own_grad, precision=highest)
    ada_term = lax.dynamic_update_slice(
        jnp.zeros((feat_width, 6 * feat_width), jnp.float32),
        own_term,
        (jnp.zeros((), jnp.int32), col_start),
    )
    ada_bias_grad = lax.dynamic_update_slice(
        jnp.zeros((6 * feat_width,), jnp.float32), jnp.sum(own_grad, axis=0), (col_start,)
    )
    cond_part = silu_slope(own_cond) * jnp.dot(own_grad, ada_half.T, precision=highest)
    grad_cond = lax.psum_scatter(cond_part, "seq", scatter_dimension=1, tiled=True)
    qkv_sum, out_sum, up_sum, down_sum, ada_sum = (
        lax.psum_scatter(
            blocked(qkv_term, dp_count, seq_count), ("dp", "seq"), scatter_dimension=0, tiled=True
        ),
        lax.psum_scatter(
            blocked(out_term, dp_count, seq_count), ("dp", "seq"), scatter_dimension=0, tiled=True
        ),
        lax.psum_scatter(
            blocked(up_term, dp_count, seq_count), ("dp", "seq"), scatter_dimension=0, tiled=True
        ),
        lax.psum_scatter(
            blocked(down_term, dp_count, seq_count), ("dp", "seq"), scatter_dimension=0, tiled=True
        ),
        lax.psum_scatter(
            blocked(ada_term, dp_count, seq_count), ("dp", "seq"), scatter_dimension=0, tiled=True
        ),
    )
    qv_sum, out_bias_sum, up_bias_sum, down_bias_sum, ada_bias_sum = lax.psum(
        (qv_bias_grad, out_bias_grad, up_bias_grad, down_bias_grad, ada_bias_grad), ("dp", "seq")
    )
    return (
        output,
        grad_tokens,
        grad_cond,
        qkv_sum,
        qv_sum,
        out_sum,
        out_bias_sum,
        up_sum,
        up_bias_sum,
        down_sum,
        down_bias_sum,
        ada_sum,
        ada_bias_sum,
    )


def solution(mesh):
    placed = (
        P("dp", "seq", None),
        P("dp", "seq", None),
        P("dp", None),
        P("dp"),
        P("dp"),
        P("dp", None),
        P(),
        P(),
        P(),
        P(),
        P(),
        P(),
        P(),
        P(),
        P(),
        P(),
    )
    return jax.shard_map(
        body,
        mesh=mesh,
        in_specs=placed,
        out_specs=(
            P("dp", "seq", None),
            P("dp", "seq", None),
            P("dp", "seq"),
            P("dp", "seq"),
            P(),
            P("dp", "seq"),
            P(),
            P("dp", "seq"),
            P(),
            P("dp", "seq"),
            P(),
            P("dp", "seq"),
            P(),
        ),
        check_vma=False,
    )
```

profile of v0, /device:TPU:0, one launch (start us, length us, event | category | flops | bytes accessed | tf_op | source)
XLA Modules:
  0.0 901.9 jit_solution(14020485514927090018)
XLA Ops:
  13.7 43.1 %all-gather = bf16[16,2,2304]{2,1,0:T(2,128)(2,1)S(1)} all-gather(bf16[1,2,2304]{2,1,0:T(2,128)(2,1)S(1)} %fusion.1), channel_id=1, replica_groups=mesh['dp'=16,'seq'=2] {'dp'}, dimensions={0}, use_global_device_ids=true | all-gather | bytes 156672 | tf_op jit(solution)/shard_map/all_gather | solution.py:86
  57.7 1.9 fusion.9
  62.4 3.7 all-to-all-start
  68.3 2.2 copy.162
  70.6 3.1 reshape.282
  76.5 2.1 copy.164
  78.6 4.4 all-to-all-start.1
  84.7 2.2 copy.206
  86.8 1.8 copy.166
  88.6 1.8 fusion.82
  92.1 2.8 convert_reduce_fusion
  96.6 2.5 convert_reduce_fusion.3
  100.9 1.9 copy.168
  102.8 1.8 copy.169
  104.6 4.2 all-to-all-start.2
  108.8 1.7 all-to-all-done.2
  110.5 2.1 copy.170
  112.7 2.0 reshape.286
  114.7 3.5 fusion.17
  124.8 2.1 copy.174
  126.9 2.2 pad_maximum_fusion
  129.1 5.8 all_to_all.60
  135.0 4.2 copy.207
  140.5 2.2 fusion.47
  145.3 1.8 reshape.288
  147.1 10.2 %copy.216 = f32[2,16,2,1152]{0,3,2,1:T(8,128)} copy(f32[2,16,2,1152]{3,2,0,1:T(2,128)} %bitcast.189) | data formatting | bytes 589824
  157.4 1.9 copy.186
  159.3 200.9 %reduce-scatter.22.cloned.1.call-done = f32[1152,2]{1,0:T(8,128)} async-done(((f32[36864,2]{1,0:T(8,128)}), f32[1152,2]{1,0:T(8,128)}) %reduce-scatter.22.cloned.1.call-update) | async-done | bytes 9232
  360.3 2.1 convolution_multiply_fusion.2
  363.3 2.4 fusion.52
  365.8 2.8 fusion.63
  369.9 3.3 fusion.26
  373.2 4.0 convolution_bitcast_fusion.1
  377.2 3.9 reshape.292
  381.1 3.3 copy.190
  384.5 4.8 convolution_bitcast_fusion
  389.2 5.3 reshape.294
  394.5 4.1 copy.192
  398.9 2.0 broadcast_in_dim.62
  400.9 3.3 convolution_dynamic-update-slice_fusion
  404.2 5.5 reshape.296
  409.7 4.0 copy.193
  416.8 39.9 %all-reduce.2 = (f32[2,384]{1,0:T(2,128)}, f32[384]{0:T(512)}, f32[1536]{0:T(1024)}, f32[384]{0:T(512)}, f32[2304]{0:T(1024)}) all-reduce(f32[2,384]{1,0:T(2,128)S(1)} %pad_maximum_fusion.1, f32[384]{0:T(512)S(1)} %get-tuple-element.37, f32[1536]{0:T(1024)S(1)} %get-tuple-element.58, ...), channel_id=1, replica_groups=mesh['dp'=16,'seq'=2] {'dp','seq'}, use_global_device_ids=true, to_apply=%region_21.22 | all-reduce | flops 5376 | bytes 43008 | tf_op jit(solution)/shard_map/psum | solution.py:266
  458.3 14.0 %reduce-scatter.16.cloned.1.call-done = f32[24,192]{1,0:T(8,128)} async-done(((f32[768,192]{1,0:T(8,128)}), f32[24,192]{1,0:T(8,128)}) %reduce-scatter.16.cloned.1.call-update) | async-done | bytes 18448 | tf_op jit(solution)/shard_map/reduce_scatter | solution.py:253
  472.3 102.8 %reduce-scatter.26.cloned.1.call-done = f32[24,576]{1,0:T(8,128)} async-done(((f32[768,576]{1,0:T(8,128)}), f32[24,576]{1,0:T(8,128)}) %reduce-scatter.26.cloned.1.call-update) | async-done | bytes 55312
  575.1 103.8 %reduce-scatter.18.cloned.1.call-done = f32[24,768]{1,0:T(8,128)} async-done(((f32[768,768]{1,0:T(8,128)}), f32[24,768]{1,0:T(8,128)}) %reduce-scatter.18.cloned.1.call-update) | async-done | bytes 73744 | tf_op jit(solution)/shard_map/reduce_scatter | solution.py:256
  678.9 107.3 %reduce-scatter.20.cloned.1.call-done = f32[96,192]{1,0:T(8,128)} async-done(((f32[3072,192]{1,0:T(8,128)}), f32[96,192]{1,0:T(8,128)}) %reduce-scatter.20.cloned.1.call-update) | async-done | bytes 73744 | tf_op jit(solution)/shard_map/reduce_scatter | solution.py:259
  786.2 108.8 %reduce-scatter.28.cloned.1.call-done = f32[24,1152]{1,0:T(8,128)} async-done(((f32[768,1152]{1,0:T(8,128)}), f32[24,1152]{1,0:T(8,128)}) %reduce-scatter.28.cloned.1.call-update) | async-done | bytes 110608
  (136 shorter events, 38.8 us)
Async XLA Ops:
  7.2 5.5 copy-start
  7.2 50.5 %copy-start.3 = (bf16[4,128,384]{2,1,0:T(8,128)(2,1)S(1)}, bf16[4,128,384]{2,1,0:T(8,128)(2,1)}, u32[]{:S(2)}) copy-start(bf16[4,128,384]{2,1,0:T(8,128)(2,1)} %param.16) | copy-start | bytes 1179652
  7.2 50.5 %copy-start.21 = (bf16[384,1152]{1,0:T(8,128)(2,1)S(1)}, bf16[384,1152]{1,0:T(8,128)(2,1)}, u32[]{:S(2)}) copy-start(bf16[384,1152]{1,0:T(8,128)(2,1)} %param.22) | copy-start | bytes 2654212
  62.4 11.3 %copy-start.14 = (s32[4,256]{1,0:T(4,128)S(1)}, s32[4,256]{1,0:T(4,128)}, u32[]{:S(2)}) copy-start(s32[4,256]{1,0:T(4,128)} %param.21) | copy-start | bytes 12292
  62.4 5.9 all-to-all-start
  74.6 1.9 copy-start.1
  75.0 8.0 copy-start.16
  75.0 8.0 copy-start.17
  75.0 8.0 copy-start.15
  78.6 6.1 all-to-all-start.1
  88.6 2.1 copy-start.19
  90.4 6.1 copy-start.4
  90.4 1.4 copy-start.11
  90.4 1.7 copy-start.20
  91.8 4.7 copy-start.22
  94.9 1.6 copy-start.23
  96.5 2.5 copy-start.8
  96.5 3.2 copy-start.10
  99.0 0.7 copy-start.9
  104.6 5.9 all-to-all-start.2
  108.8 251.5 %reduce-scatter.22.cloned.1.call-start = ((), (), s32[]{:S(2)}) async-start(), calls=%async_computation.14 | async-start | bytes 19464192
  114.7 3.5 copy-start.2
  114.7 3.5 copy-start.6
  139.2 4.9 copy-start.18
  139.5 1.0 copy-start.5
  142.7 0.9 copy-start.7
  157.4 202.9 %copy-start.13 = (bf16[2,384]{1,0:T(2,128)(2,1)S(1)}, bf16[2,384]{1,0:T(2,128)(2,1)}, u32[]{:S(2)}) copy-start(bf16[2,384]{1,0:T(2,128)(2,1)} %param.18) | copy-start | bytes 4612
  157.4 299.4 %reduce-scatter.24.cloned.1.call-start = ((), (), s32[]{:S(2)}) async-start(), calls=%async_computation.15 | async-start | bytes 294912
  363.3 109.1 %reduce-scatter.16.cloned.1.call-start = ((), (), s32[]{:S(2)}) async-start(), calls=%async_computation.11 | async-start | bytes 811008 | tf_op jit(solution)/shard_map/reduce_scatter | solution.py:253
  365.7 209.4 %reduce-scatter.26.cloned.1.call-start = ((), (), s32[]{:S(2)}) async-start(), calls=%async_computation.16 | async-start | bytes 2027520
  373.1 305.7 %reduce-scatter.18.cloned.1.call-start = ((), (), s32[]{:S(2)}) async-start(), calls=%async_computation.12 | async-start | bytes 2433024 | tf_op jit(solution)/shard_map/reduce_scatter | solution.py:256
  381.1 3.3 copy-start.12
  384.4 401.8 %reduce-scatter.20.cloned.1.call-start = ((), (), s32[]{:S(2)}) async-start(), calls=%async_computation.13 | async-start | bytes 3244032 | tf_op jit(solution)/shard_map/reduce_scatter | solution.py:259
  398.6 496.4 %reduce-scatter.28.cloned.1.call-start = ((), (), s32[]{:S(2)}) async-start(), calls=%async_computation.17 | async-start | bytes 3649536
Sparse Core Ops, SparseCore 0:
  157.5 202.7 reduce-scatter.21
  363.4 6.4 reduce-scatter.23
  375.6 96.6 reduce-scatter.15
  478.0 97.0 reduce-scatter.25
  580.8 98.0 reduce-scatter.17
  685.6 100.5 reduce-scatter.19
  793.1 101.9 reduce-scatter.27
where the time goes:
time: 904 us; the launch traced here: 902 us
  waiting for transfers between devices  643 us (71%)
  blocking collectives  88.9 us (10%)
  local copies, waits for them, and re-layouts  81.9 us (9%)
  matrix products  45.5 us (5%)
  between operations  15.4 us (2%)
  other arithmetic  14.7 us (2%)
  starting transfers between devices  12.8 us (1%)
    unnamed x11, waiting for transfers between devices  413 us
    reduce_scatter x1, waiting for transfers between devices, body(): lax.psum_scatter(blocked(down_term, dp_count, seq_count), ('dp', 'seq'),...  107 us
    reduce_scatter x1, waiting for transfers between devices, body(): lax.psum_scatter(blocked(up_term, dp_count, seq_count), ('dp', 'seq'), sc...  104 us
    all_gather x1, blocking collectives, body(): mod_rows = lax.all_gather(own_mod, 'dp', axis=0, tiled=True)  43.1 us
    psum x1, blocking collectives, body(): lax.psum((qv_bias_grad, out_bias_grad, up_bias_grad, down_bias_grad, ada_...  39.9 us
  transfers between devices with their start and end apart: 10, of which 9 were waited for; matrix products, arithmetic and copies ran while one was open for 6% of the time, Pallas kernels for 0%

commit v1 on v0

v1 whole, which is shorter than its diff:
```python
from functools import partial

import jax
import jax.numpy as jnp
from jax import lax
from jax.experimental import pallas as pl
from jax.experimental.pallas import tpu as pltpu
from jax.sharding import PartitionSpec as P

HEADS = 6
HEAD_DIM = 64
PAIR = 2 * HEAD_DIM
CORE_SWAP = ((0, 1), (1, 0))
CHUNK = 256
LANES = 128
GROUPS_PER_RANK = 2
GENERAL = False
F32 = jnp.float32
LOW = jnp.bfloat16


def nn(left, right):
    return lax.dot_general(left, right, (((1,), (0,)), ((), ())), preferred_element_type=F32)


def nt(left, right):
    return lax.dot_general(left, right, (((1,), (1,)), ((), ())), preferred_element_type=F32)


def tn(left, right):
    return lax.dot_general(left, right, (((0,), (0,)), ((), ())), preferred_element_type=F32)


def normalize(values):
    center = values - jnp.mean(values, axis=-1, keepdims=True)
    spread = jnp.mean(center * center, axis=-1, keepdims=True)
    inverse = lax.rsqrt(spread + 1e-06)
    return center * inverse, inverse


def norm_back(grad, normed, inverse):
    return inverse * (
        grad
        - jnp.mean(grad, axis=-1, keepdims=True)
        - normed * jnp.mean(grad * normed, axis=-1, keepdims=True)
    )


def column_sum(values):
    return jnp.sum(values, axis=0, keepdims=True)


def head_masks(rows):
    lane = lax.broadcasted_iota(jnp.int32, (rows, PAIR), 1)
    return lane < HEAD_DIM, lane >= HEAD_DIM


def masked(values, mask):
    return jnp.where(mask, values, jnp.zeros_like(values))


def softmax_rows(queries, keys, penalty):
    scores = nt(queries, keys) + penalty
    exps = jnp.exp(scores - jnp.max(scores, axis=-1, keepdims=True))
    return exps / jnp.sum(exps, axis=-1, keepdims=True)


def fetch(pairs, sems):
    copies = []
    for index, (source, target) in enumerate(pairs):
        copy = pltpu.make_async_copy(source, target, sems.at[index])
        copy.start()
        copies.append(copy)
    return copies


def own_images(near_ref, far_ref, target_ref, first_image):
    half_len = near_ref.shape[1]
    pairs = []
    for image in range(target_ref.shape[0]):
        slot = first_image + image
        pairs.append((near_ref.at[slot], target_ref.at[image, pl.ds(0, half_len)]))
        pairs.append((far_ref.at[slot], target_ref.at[image, pl.ds(half_len, half_len)]))
    return pairs


def own_marks(mask_ref, counts_ref, core, image, image_count, half_len):
    slot = core * image_count + image
    live = jnp.where(slot < counts_ref[0], 1.0, 0.0)
    marks = mask_ref[pl.ds(slot, 1), :].astype(F32) * live
    low_marks, high_marks = marks[:, :half_len], marks[:, half_len:]
    return jnp.concatenate(
        [
            jnp.where(core == 0, low_marks, high_marks),
            jnp.where(core == 0, high_marks, low_marks),
        ],
        axis=1,
    )


def as_row(ref):
    return ref[...].astype(F32).reshape(1, ref.shape[0])


def forward_kernel(
    lead_rows,
    tokens_hbm,
    tokens_far_hbm,
    cot_hbm,
    cot_far_hbm,
    cond_hbm,
    ids_hbm,
    counts_hbm,
    mask_hbm,
    qkv_w_hbm,
    qv_b_hbm,
    out_w_hbm,
    out_b_hbm,
    up_w_hbm,
    up_b_hbm,
    down_w_hbm,
    down_b_hbm,
    ada_w_hbm,
    ada_b_hbm,
    output_hbm,
    qkv_hbm,
    grad_att_hbm,
    grad_mid_hbm,
    mod_hbm,
    images_hbm,
    penalty_hbm,
    lead_hbm,
    keep_ref,
    send_ref,
    small_ref,
    tokens_ref,
    cot_ref,
    cond_ref,
    mask_ref,
    qkv_w_ref,
    qv_b_ref,
    out_w_ref,
    out_b_ref,
    up_w_ref,
    up_b_ref,
    down_w_ref,
    down_b_ref,
    ada_w_ref,
    ada_b_ref,
    ids_ref,
    counts_ref,
    output_ref,
    qkv_ref,
    grad_att_ref,
    grad_mid_ref,
    mod_ref,
    penalty_ref,
    valid_ref,
    att_ref,
    mid_ref,
    attn_ref,
    h2_ref,
    gffn_ref,
    act_ref,
    gpre_ref,
    ffn_ref,
    gh2_ref,
    turned_ref,
    lead_ref,
    in_sems,
    out_sems,
):
    core = lax.axis_index("seq")
    image_count, length, width = tokens_ref.shape
    half_len = length // 2
    half = width // 2
    ff_width = up_w_ref.shape[1]
    first_image = core * image_count
    copies = fetch(
        [
            (ids_hbm, ids_ref),
            (counts_hbm, counts_ref),
            (cond_hbm, cond_ref),
            (ada_w_hbm, ada_w_ref),
            (ada_b_hbm, ada_b_ref),
            (mask_hbm, mask_ref),
        ]
        + own_images(tokens_hbm, tokens_far_hbm, tokens_ref, first_image)
        + [
            (qkv_w_hbm, qkv_w_ref),
            (qv_b_hbm, qv_b_ref),
            (out_w_hbm, out_w_ref),
            (out_b_hbm, out_b_ref),
        ]
        + own_images(cot_hbm, cot_far_hbm, cot_ref, first_image)
        + [
            (up_w_hbm, up_w_ref),
            (up_b_hbm, up_b_ref),
            (down_w_hbm, down_w_ref),
            (down_b_hbm, down_b_ref),
        ],
        in_sems,
    )
    token_copies = 6 + 2 * image_count
    for copy in copies[:5]:
        copy.wait()
    block_count, block_rows = cond_ref.shape[:2]
    cond = cond_ref[...].reshape(block_count * block_rows, width).astype(F32)
    silu = (cond / (1.0 + jnp.exp(-cond))).astype(LOW)
    row = lax.broadcasted_iota(jnp.int32, (8, block_count * block_rows), 0)
    column = lax.broadcasted_iota(jnp.int32, (8, block_count * block_rows), 1)
    hot = jnp.zeros((8, block_count * block_rows), F32)
    for image in range(image_count):
        group = ids_ref[first_image + image]
        place = block_rows * (group // GROUPS_PER_RANK) + group % GROUPS_PER_RANK
        hot = jnp.where((row == image) & (column == place), 1.0, hot)
    image_silu = nn(hot.astype(LOW), silu).astype(LOW)
    mod_ref[...] = (nn(image_silu, ada_w_ref[...]) + as_row(ada_b_ref)).astype(LOW)
    if lead_rows:
        turned_ref[...] = silu.astype(F32).T
        start = pl.multiple_of(lax.axis_index("dp") * lead_rows, 8)
        lead_ref[...] = turned_ref[pl.ds(start, lead_rows), :].astype(LOW)
    else:
        lead_ref[...] = jnp.zeros_like(lead_ref)
    results = fetch([(mod_ref, mod_hbm), (lead_ref, lead_hbm)], out_sems)
    for copy in copies[5 : token_copies + 2]:
        copy.wait()

    def part(image, which):
        return mod_ref[image : image + 1, which * width : (which + 1) * width].astype(F32)

    def rows_of(image):
        return slice(image * length, (image + 1) * length)

    small_ref[...] = jnp.zeros_like(small_ref)
    qkv_bias = jnp.concatenate(
        [qv_b_ref[0:1, :], jnp.zeros((1, width), LOW), qv_b_ref[1:2, :]], axis=1
    ).astype(F32)
    for image in range(image_count):
        rows = rows_of(image)
        marks = own_marks(mask_ref, counts_ref, core, image, image_count, half_len)
        penalty_ref[image : image + 1, :] = (marks - 1.0) * 30000.0
        valid_ref[rows, :] = jnp.broadcast_to(marks, (LANES, length)).T
        normed, _ = normalize(tokens_ref[image].astype(F32))
        h1 = (normed * (1.0 + part(image, 1)) + part(image, 0)).astype(LOW)
        qkv_ref[rows, :] = (nn(h1, qkv_w_ref[...]) + qkv_bias).astype(LOW)

    results += fetch(
        [(qkv_ref, qkv_hbm), (tokens_ref, images_hbm), (penalty_ref, penalty_hbm)],
        out_sems.at[pl.ds(2, 3)],
    )

    def valid_of(image):
        column = valid_ref[rows_of(image), :]
        return jnp.concatenate([column] * (width // LANES), axis=1)

    first, second = head_masks(length)

    def pair_step(step, carry):
        image = step // (HEADS // 2)
        pair = step % (HEADS // 2)
        rows = pl.ds(pl.multiple_of(image * length, length), length)

        def lanes(which):
            return pl.ds(pl.multiple_of(which * width + pair * PAIR, PAIR), PAIR)

        queries = qkv_ref[rows, lanes(0)] * jnp.asarray(HEAD_DIM**-0.5, LOW)
        keys = qkv_ref[rows, lanes(1)]
        values = qkv_ref[rows, lanes(2)]
        penalty = penalty_ref[pl.ds(image, 1), :]
        total = jnp.zeros((length, PAIR), F32)
        for mask in (first, second):
            probs = softmax_rows(masked(queries, mask), keys, penalty).astype(LOW)
            total = total + nn(probs, masked(values, mask))
        att_ref[rows, lanes(0)] = total.astype(LOW)
        return carry

    lax.fori_loop(0, image_count * (HEADS // 2), pair_step, 0)

    for copy in copies[token_copies + 2 :]:
        copy.wait()
    down_bias_grad = jnp.zeros((1, width), F32)
    for image in range(image_count):
        rows = rows_of(image)
        valid = valid_of(image)
        attn = nn(att_ref[rows, :], out_w_ref[...]) + as_row(out_b_ref)
        attn_ref[rows, :] = attn
        middle = tokens_ref[image].astype(F32) + valid * part(image, 2) * attn
        mid_ref[rows, :] = middle
        normed, _ = normalize(middle)
        h2_ref[rows, :] = (normed * (1.0 + part(image, 4)) + part(image, 3)).astype(LOW)
        grad_ffn = (valid * part(image, 5) * cot_ref[image].astype(F32)).astype(LOW)
        gffn_ref[rows, :] = grad_ffn
        down_bias_grad = down_bias_grad + column_sum(grad_ffn.astype(F32))
        ffn_ref[rows, :] = jnp.zeros((length, width), F32)
        gh2_ref[rows, :] = jnp.zeros((length, width), F32)
    small_ref[13:14, :] = down_bias_grad
    for image in range(image_count):
        group = ids_ref[first_image + image].astype(F32)
        small_ref[14 + image : 15 + image, :] = jnp.full((1, width), group, F32)

    first_half = gffn_ref[:, :half]
    second_half = gffn_ref[:, half:]
    gffn_keep = jnp.where(core == 0, first_half, second_half)
    gffn_send = jnp.where(core == 0, second_half, first_half)
    side_chunks = ff_width // CHUNK // 2
    up_bias = as_row(up_b_ref)

    def ffn_chunk(chunk):
        columns = slice(chunk * CHUNK, (chunk + 1) * CHUNK)
        up_w = up_w_ref[:, columns]
        down_w = down_w_ref[columns, :]
        up_b = up_bias[:, columns]
        for image in range(image_count):
            rows = rows_of(image)
            pre = nn(h2_ref[rows, :], up_w) + up_b
            square = pre * pre
            inner = jnp.tanh(0.7978845608028654 * (pre + 0.044715 * (square * pre)))
            cdf = 0.5 * (1.0 + inner)
            act = (pre * cdf).astype(LOW)
            slope = cdf + 0.5 * pre * (1.0 - inner * inner) * (
                0.7978845608028654 * (1.0 + 3.0 * 0.044715 * square)
            )
            grad_pre = (nt(gffn_ref[rows, :], down_w) * slope).astype(LOW)
            act_ref[rows, :] = act
            gpre_ref[rows, :] = grad_pre
            ffn_ref[rows, :] += nn(act, down_w)
            gh2_ref[rows, :] += nt(grad_pre, up_w)
        bias = column_sum(gpre_ref[...].astype(F32))
        for tile in range(CHUNK // LANES):
            start = chunk * CHUNK + tile * LANES
            small_ref[9 + start // width : 10 + start // width, start % width : start % width + LANES] = (
                bias[:, tile * LANES : (tile + 1) * LANES]
            )
        return (
            tn(h2_ref[...], gpre_ref[...]),
            tn(act_ref[...], gffn_keep),
            tn(act_ref[...], gffn_send),
        )

    for step in range(side_chunks):
        up_low, keep_low, send_low = ffn_chunk(step)
        up_high, keep_high, send_high = ffn_chunk(step + side_chunks)
        up_keep = jnp.where(core == 0, up_low, up_high)
        up_send = jnp.where(core == 0, up_high, up_low).astype(LOW)
        for tile in range(CHUNK // LANES):
            start = step * CHUNK + tile * LANES
            rows = slice(start // width * width, (start // width + 1) * width)
            columns = slice(start % width, start % width + LANES)
            keep_ref[rows, columns] = up_keep[:, tile * LANES : (tile + 1) * LANES]
            send_ref[rows, columns] = up_send[:, tile * LANES : (tile + 1) * LANES]
        rows = slice(2 * width + step * CHUNK, 2 * width + (step + 1) * CHUNK)
        keep_ref[rows, :] = jnp.concatenate([keep_low, keep_high], axis=1)
        send_ref[rows, :] = jnp.concatenate([send_low, send_high], axis=1).astype(LOW)

    out_bias_grad = jnp.zeros((1, width), F32)
    for image in range(image_count):
        rows = rows_of(image)
        valid = valid_of(image)
        upstream = cot_ref[image].astype(F32)
        middle = mid_ref[rows, :]
        ffn = ffn_ref[rows, :] + as_row(down_b_ref)
        result = (middle + valid * part(image, 5) * ffn).astype(LOW)
        output_ref[image] = result
        start = keep_ref.shape[0] + 16 + image * half_len
        send_ref[start : start + half_len, :] = result[half_len:]
        small_ref[6 + image : 7 + image, :] = column_sum(valid * ffn * upstream)
        normed, inverse = normalize(middle)
        grad_h2 = gh2_ref[rows, :]
        small_ref[2 + image : 3 + image, :] = column_sum(grad_h2)
        small_ref[4 + image : 5 + image, :] = column_sum(grad_h2 * normed)
        grad_mid = upstream + norm_back(grad_h2 * (1.0 + part(image, 4)), normed, inverse)
        grad_mid_ref[rows, :] = grad_mid
        small_ref[image : image + 1, :] = column_sum(valid * attn_ref[rows, :] * grad_mid)
        grad_attn = (valid * part(image, 2) * grad_mid).astype(LOW)
        h2_ref[rows, :] = grad_attn
        out_bias_grad = out_bias_grad + column_sum(grad_attn.astype(F32))
        grad_att_ref[rows, :] = nt(grad_attn, out_w_ref[...]).astype(LOW)
    small_ref[8:9, :] = out_bias_grad
    results += fetch(
        [
            (grad_att_ref, grad_att_hbm),
            (grad_mid_ref, grad_mid_hbm),
            (
                output_ref.at[:, pl.ds(0, half_len)],
                output_hbm.at[pl.ds(first_image, image_count)],
            ),
        ],
        out_sems.at[pl.ds(5, 3)],
    )
    out_term = tn(att_ref[...], h2_ref[...])
    out_first = jnp.concatenate([out_term[:half, :half], out_term[half:, :half]], axis=1)
    out_second = jnp.concatenate([out_term[:half, half:], out_term[half:, half:]], axis=1)
    rows = slice(2 * width + ff_width // 2, 2 * width + ff_width // 2 + half)
    keep_ref[rows, :] = jnp.where(core == 0, out_first, out_second)
    send_ref[rows, :] = jnp.where(core == 0, out_second, out_first).astype(LOW)
    send_ref[keep_ref.shape[0] : keep_ref.shape[0] + 16, :] = small_ref[...].astype(LOW)
    for copy in results:
        copy.wait()


def backward_kernel(
    images_hbm,
    penalty_hbm,
    qkv_w_hbm,
    qkv_hbm,
    grad_att_hbm,
    grad_mid_hbm,
    mod_hbm,
    after_ref,
    grad_tokens_hbm,
    far_ref,
    h1_ref,
    gqkv_ref,
    small_ref,
    tokens_ref,
    penalty_ref,
    qkv_w_ref,
    qkv_ref,
    grad_att_ref,
    grad_mid_ref,
    mod_ref,
    grad_tokens_ref,
    in_sems,
    out_sems,
):
    image_count, length, width = tokens_ref.shape
    half_len = length // 2
    copies = fetch(
        [
            (penalty_hbm, penalty_ref),
            (qkv_hbm, qkv_ref),
            (grad_att_hbm, grad_att_ref),
            (mod_hbm, mod_ref),
            (images_hbm, tokens_ref),
            (qkv_w_hbm, qkv_w_ref),
            (grad_mid_hbm, grad_mid_ref),
        ],
        in_sems,
    )
    for copy in copies[:3]:
        copy.wait()
    first, second = head_masks(length)

    def pair_step(step, carry):
        image = step // (HEADS // 2)
        pair = step % (HEADS // 2)
        rows = pl.ds(pl.multiple_of(image * length, length), length)

        def lanes(which):
            return pl.ds(pl.multiple_of(which * width + pair * PAIR, PAIR), PAIR)

        queries = qkv_ref[rows, lanes(0)] * jnp.asarray(HEAD_DIM**-0.5, LOW)
        keys = qkv_ref[rows, lanes(1)]
        values = qkv_ref[rows, lanes(2)]
        grad_att = grad_att_ref[rows, lanes(0)]
        penalty = penalty_ref[pl.ds(image, 1), :]
        grad_q = jnp.zeros((length, PAIR), F32)
        grad_k = jnp.zeros((length, PAIR), F32)
        grad_v = jnp.zeros((length, PAIR), F32)
        for mask in (first, second):
            own_queries = masked(queries, mask)
            own_grad = masked(grad_att, mask)
            probs = softmax_rows(own_queries, keys, penalty)
            grad_probs = nt(own_grad, values)
            dots = jnp.sum(probs * grad_probs, axis=-1, keepdims=True)
            grad_scores = (probs * (grad_probs - dots)).astype(LOW)
            grad_v = grad_v + tn(probs.astype(LOW), own_grad)
            grad_q = grad_q + nn(grad_scores, masked(keys, mask))
            grad_k = grad_k + tn(grad_scores, own_queries)
        gqkv_ref[rows, lanes(0)] = (grad_q * HEAD_DIM**-0.5).astype(LOW)
        gqkv_ref[rows, lanes(1)] = grad_k.astype(LOW)
        gqkv_ref[rows, lanes(2)] = grad_v.astype(LOW)
        return carry

    lax.fori_loop(0, image_count * (HEADS // 2), pair_step, 0)

    def part(image, which):
        return mod_ref[image : image + 1, which * width : (which + 1) * width].astype(F32)

    for copy in copies[3:]:
        copy.wait()
    small_ref[...] = jnp.zeros_like(small_ref)
    small_ref[4:5, :] = column_sum(gqkv_ref[:, :width].astype(F32))
    small_ref[5:6, :] = column_sum(gqkv_ref[:, 2 * width :].astype(F32))
    for image in range(image_count):
        rows = slice(image * length, (image + 1) * length)
        normed, inverse = normalize(tokens_ref[image].astype(F32))
        h1_ref[rows, :] = (normed * (1.0 + part(image, 1)) + part(image, 0)).astype(LOW)
        grad_h1 = nt(gqkv_ref[rows, :], qkv_w_ref[...])
        small_ref[image : image + 1, :] = column_sum(grad_h1)
        small_ref[2 + image : 3 + image, :] = column_sum(grad_h1 * normed)
        grad_in = norm_back(grad_h1 * (1.0 + part(image, 1)), normed, inverse)
        result = (grad_mid_ref[rows, :] + grad_in).astype(LOW)
        grad_tokens_ref[image] = result
        far_ref[image] = result[half_len:]
    results = fetch(
        [
            (
                grad_tokens_ref.at[:, pl.ds(0, half_len)],
                grad_tokens_hbm.at[pl.ds(lax.axis_index("seq") * image_count, image_count)],
            ),
        ],
        out_sems,
    )
    for copy in results:
        copy.wait()


def qkv_kernel(h1_ref, gqkv_ref, small_ref, keep_ref, send_ref, other_ref):
    core = lax.axis_index("seq")
    width = keep_ref.shape[1]
    half = width // 2
    low_term = tn(h1_ref[...], gqkv_ref[:, :width])
    high_term = tn(h1_ref[...], gqkv_ref[:, 2 * width :])
    keep_ref[:width, :] = jnp.where(core == 0, low_term, high_term)
    pair = jnp.where(core == 0, high_term, low_term).astype(LOW)
    send_ref[...] = pair[: width // 4 * 3]
    other_ref[: width // 4, :] = pair[width // 4 * 3 :]
    term = tn(h1_ref[...], gqkv_ref[:, width : 2 * width])
    low_unit = jnp.concatenate([term[:half, :half], term[half:, :half]], axis=1)
    high_unit = jnp.concatenate([term[:half, half:], term[half:, half:]], axis=1)
    keep_ref[width:, :] = jnp.where(core == 0, low_unit, high_unit)
    start = width // 4
    other_ref[start : start + half, :] = jnp.where(core == 0, high_unit, low_unit).astype(LOW)
    other_ref[start + half : start + half + 8, :] = small_ref[...].astype(LOW)


def by_core(core, near, far):
    return [jnp.where(core == 0, near, far), jnp.where(core == 0, far, near)]


def split_kernel(keep_ref, recv_ref, small_ref, own_ref, one_ref, two_ref, three_ref):
    core = lax.axis_index("seq")
    width = keep_ref.shape[1]
    piece = width // 16
    long = 4 * piece
    near = small_ref[...].astype(LOW).astype(F32)
    far = recv_ref[keep_ref.shape[0] : keep_ref.shape[0] + 16, :].astype(F32)
    first, second = by_core(core, near, far)
    mods = []
    for row in range(0, 6, 2):
        low_kind = [first[:2], second[:2]] if row == 0 else [jnp.zeros((4, width), F32)]
        high_kind = [first[row + 2 : row + 4], second[row + 2 : row + 4]]
        mods.append(
            jnp.where(
                core == 0, jnp.concatenate(low_kind, axis=0), jnp.concatenate(high_kind, axis=0)
            )
        )
    mods += [first[14:16], second[14:16], first[8:14] + second[8:14], jnp.zeros((2, width), F32)]
    small = jnp.concatenate(mods, axis=0)
    for step, target in enumerate((own_ref, one_ref, two_ref, three_ref)):
        who = (lax.axis_index("dp") & 3) ^ step

        def move(start, size, to):
            rows = pl.ds(pl.multiple_of(start, 8), size)
            target[to : to + size, :] = (
                keep_ref[rows, :] + recv_ref[rows, :].astype(F32)
            ).astype(target.dtype)

        for z in range(4):
            for side in range(2):
                move(side * width + piece * (4 * z + who), piece, (2 * z + side) * piece)
        for z in range(2):
            move(2 * width + long * (4 * z + who), long, 8 * piece + z * long)
            move(2 * width + 8 * long + piece * (4 * z + who), piece, 16 * piece + z * piece)
        target[18 * piece :, :] = small.astype(LOW).astype(target.dtype)


def split_qkv_kernel(keep_ref, recv_ref, other_ref, small_ref, *refs):
    core = lax.axis_index("seq")
    width = keep_ref.shape[1]
    piece = width // 16
    quarter = recv_ref.shape[0]
    near = small_ref[...].astype(LOW).astype(F32)
    start = keep_ref.shape[0] - quarter
    far = other_ref[start : start + 8, :].astype(F32)
    first, second = by_core(core, near, far)
    mods = jnp.concatenate([first[0:2], second[0:2], first[2:4], second[2:4]], axis=0)
    small = jnp.concatenate(
        [mods, first[4:6] + second[4:6], jnp.zeros((6, width), F32)], axis=0
    ).astype(LOW)
    total_ref = refs[-1]
    total_ref[:quarter, :] = keep_ref[:quarter, :] + recv_ref[...].astype(F32)
    total_ref[quarter:, :] = keep_ref[quarter:, :] + other_ref[:start, :].astype(F32)
    for step, target in enumerate(refs[-5:-1]):
        who = (lax.axis_index("dp") & 3) ^ step
        for z in range(6):
            start = width + piece * (4 * (z - 4) + who) if z >= 4 else piece * (4 * z + who)
            rows = pl.ds(pl.multiple_of(start, 8), piece)
            target[piece * z : piece * (z + 1), :] = total_ref[rows, :].astype(target.dtype)
        target[6 * piece :, :] = small.astype(target.dtype)


def fold_kernel(*refs):
    ones, twos = refs[:4], refs[4:8]
    rest_ref, rest_small_ref = refs[8:10]
    sends = refs[10:13]
    one_ref, two_ref, group_ref, late_ref = refs[13:]
    core = lax.axis_index("seq")
    width = one_ref.shape[1]
    piece = width // 16
    long = 4 * piece
    half = width // 2
    plane = lax.axis_index("dp") & 3

    def summed(sources, rows):
        return sum((source[rows, :].astype(F32) for source in sources[1:]), sources[0][rows, :])

    one_ref[...] = summed(ones, slice(0, 18 * piece))
    two_ref[...] = summed(twos, slice(0, 6 * piece))
    for step in range(4):
        group_ref[plane ^ step] = ones[step][18 * piece :, :].astype(F32)
        late_ref[plane ^ step] = twos[step][6 * piece :, :].astype(F32)
    rows = []
    for q in range(4):
        early, late = group_ref[q], late_ref[q]
        rows.append(
            jnp.where(
                core == 0, jnp.concatenate([late[:8], early[:4]], axis=0), early[:12]
            )
        )
        rows.append(early[12:16])
    early = group_ref[0] + group_ref[1] + group_ref[2] + group_ref[3]
    late = late_ref[0] + late_ref[1] + late_ref[2] + late_ref[3]
    rows += [early[16:22], late[8:10]]
    small = jnp.concatenate(rows, axis=0).astype(LOW)
    rest_small_ref[...] = small
    for step, target in enumerate((rest_ref,) + tuple(sends)):
        who = (lax.axis_index("dp") >> 2) ^ step
        dtype = target.dtype

        def block(ref, start, size):
            return ref[pl.ds(pl.multiple_of(start, 8), size), :]

        def side(value):
            return jnp.where(who < 2, value[:, :half], value[:, half:])

        target[: 2 * piece, :] = block(one_ref, 2 * piece * who, 2 * piece).astype(dtype)
        down = side(block(one_ref, 8 * piece + long * (who % 2), long))
        down = jnp.concatenate([down[: 2 * piece], down[2 * piece :]], axis=1)
        target[2 * piece : 4 * piece, :] = down.astype(dtype)
        out = side(block(one_ref, 16 * piece + piece * (who % 2), piece))
        unit = side(block(two_ref, 4 * piece + piece * (who % 2), piece))
        target[4 * piece : 5 * piece, :] = jnp.concatenate([out, unit], axis=1).astype(dtype)
        target[5 * piece : 6 * piece, :] = block(two_ref, piece * who, piece).astype(dtype)
        if step:
            target[6 * piece :, :] = small


def group_parts(lead, own_groups, hot, kinds, kind_of, extra):
    silu_rows = nn(lead, hot).astype(LOW)
    zeros = jnp.zeros_like(kind_of, F32)
    blocks = [masked(silu_rows, kind_of == kind) for kind in kinds]
    rows = []
    for kind in kinds:
        for one in own_groups:
            rows.append(jnp.where((kind_of == kind) & one, 1.0, zeros))
    for kind in kinds:
        rows.append(jnp.where(kind_of == kind, 1.0, zeros))
    for mark in extra:
        rows.append(jnp.where(mark, 1.0, zeros))
    while len(rows) % 8:
        rows.append(zeros)
    return blocks, jnp.concatenate(rows, axis=0).astype(LOW)


def split_dot(values, weight):
    high = values.astype(LOW)
    low = (values - high.astype(F32)).astype(LOW)
    return nt(high, weight) + nt(low, weight)


def spread_ids(marks, count, row_of):
    column = lax.broadcasted_iota(jnp.int32, (marks.shape[1], count), 1)
    row = lax.broadcasted_iota(jnp.int32, (marks.shape[1], count), 0)
    chosen = jnp.where(row == row_of(column), 1.0, 0.0).astype(LOW)
    return nn(marks, chosen)[:1].astype(jnp.int32)


def one_hot(ids, lead):
    place = lax.broadcasted_iota(jnp.int32, (lead.shape[1], ids.shape[1]), 0)
    wanted = (ids // GROUPS_PER_RANK) * 8 + ids % GROUPS_PER_RANK
    return jnp.where(place == wanted, 1.0, 0.0).astype(LOW)


def late_kernel(
    own_ref,
    own_small_ref,
    one_ref,
    two_ref,
    three_ref,
    lead_ref,
    ada_hbm,
    recv_ref,
    far_ref,
    output_hbm,
    grad_tokens_hbm,
    output_to,
    grad_tokens_to,
    up_ref,
    out_ref,
    down_ref,
    qkv_ref,
    ada_out_ref,
    own_sums_ref,
    send_ref,
    out_bias_ref,
    up_bias_ref,
    down_bias_ref,
    qv_ref,
    stack_ref,
    bias_ref,
    ada_ref,
    sems,
):
    core = lax.axis_index("seq")
    width = own_ref.shape[1]
    piece = width // 16
    half = width // 2
    count, half_len = far_ref.shape[:2]
    start = recv_ref.shape[0] - count * half_len
    pairs = [
        (ada_hbm.at[:, pl.ds(pl.multiple_of(core * 3 * width, LANES), 3 * width)], ada_ref),
        (far_ref, grad_tokens_to.at[pl.ds((1 - core) * count, count)]),
    ]
    for image in range(count):
        pairs.append(
            (
                recv_ref.at[pl.ds(start + image * half_len, half_len)],
                output_to.at[(1 - core) * count + image],
            )
        )
    copies = fetch(pairs, sems)
    parts = (own_ref, one_ref, two_ref, three_ref)
    weights = slice(0, 6 * piece)
    total = sum((part[weights, :].astype(F32) for part in parts[1:]), own_ref[weights, :])
    up_ref[...] = jnp.concatenate([total[:piece], total[piece : 2 * piece]], axis=1)
    down = total[2 * piece : 4 * piece]
    down_ref[...] = jnp.concatenate([down[:, :half], down[:, half:]], axis=0)
    out_ref[...] = total[4 * piece : 5 * piece, :half]
    unit = total[4 * piece : 5 * piece, half:]
    pair = total[5 * piece :]
    qkv_ref[...] = jnp.where(
        core == 0,
        jnp.concatenate([pair, unit], axis=1),
        jnp.concatenate([unit, pair], axis=1),
    )
    line = lax.axis_index("dp") >> 2
    smalls = (own_small_ref[...],) + tuple(part[6 * piece :, :] for part in parts[1:])
    for step, small in enumerate(smalls):
        stack_ref[line ^ step] = small[:64]
        bias_ref[line ^ step] = small[64:].astype(F32)
    bias = bias_ref[0] + bias_ref[1] + bias_ref[2] + bias_ref[3]
    out_bias_ref[...] = bias[0:1].reshape(width)
    up_bias_ref[...] = jnp.concatenate([bias[1 + row : 2 + row] for row in range(4)], axis=1).reshape(
        4 * width
    )
    down_bias_ref[...] = bias[5:6].reshape(width)
    qv_ref[...] = bias[6:8]
    stack = stack_ref[...].reshape(256, width)
    lead = lead_ref[...]
    corner = (lax.broadcasted_iota(jnp.int32, (8, LANES), 1) == 0).astype(F32).astype(LOW)
    marks = nt(corner, stack[:, :LANES]).astype(LOW)
    ids = spread_ids(marks, 256, lambda index: index - index % 16 + 12 + index % 4)
    hot = one_hot(ids, lead)
    item = lax.broadcasted_iota(jnp.int32, (1, 256), 1) % 16
    base = GROUPS_PER_RANK * lax.axis_index("dp")
    own = [ids == base + index for index in range(GROUPS_PER_RANK)]
    blocks, rows = group_parts(lead, own, hot, range(3), item // 4, [])
    for kind in range(3):
        ada_out_ref[:, kind * width : (kind + 1) * width] = nn(blocks[kind], stack)
    sums = nn(rows, stack)
    copies[0].wait()
    cond = jnp.zeros((8, width), F32)
    for kind in range(3):
        own_sum = jnp.concatenate(
            [sums[2 * kind : 2 * kind + 2], jnp.zeros((6, width), F32)], axis=0
        )
        cond = cond + split_dot(own_sum, ada_ref[:, kind * width : (kind + 1) * width])
    low_cond, high_cond = cond[:2, :half], cond[:2, half:]
    kept = jnp.where(core == 0, low_cond, high_cond)
    sent = jnp.where(core == 0, high_cond, low_cond)
    zeros = jnp.zeros((2, half), F32)
    pad = jnp.zeros((3, width), F32)
    own_sums_ref[...] = jnp.concatenate(
        [jnp.concatenate([kept, zeros], axis=1), sums[6:9], pad], axis=0
    )
    send_ref[...] = jnp.concatenate(
        [jnp.concatenate([sent, zeros], axis=1), sums[6:9], pad], axis=0
    )
    for copy in copies[1:]:
        copy.wait()


def final_kernel(own_ref, recv_ref, own_cond_ref, cond_ref, bias_ref):
    core = lax.axis_index("seq")
    width = own_ref.shape[1]
    half = width // 2
    near, far = own_ref[...], recv_ref[...]
    values = own_cond_ref[...].astype(F32)
    values = jnp.where(core == 0, values[:, :half], values[:, half:])
    gate = 1.0 / (1.0 + jnp.exp(-values))
    cond_ref[...] = (near[:2, :half] + far[:2, :half]) * (gate * (1.0 + values * (1.0 - gate)))
    rows = [block[row : row + 1] for block in by_core(core, near, far) for row in range(2, 5)]
    bias_ref[...] = jnp.concatenate(rows, axis=1).reshape(6 * width)


def silu_slope(values):
    sigmoid_val = jax.nn.sigmoid(values)
    return sigmoid_val * (1.0 + values * (1.0 - sigmoid_val))


def swap_cores(values):
    return lax.ppermute(values, "seq", CORE_SWAP)


def pick(core, first, second):
    return jnp.where(core == 0, first, second)


def to_patches(placed, far, core):
    return lax.dynamic_update_slice_in_dim(
        placed, swap_cores(far), (1 - core) * far.shape[0], 0
    )


def call(kernel, name, shapes, scratch, limit, spaces, *operands, aliases=None):
    chosen = {
        "s": pl.BlockSpec(memory_space=pltpu.SMEM),
        "v": pl.BlockSpec(memory_space=pltpu.VMEM),
        "V": pl.BlockSpec(memory_space=pltpu.VMEM),
        "a": pl.BlockSpec(memory_space=pl.ANY),
        "h": pl.BlockSpec(memory_space=pltpu.HBM),
    }
    pinned = {"h": pltpu.HBM, "V": pltpu.VMEM}
    into, out_of = spaces
    operands = [
        pltpu.with_memory_space_constraint(item, pinned[kind]) if kind in pinned else item
        for kind, item in zip(into, operands)
    ]
    return pl.pallas_call(
        kernel,
        out_shape=tuple(
            pinned.get(kind, jax.ShapeDtypeStruct)(shape, dtype)
            for kind, (shape, dtype) in zip(out_of, shapes)
        ),
        in_specs=[chosen[kind] for kind in into],
        out_specs=[chosen[kind] for kind in out_of],
        scratch_shapes=scratch,
        compiler_params=pltpu.CompilerParams(vmem_limit_bytes=limit << 20),
        cost_estimate=pl.CostEstimate(flops=1, bytes_accessed=1, transcendentals=0),
        input_output_aliases=aliases or {},
        name=name,
    )(*operands)


def rank_swap(values, step, count):
    return lax.ppermute(values, "dp", [(rank, rank ^ step) for rank in range(count)])


def owner_total(term, dp_count):
    blocks = term.astype(LOW).reshape(dp_count, term.shape[0] // dp_count, term.shape[1])
    return jnp.sum(lax.all_to_all(blocks, "dp", 0, 0, tiled=True).astype(F32), axis=0)


def general_tail(
    core, dp_count, dp_rank, sides, smalls, heads, cond_rows, cond, own_ids, ada_weight
):
    highest = lax.Precision.HIGHEST
    width, mod_width = ada_weight.shape
    half = width // 2
    (keep_one, send_one), (keep_two, send_two) = sides
    far_rows = send_one[keep_one.shape[0] + 16 :]
    small_one, small_two = smalls
    first_sum = keep_one + swap_cores(send_one[: keep_one.shape[0]]).astype(F32)
    second_sum = keep_two + swap_cores(send_two)[: keep_two.shape[0]].astype(F32)
    ff_half = first_sum.shape[0] - 2 * width - half
    up = jnp.concatenate([first_sum[:width], first_sum[width : 2 * width]], axis=1)
    down = first_sum[2 * width : 2 * width + ff_half]
    down = jnp.concatenate([down[:, :half], down[:, half:]], axis=0)
    out = first_sum[2 * width + ff_half :]
    out = jnp.concatenate([out[:, :half], out[:, half:]], axis=0)
    pair, unit = second_sum[:width], second_sum[width:]
    unit = jnp.concatenate([unit[:, :half], unit[:, half:]], axis=0)
    qkv = pick(
        core, jnp.concatenate([pair, unit], axis=1), jnp.concatenate([unit, pair], axis=1)
    )
    sums = [owner_total(term, dp_count) for term in (qkv, out, up, down)]
    image_grad = jnp.concatenate(
        [small_two[0:2], small_two[2:4], small_one[0:2], small_one[2:4], small_one[4:6], small_one[6:8]],
        axis=1,
    )
    biases = jnp.concatenate([small_two[4:6], small_one[8:14]], axis=0)
    marks = jnp.broadcast_to(own_ids.astype(F32)[:, None], (own_ids.shape[0], width))
    packed = jnp.concatenate([image_grad.reshape(-1, width), biases, marks], axis=0)
    gathered = lax.all_to_all(
        jnp.broadcast_to(packed[None], (2 * dp_count,) + packed.shape),
        ("dp", "seq"),
        0,
        0,
        tiled=True,
    )
    grad_rows = gathered[:, :12].reshape(-1, mod_width)
    bias_sums = jnp.sum(gathered[:, 12:20], axis=0)
    all_ids = gathered[:, 20:, 0].reshape(-1).astype(jnp.int32)
    group_count = cond_rows.shape[0]
    all_hot = (all_ids[:, None] == jnp.arange(group_count, dtype=jnp.int32)[None, :]).astype(F32)
    group_grad = jnp.dot(all_hot.T, grad_rows, precision=highest)
    own_rows = width // dp_count
    silu_rows = lax.reduce_precision(jax.nn.silu(cond_rows.astype(F32)), 8, 7)
    silu_part = lax.dynamic_slice_in_dim(silu_rows, dp_rank * own_rows, own_rows, 1)
    grad_half = pick(core, group_grad[:, : mod_width // 2], group_grad[:, mod_width // 2 :])
    ada_sum = jnp.dot(silu_part.T, grad_half, precision=highest)
    own_grad = lax.dynamic_slice_in_dim(
        group_grad, dp_rank * GROUPS_PER_RANK, GROUPS_PER_RANK, 0
    )
    ada_half = lax.dynamic_slice_in_dim(ada_weight, core * half, half, 0).astype(F32)
    cond_half = pick(core, cond[:, :half], cond[:, half:]).astype(F32)
    grad_cond = silu_slope(cond_half) * jnp.dot(own_grad, ada_half.T, precision=highest)
    return (
        to_patches(heads[0], far_rows.reshape(heads[2].shape), core),
        to_patches(heads[1], heads[2], core),
        grad_cond,
        sums[0],
        bias_sums[:2],
        sums[1],
        bias_sums[2],
        sums[2],
        bias_sums[3:7].reshape(-1),
        sums[3],
        bias_sums[7],
        ada_sum,
        jnp.sum(grad_rows, axis=0),
    )


def body(
    tokens,
    cotangent,
    cond,
    group_ids,
    image_counts,
    patch_mask,
    qkv_weight,
    qv_bias,
    out_weight,
    out_bias,
    up_weight,
    up_bias,
    down_weight,
    down_bias,
    ada_weight,
    ada_bias,
):
    slot_count, half_len, width = tokens.shape
    ff_width = up_weight.shape[1]
    mod_width = ada_weight.shape[1]
    dp_count = lax.axis_size("dp")
    core = lax.axis_index("seq").astype(jnp.int32)
    dp_rank = lax.axis_index("dp").astype(jnp.int32)
    image_count = slot_count // 2
    length = 2 * half_len
    row_count = image_count * length
    half = width // 2
    piece = width // dp_count
    fast = dp_count == 16 and not GENERAL
    block_shape = (dp_count, 8, width)
    block_rows = lax.broadcasted_iota(jnp.int32, block_shape, 1)
    block = jnp.zeros(block_shape, LOW)
    for row in range(GROUPS_PER_RANK):
        block = jnp.where(block_rows == row, cond[row][None, None], block)
    cond_blocks = lax.all_to_all(block, "dp", 0, 0, tiled=True)
    tokens_far = swap_cores(tokens)
    cot_far = swap_cores(cotangent)
    half_shape = (image_count, half_len, width)
    image_shape = (image_count, length, width)
    packed_rows = 2 * width + ff_width // 2 + half
    vmem = pltpu.VMEM
    (
        output,
        qkv,
        grad_att,
        grad_mid,
        image_mod,
        images,
        penalty,
        lead,
        keep_one,
        send_one,
        small_one,
    ) = call(
        partial(forward_kernel, piece if fast else 0),
        "forward_and_ffn_back",
        (
            (tokens.shape, LOW),
            ((row_count, 3 * width), LOW),
            ((row_count, width), LOW),
            ((row_count, width), F32),
            ((8, mod_width), LOW),
            (image_shape, LOW),
            ((8, length), F32),
            ((24, 8 * dp_count), LOW),
            ((packed_rows, width), F32),
            ((packed_rows + 16 + image_count * half_len, width), LOW),
            ((16, width), F32),
        ),
        [
            vmem(image_shape, LOW),
            vmem(image_shape, LOW),
            vmem(block_shape, LOW),
            vmem(patch_mask.shape, jnp.int32),
            vmem(qkv_weight.shape, LOW),
            vmem(qv_bias.shape, LOW),
            vmem(out_weight.shape, LOW),
            vmem(out_bias.shape, LOW),
            vmem(up_weight.shape, LOW),
            vmem(up_bias.shape, LOW),
            vmem(down_weight.shape, LOW),
            vmem(down_bias.shape, LOW),
            vmem(ada_weight.shape, LOW),
            vmem(ada_bias.shape, LOW),
            pltpu.SMEM(group_ids.shape, jnp.int32),
            pltpu.SMEM(image_counts.shape, jnp.int32),
            vmem(image_shape, LOW),
            vmem((row_count, 3 * width), LOW),
            vmem((row_count, width), LOW),
            vmem((row_count, width), F32),
            vmem((8, mod_width), LOW),
            vmem((8, length), F32),
            vmem((row_count, LANES), F32),
            vmem((row_count, width), LOW),
            vmem((row_count, width), F32),
            vmem((row_count, width), F32),
            vmem((row_count, width), LOW),
            vmem((row_count, width), LOW),
            vmem((row_count, CHUNK), LOW),
            vmem((row_count, CHUNK), LOW),
            vmem((row_count, width), F32),
            vmem((row_count, width), F32),
            vmem((width, 8 * dp_count), F32),
            vmem((24, 8 * dp_count), LOW),
            pltpu.SemaphoreType.DMA((14 + 4 * image_count,)),
            pltpu.SemaphoreType.DMA((8,)),
        ],
        40,
        ("hahaaaa" + "h" * 11, "h" * 8 + "VVV"),
        tokens,
        tokens_far,
        cotangent,
        cot_far,
        cond_blocks,
        group_ids,
        image_counts,
        patch_mask,
        qkv_weight,
        qv_bias,
        out_weight,
        out_bias,
        up_weight,
        up_bias,
        down_weight,
        down_bias,
        ada_weight,
        ada_bias,
    )

    def attention_back(after):
        return call(
            backward_kernel,
            "attention_back",
            (
                (tokens.shape, LOW),
                (half_shape, LOW),
                ((row_count, width), LOW),
                ((row_count, 3 * width), LOW),
                ((8, width), F32),
            ),
            [
                vmem(image_shape, LOW),
                vmem((8, length), F32),
                vmem(qkv_weight.shape, LOW),
                vmem((row_count, 3 * width), LOW),
                vmem((row_count, width), LOW),
                vmem((row_count, width), F32),
                vmem((8, mod_width), LOW),
                vmem(image_shape, LOW),
                pltpu.SemaphoreType.DMA((7,)),
                pltpu.SemaphoreType.DMA((1,)),
            ],
            24,
            ("h" * 7 + "a", "hVVVV"),
            images,
            penalty,
            qkv_weight,
            qkv,
            grad_att,
            grad_mid,
            image_mod,
            after,
        )

    def qkv_back(h1, grad_qkv, small_two):
        return call(
            qkv_kernel,
            "qkv_back",
            (
                ((width + half, width), F32),
                ((width // 4 * 3, width), LOW),
                ((width // 4 + half + 8, width), LOW),
            ),
            [],
            16,
            ("VVV", "VVV"),
            h1,
            grad_qkv,
            small_two,
        )

    if not fast:
        grad_tokens, grad_far, h1, grad_qkv, small_two = attention_back(small_one)
        keep_two, *sent_two = qkv_back(h1, grad_qkv, small_two)
        own_ids = lax.dynamic_slice_in_dim(group_ids, core * image_count, image_count, 0)
        return general_tail(
            core,
            dp_count,
            dp_rank,
            ((keep_one, send_one), (keep_two, jnp.concatenate(sent_two, axis=0))),
            (small_one, small_two),
            (output, grad_tokens, grad_far),
            cond_blocks[:, :GROUPS_PER_RANK].reshape(-1, width),
            cond,
            own_ids,
            ada_weight,
        )

    recv_one = swap_cores(send_one)
    split_rows = 18 * piece + 24
    own_part, *sent_parts = call(
        split_kernel,
        "split_plane",
        (((split_rows, width), F32),) + (((split_rows, width), LOW),) * 3,
        [],
        16,
        ("VVV", "VVVV"),
        keep_one,
        recv_one,
        small_one,
    )
    near_parts = [rank_swap(item, step + 1, 16) for step, item in enumerate(sent_parts)]
    grad_tokens, grad_far, h1, grad_qkv, small_two = attention_back(sent_parts[2])
    keep_two, send_two, send_other = qkv_back(h1, grad_qkv, small_two)
    recv_far = swap_cores(grad_far)
    split_rows = 6 * piece + 16
    own_qkv, *sent_qkv = call(
        split_qkv_kernel,
        "split_qkv_plane",
        (((split_rows, width), F32),) + (((split_rows, width), LOW),) * 3,
        [vmem((width + half, width), F32)],
        16,
        ("VVVVaaa", "VVVV"),
        keep_two,
        swap_cores(send_two),
        swap_cores(send_other),
        small_two,
        *near_parts,
    )
    near_qkv = [rank_swap(item, step + 1, 16) for step, item in enumerate(sent_qkv)]
    line_rows = 6 * piece + 72
    rest, rest_small, *lines = call(
        fold_kernel,
        "fold_plane",
        (((6 * piece, width), F32), ((72, width), LOW)) + (((line_rows, width), LOW),) * 3,
        [
            vmem((18 * piece, width), F32),
            vmem((6 * piece, width), F32),
            vmem((4, 24, width), F32),
            vmem((4, 16, width), F32),
        ],
        16,
        ("V" * 8, "VVVVV"),
        own_part,
        *near_parts,
        own_qkv,
        *near_qkv,
    )
    lines = [rank_swap(item, 4 * (step + 1), 16) for step, item in enumerate(lines)]
    (
        output,
        grad_tokens,
        up_sum,
        out_sum,
        down_sum,
        qkv_sum,
        ada_sum,
        own_sums,
        send_sums,
        out_bias_sum,
        up_bias_sum,
        down_bias_sum,
        qv_sum,
    ) = call(
        late_kernel,
        "late_groups",
        (
            (tokens.shape, LOW),
            (tokens.shape, LOW),
            ((piece, ff_width // 2), F32),
            ((piece, half), F32),
            ((4 * piece, half), F32),
            ((piece, 3 * half), F32),
            ((piece, mod_width // 2), F32),
            ((8, width), F32),
            ((8, width), F32),
            ((width,), F32),
            ((ff_width,), F32),
            ((width,), F32),
            ((2, width), F32),
        ),
        [
            vmem((4, 64, width), LOW),
            vmem((4, 8, width), F32),
            vmem((width, mod_width // 2), LOW),
            pltpu.SemaphoreType.DMA((2 + image_count,)),
        ],
        16,
        ("VVVVVVhVVhh", "hhvvvvvVVvvvv"),
        rest,
        rest_small,
        *lines,
        lead,
        ada_weight,
        recv_one,
        recv_far,
        output,
        grad_tokens,
        aliases={9: 0, 10: 1},
    )
    grad_cond, ada_bias_sum = call(
        final_kernel,
        "final_groups",
        (((GROUPS_PER_RANK, half), F32), ((mod_width,), F32)),
        [],
        16,
        ("VVv", "vv"),
        own_sums,
        swap_cores(send_sums),
        cond,
    )
    return (
        output,
        grad_tokens,
        grad_cond,
        qkv_sum,
        qv_sum,
        out_sum,
        out_bias_sum,
        up_sum,
        up_bias_sum,
        down_sum,
        down_bias_sum,
        ada_sum,
        ada_bias_sum,
    )


def solution(mesh):
    placed = (
        P("dp", "seq", None),
        P("dp", "seq", None),
        P("dp", None),
        P("dp"),
        P("dp"),
        P("dp", None),
        P(),
        P(),
        P(),
        P(),
        P(),
        P(),
        P(),
        P(),
        P(),
        P(),
    )
    return jax.shard_map(
        body,
        mesh=mesh,
        in_specs=placed,
        out_specs=(
            P("dp", "seq", None),
            P("dp", "seq", None),
            P("dp", "seq"),
            P("dp", "seq"),
            P(),
            P("dp", "seq"),
            P(),
            P("dp", "seq"),
            P(),
            P("dp", "seq"),
            P(),
            P("dp", "seq"),
            P(),
        ),
        check_vma=False,
    )
```

time: 904 us -> 87.2 us (0.10)
  waiting for transfers between devices: 643 us -> 30.7 us
  blocking collectives: 88.9 us -> 0 us
  local copies, waits for them, and re-layouts: 81.9 us -> 1.44 us
  matrix products: 45.5 us -> 0 us
  Pallas kernels: 0 us -> 31.5 us
  between operations: 15.4 us -> 1.4 us
  other arithmetic: 14.7 us -> 0.73 us
    unnamed x11 -> x0, waiting for transfers between devices: 413 us -> none
    reduce_scatter x3 -> x0, waiting for transfers between devices: 225 us -> none  [the longest x1 107 us: body(): lax.psum_scatter(blocked(down_term, dp_count, seq_count), ('dp', 'seq'),...]
    dot_general x22 -> x0, matrix products: 45.5 us -> none  [the longest x1 4.75 us: body(): jnp.einsum('tpf,tpd->fd', hidden, grad_ffn, preferred_element_type=jnp.fl...]
    all_gather x1 -> x0, blocking collectives: 43.1 us -> none  [body(): mod_rows = lax.all_gather(own_mod, 'dp', axis=0, tiled=True)]
    psum x1 -> x0, blocking collectives: 39.9 us -> none  [body(): lax.psum((qv_bias_grad, out_bias_grad, up_bias_grad, down_bias_grad, ada_...]
    pallas_call x0 -> x8, Pallas kernels: none -> 31.5 us  [call(): pl.pallas_call(kernel, out_shape=tuple((pinned.get(kind, jax.ShapeDtypeSt...]
    reshape x9 -> x0, local copies, waits for them, and re-layouts: 26.6 us -> none  [the longest x3 14.7 us: blocked(): local_term.reshape(dp_count, row_count // dp_count, seq_count, col_count...]
    ppermute x0 -> x16, waiting for transfers between devices: none -> 23.6 us  [the longest x9 17.8 us: rank_swap(): lax.ppermute(values, 'dp', [(rank, rank ^ step) for rank in range(count)])]
  transfers between devices with their start and end apart: 10 -> 17, of which waited for: 9 -> 9; matrix products, arithmetic and copies ran while one was open for 6% -> 2% of each run, Pallas kernels for 0% -> 12%
where the time goes in v1:
time: 87.2 us; the launch traced here: 86.9 us
  Pallas kernels  31.5 us (36%)
  waiting for transfers between devices  30.7 us (35%)
  starting transfers between devices  21.2 us (24%)
  local copies, waits for them, and re-layouts  1.44 us (2%)
  between operations  1.4 us (2%)
    pallas_call x8, Pallas kernels, call(): pl.pallas_call(kernel, out_shape=tuple((pinned.get(kind, jax.ShapeDtypeSt...  31.5 us
    ppermute x9, waiting for transfers between devices, rank_swap(): lax.ppermute(values, 'dp', [(rank, rank ^ step) for rank in range(count)])  17.8 us
    ppermute x9, starting transfers between devices, rank_swap(): lax.ppermute(values, 'dp', [(rank, rank ^ step) for rank in range(count)])  11.6 us
    all_to_all x1, starting transfers between devices, body(): cond_blocks = lax.all_to_all(block, 'dp', 0, 0, tiled=True)  8.29 us
    all_to_all x1, waiting for transfers between devices, body(): cond_blocks = lax.all_to_all(block, 'dp', 0, 0, tiled=True)  7.02 us
    ppermute x7, waiting for transfers between devices, swap_cores(): return lax.ppermute(values, 'seq', CORE_SWAP)  5.81 us
  transfers between devices with their start and end apart: 17, of which 9 were waited for; matrix products, arithmetic and copies ran while one was open for 2% of the time, Pallas kernels for 12%

profile of v1, /device:TPU:0, one launch (start us, length us, event | category | flops | bytes accessed | tf_op | source)
XLA Modules:
  0.0 86.9 jit_solution(10552233372771635969)
XLA Ops:
  0.6 0.5 collective-permute-start
  1.2 0.1 collective-permute-start.1
  1.2 0.8 slice_reduce_fusion.1
  2.0 0.7 select_select_fusion
  2.7 8.3 %all-to-all-start = ((bf16[16,8,384]{2,1,0:T(8,128)(2,1)}), bf16[16,8,384]{2,1,0:T(8,128)(2,1)S(1)}, u32[]{:S(2)}, u32[]{:S(2)}) async-start(bf16[16,8,384]{2,1,0:T(8,128)(2,1)} %select_select_fusion), calls=%async_computation | async-start | bytes 196608 | tf_op jit(solution)/shard_map/all_to_all | solution.py:973
  11.7 7.0 %all-to-all-done.cond_hbm = bf16[16,8,384]{2,1,0:T(8,128)(2,1)S(1)} async-done(((bf16[16,8,384]{2,1,0:T(8,128)(2,1)}), bf16[16,8,384]{2,1,0:T(8,128)(2,1)S(1)}, u32[]{:S(2)}, u32[]{:S(2)}) %all-to-all-start) | async-done | bytes 98336 | tf_op jit(solution)/shard_map/all_to_all | solution.py:973
  18.7 0.0 collective-permute-done.tokens_far_hbm
  18.7 0.0 collective-permute-done.1.cot_far_hbm
  18.7 0.7 copy-done.2
  19.4 16.2 %forward_and_ffn_back.1 = (bf16[4,128,384]{2,1,0:T(8,128)(2,1)}, bf16[512,1152]{1,0:T(8,128)(2,1)}, bf16[512,384]{1,0:T(8,128)(2,1)}, f32[512,384]{1,0:T(8,128)}...) custom-call(bf16[4,128,384]{2,1,0:T(8,128)(2,1)} %tokens_hbm.1, ...), custom_call_target="tpu_custom_call" | custom-call | flops 1 | bytes 1 | tf_op jit(solution)/shard_map/forward_and_ffn_back/pallas_call | solution.py:842
  35.6 0.1 collective-permute-start.2
  35.7 3.3 %collective-permute-done.2.recv_ref = bf16[2000,384]{1,0:T(8,128)(2,1)S(1)} collective-permute-done((bf16[2000,384]{1,0:T(8,128)(2,1)S(1)}, bf16[2000,384]{1,0:T(8,128)(2,1)S(1)}, u32[]{:S(2)}, u32[]{:S(2)}) %collective-permute-start.2) | collective-permute-done | bytes 1536032 | tf_op jit(solution)/shard_map/ppermute | solution.py:815
  39.0 0.3 split_plane.1
  39.3 1.0 %collective-permute-start.3 = (bf16[456,384]{1,0:T(8,128)(2,1)S(1)}, bf16[456,384]{1,0:T(8,128)(2,1)S(1)}, u32[]{:S(2)}, u32[]{:S(2)}) collective-permute-start(bf16[456,384]{1,0:T(8,128)(2,1)S(1)} %get-tuple-element.64), channel_id=1, source_target_pairs={{0,2},{2,0},{4,6},{6,4},{8,10},{10,8},{12,14},{14,12},{16,18},{18,... | collective-permute-start | bytes 1050632 | tf_op jit(solution)/shard_map/ppermute | solution.py:859
  40.3 0.3 collective-permute-start.4
  40.6 2.2 %collective-permute-start.5 = (bf16[456,384]{1,0:T(8,128)(2,1)S(1)}, bf16[456,384]{1,0:T(8,128)(2,1)S(1)}, u32[]{:S(2)}, u32[]{:S(2)}) collective-permute-start(bf16[456,384]{1,0:T(8,128)(2,1)S(1)} %get-tuple-element.66.after_ref), channel_id=1, source_target_pairs={{0,6},{2,4},{4,2},{6,0},{8,14},{10,12},{12,10},{14,8},{16,22},{18,... | collective-permute-start | bytes 1050632 | tf_op jit(solution)/shard_map/ppermute | solution.py:859
  42.9 9.2 %attention_back.1 = (bf16[4,128,384]{2,1,0:T(8,128)(2,1)}, bf16[2,128,384]{2,1,0:T(8,128)(2,1)S(1)}, bf16[512,384]{1,0:T(8,128)(2,1)S(1)}, bf16[512,1152]{1,0:T(8,128)(2,1)S(1)}, f32[8,384]{1,0:T(8,128)S(1)}) custom-call(bf16[2,256,384]{2,1,0:T(8,128)(2,1)} %get-tuple-element.67.images_hbm, f32[8,256]{1,0:T(8,128)} %get-tuple-element.68.penalty_hbm, ...), custom_call_target="tpu_custom_call" | custom-call | flops 1 | bytes 1 | tf_op jit(solution)/shard_map/attention_back/pallas_call | solution.py:842
  52.0 0.9 %qkv_back.1 = (f32[576,384]{1,0:T(8,128)S(1)}, bf16[288,384]{1,0:T(8,128)(2,1)S(1)}, bf16[296,384]{1,0:T(8,128)(2,1)S(1)}) custom-call(bf16[512,384]{1,0:T(8,128)(2,1)S(1)} %get-tuple-element.73.h1_ref, bf16[512,1152]{1,0:T(8,128)(2,1)S(1)} %get-tuple-element.74.gqkv_ref, f32[8,384]{1,0:T(8,128)S(1)} %get-tuple-element.75.small_ref), custom_call_target="tpu_custom_call" | custom-call | flops 1 | bytes 1 | tf_op jit(solution)/shard_map/qkv_back/pallas_call | solution.py:842
  52.9 0.1 collective-permute-start.7
  53.0 0.5 collective-permute-start.6
  53.5 1.3 %collective-permute-done.6.recv_ref = bf16[288,384]{1,0:T(8,128)(2,1)S(1)} collective-permute-done((bf16[288,384]{1,0:T(8,128)(2,1)S(1)}, bf16[288,384]{1,0:T(8,128)(2,1)S(1)}, u32[]{:S(2)}, u32[]{:S(2)}) %collective-permute-start.6) | collective-permute-done | bytes 221216 | tf_op jit(solution)/shard_map/ppermute | solution.py:815
  54.8 0.0 collective-permute-done.7.other_ref
  54.8 0.0 collective-permute-done.3.refs_0_.refs_1_
  54.8 3.0 %collective-permute-done.4.refs_1_.refs_2_ = bf16[456,384]{1,0:T(8,128)(2,1)S(1)} collective-permute-done((bf16[456,384]{1,0:T(8,128)(2,1)S(1)}, bf16[456,384]{1,0:T(8,128)(2,1)S(1)}, u32[]{:S(2)}, u32[]{:S(2)}) %collective-permute-start.4) | collective-permute-done | bytes 350240 | tf_op jit(solution)/shard_map/ppermute | solution.py:859
  57.8 0.0 collective-permute-done.5.refs_2_.refs_3_
  57.8 0.2 split_qkv_plane.1
  58.0 0.0 copy-start.1
  58.0 1.1 %collective-permute-start.8 = (bf16[160,384]{1,0:T(8,128)(2,1)S(1)}, bf16[160,384]{1,0:T(8,128)(2,1)S(1)}, u32[]{:S(2)}, u32[]{:S(2)}) collective-permute-start(bf16[160,384]{1,0:T(8,128)(2,1)S(1)} %get-tuple-element.80), channel_id=1, source_target_pairs={{0,2},{2,0},{4,6},{6,4},{8,10},{10,8},{12,14},{14,12},{16,18},{18,... | collective-permute-start | bytes 368648 | tf_op jit(solution)/shard_map/ppermute | solution.py:859
  59.1 0.7 collective-permute-start.9
  59.8 1.7 %collective-permute-start.10 = (bf16[160,384]{1,0:T(8,128)(2,1)S(1)}, bf16[160,384]{1,0:T(8,128)(2,1)S(1)}, u32[]{:S(2)}, u32[]{:S(2)}) collective-permute-start(bf16[160,384]{1,0:T(8,128)(2,1)S(1)} %get-tuple-element.82), channel_id=1, source_target_pairs={{0,6},{2,4},{4,2},{6,0},{8,14},{10,12},{12,10},{14,8},{16,22},{18,... | collective-permute-start | bytes 368648 | tf_op jit(solution)/shard_map/ppermute | solution.py:859
  61.5 0.0 collective-permute-start.14
  61.6 2.0 %collective-permute-done.8.refs_5_ = bf16[160,384]{1,0:T(8,128)(2,1)S(1)} collective-permute-done((bf16[160,384]{1,0:T(8,128)(2,1)S(1)}, bf16[160,384]{1,0:T(8,128)(2,1)S(1)}, u32[]{:S(2)}, u32[]{:S(2)}) %collective-permute-start.8) | collective-permute-done | bytes 122912 | tf_op jit(solution)/shard_map/ppermute | solution.py:859
  63.5 2.8 %collective-permute-done.9.refs_6_ = bf16[160,384]{1,0:T(8,128)(2,1)S(1)} collective-permute-done((bf16[160,384]{1,0:T(8,128)(2,1)S(1)}, bf16[160,384]{1,0:T(8,128)(2,1)S(1)}, u32[]{:S(2)}, u32[]{:S(2)}) %collective-permute-start.9) | collective-permute-done | bytes 122912 | tf_op jit(solution)/shard_map/ppermute | solution.py:859
  66.3 0.0 collective-permute-done.10.refs_7_
  66.3 0.7 fold_plane.1
  67.0 0.5 collective-permute-start.11
  67.5 1.0 %collective-permute-start.12 = (bf16[216,384]{1,0:T(8,128)(2,1)S(1)}, bf16[216,384]{1,0:T(8,128)(2,1)S(1)}, u32[]{:S(2)}, u32[]{:S(2)}) collective-permute-start(bf16[216,384]{1,0:T(8,128)(2,1)S(1)} %get-tuple-element.86), channel_id=1, source_target_pairs={{0,16},{2,18},{4,20},{6,22},{8,24},{10,26},{12,28},{14,30},{16,0},... | collective-permute-start | bytes 497672 | tf_op jit(solution)/shard_map/ppermute | solution.py:859
  68.5 3.0 %collective-permute-start.13 = (bf16[216,384]{1,0:T(8,128)(2,1)S(1)}, bf16[216,384]{1,0:T(8,128)(2,1)S(1)}, u32[]{:S(2)}, u32[]{:S(2)}) collective-permute-start(bf16[216,384]{1,0:T(8,128)(2,1)S(1)} %get-tuple-element.87), channel_id=1, source_target_pairs={{0,24},{2,26},{4,28},{6,30},{8,16},{10,18},{12,20},{14,22},{16,8},... | collective-permute-start | bytes 497672 | tf_op jit(solution)/shard_map/ppermute | solution.py:859
  71.4 0.0 collective-permute-done.14.far_ref
  71.4 3.1 %collective-permute-done.11.one_ref = bf16[216,384]{1,0:T(8,128)(2,1)S(1)} collective-permute-done((bf16[216,384]{1,0:T(8,128)(2,1)S(1)}, bf16[216,384]{1,0:T(8,128)(2,1)S(1)}, u32[]{:S(2)}, u32[]{:S(2)}) %collective-permute-start.11) | collective-permute-done | bytes 165920 | tf_op jit(solution)/shard_map/ppermute | solution.py:859
  74.5 7.0 %collective-permute-done.12.two_ref = bf16[216,384]{1,0:T(8,128)(2,1)S(1)} collective-permute-done((bf16[216,384]{1,0:T(8,128)(2,1)S(1)}, bf16[216,384]{1,0:T(8,128)(2,1)S(1)}, u32[]{:S(2)}, u32[]{:S(2)}) %collective-permute-start.12) | collective-permute-done | bytes 165920 | tf_op jit(solution)/shard_map/ppermute | solution.py:859
  81.5 0.0 collective-permute-done.13.three_ref
  81.5 0.0 copy-done.1
  81.5 3.4 %late_groups.1 = (bf16[4,128,384]{2,1,0:T(8,128)(2,1)}, bf16[4,128,384]{2,1,0:T(8,128)(2,1)}, f32[24,768]{1,0:T(8,128)}, f32[24,192]{1,0:T(8,128)}, f32[96,192]{...) custom-call(f32[144,384]{1,0:T(8,128)S(1)} %get-tuple-element.83.own, ...), custom_call_target="tpu_custom_call", output_to_operand_aliasing={{0}: (9, {}), {1}: (10, {})} | custom-call | flops 1 | bytes 1 | tf_op jit(solution)/shard_map/late_groups/pallas_call | solution.py:842
  85.0 0.1 collective-permute-start.15
  85.0 1.2 %collective-permute-done.15.recv_ref = f32[8,384]{1,0:T(8,128)S(1)} collective-permute-done((f32[8,384]{1,0:T(8,128)S(1)}, f32[8,384]{1,0:T(8,128)S(1)}, u32[]{:S(2)}, u32[]{:S(2)}) %collective-permute-start.15) | collective-permute-done | bytes 12320 | tf_op jit(solution)/shard_map/ppermute | solution.py:815
  86.2 0.0 copy-done
  86.2 0.7 final_groups.1
  (3 shorter events, 0.0 us)
Async XLA Ops:
  0.6 18.1 %collective-permute-start = (bf16[4,128,384]{2,1,0:T(8,128)(2,1)}, bf16[4,128,384]{2,1,0:T(8,128)(2,1)S(1)}, u32[]{:S(2)}, u32[]{:S(2)}) collective-permute-start(bf16[4,128,384]{2,1,0:T(8,128)(2,1)} %tokens_hbm.1), channel_id=1, source_target_pairs={{0,1},{1,0},{2,3},{3,2},{4,5},{5,4},{6,7},{7,6},{8,9},{9,8},{10,11... | collective-permute-start | bytes 1179656 | tf_op jit(solution)/shard_map/ppermute | solution.py:815
  1.2 17.6 %collective-permute-start.1 = (bf16[4,128,384]{2,1,0:T(8,128)(2,1)}, bf16[4,128,384]{2,1,0:T(8,128)(2,1)S(1)}, u32[]{:S(2)}, u32[]{:S(2)}) collective-permute-start(bf16[4,128,384]{2,1,0:T(8,128)(2,1)} %cot_hbm.1), channel_id=1, source_target_pairs={{0,1},{1,0},{2,3},{3,2},{4,5},{5,4},{6,7},{7,6},{8,9},{9,8},{10,11... | collective-permute-start | bytes 1179656 | tf_op jit(solution)/shard_map/ppermute | solution.py:815
  2.7 16.0 %all-to-all-start = ((bf16[16,8,384]{2,1,0:T(8,128)(2,1)}), bf16[16,8,384]{2,1,0:T(8,128)(2,1)S(1)}, u32[]{:S(2)}, u32[]{:S(2)}) async-start(bf16[16,8,384]{2,1,0:T(8,128)(2,1)} %select_select_fusion), calls=%async_computation | async-start | bytes 196608 | tf_op jit(solution)/shard_map/all_to_all | solution.py:973
  18.7 0.7 copy-start.2
  35.6 3.4 %collective-permute-start.2 = (bf16[2000,384]{1,0:T(8,128)(2,1)S(1)}, bf16[2000,384]{1,0:T(8,128)(2,1)S(1)}, u32[]{:S(2)}, u32[]{:S(2)}) collective-permute-start(bf16[2000,384]{1,0:T(8,128)(2,1)S(1)} %get-tuple-element.61), channel_id=1, source_target_pairs={{0,1},{1,0},{2,3},{3,2},{4,5},{5,4},{6,7},{7,6},{8,9},{9,8},{10,11... | collective-permute-start | bytes 4608008 | tf_op jit(solution)/shard_map/ppermute | solution.py:815
  39.3 15.5 %collective-permute-start.3 = (bf16[456,384]{1,0:T(8,128)(2,1)S(1)}, bf16[456,384]{1,0:T(8,128)(2,1)S(1)}, u32[]{:S(2)}, u32[]{:S(2)}) collective-permute-start(bf16[456,384]{1,0:T(8,128)(2,1)S(1)} %get-tuple-element.64), channel_id=1, source_target_pairs={{0,2},{2,0},{4,6},{6,4},{8,10},{10,8},{12,14},{14,12},{16,18},{18,... | collective-permute-start | bytes 1050632 | tf_op jit(solution)/shard_map/ppermute | solution.py:859
  40.3 17.5 %collective-permute-start.4 = (bf16[456,384]{1,0:T(8,128)(2,1)S(1)}, bf16[456,384]{1,0:T(8,128)(2,1)S(1)}, u32[]{:S(2)}, u32[]{:S(2)}) collective-permute-start(bf16[456,384]{1,0:T(8,128)(2,1)S(1)} %get-tuple-element.65), channel_id=1, source_target_pairs={{0,4},{2,6},{4,0},{6,2},{8,12},{10,14},{12,8},{14,10},{16,20},{18,... | collective-permute-start | bytes 1050632 | tf_op jit(solution)/shard_map/ppermute | solution.py:859
  40.6 17.2 %collective-permute-start.5 = (bf16[456,384]{1,0:T(8,128)(2,1)S(1)}, bf16[456,384]{1,0:T(8,128)(2,1)S(1)}, u32[]{:S(2)}, u32[]{:S(2)}) collective-permute-start(bf16[456,384]{1,0:T(8,128)(2,1)S(1)} %get-tuple-element.66.after_ref), channel_id=1, source_target_pairs={{0,6},{2,4},{4,2},{6,0},{8,14},{10,12},{12,10},{14,8},{16,22},{18,... | collective-permute-start | bytes 1050632 | tf_op jit(solution)/shard_map/ppermute | solution.py:859
  52.9 1.9 %collective-permute-start.7 = (bf16[296,384]{1,0:T(8,128)(2,1)S(1)}, bf16[296,384]{1,0:T(8,128)(2,1)S(1)}, u32[]{:S(2)}, u32[]{:S(2)}) collective-permute-start(bf16[296,384]{1,0:T(8,128)(2,1)S(1)} %get-tuple-element.78), channel_id=1, source_target_pairs={{0,1},{1,0},{2,3},{3,2},{4,5},{5,4},{6,7},{7,6},{8,9},{9,8},{10,11... | collective-permute-start | bytes 681992 | tf_op jit(solution)/shard_map/ppermute | solution.py:815
  53.0 1.8 %collective-permute-start.6 = (bf16[288,384]{1,0:T(8,128)(2,1)S(1)}, bf16[288,384]{1,0:T(8,128)(2,1)S(1)}, u32[]{:S(2)}, u32[]{:S(2)}) collective-permute-start(bf16[288,384]{1,0:T(8,128)(2,1)S(1)} %get-tuple-element.77), channel_id=1, source_target_pairs={{0,1},{1,0},{2,3},{3,2},{4,5},{5,4},{6,7},{7,6},{8,9},{9,8},{10,11... | collective-permute-start | bytes 663560 | tf_op jit(solution)/shard_map/ppermute | solution.py:815
  58.0 23.5 %copy-start.1 = (bf16[24,128]{1,0:T(8,128)(2,1)S(1)}, bf16[24,128]{1,0:T(8,128)(2,1)}, u32[]{:S(2)}) copy-start(bf16[24,128]{1,0:T(8,128)(2,1)} %get-tuple-element.88.lead_ref) | copy-start | bytes 18436
  58.0 5.5 %collective-permute-start.8 = (bf16[160,384]{1,0:T(8,128)(2,1)S(1)}, bf16[160,384]{1,0:T(8,128)(2,1)S(1)}, u32[]{:S(2)}, u32[]{:S(2)}) collective-permute-start(bf16[160,384]{1,0:T(8,128)(2,1)S(1)} %get-tuple-element.80), channel_id=1, source_target_pairs={{0,2},{2,0},{4,6},{6,4},{8,10},{10,8},{12,14},{14,12},{16,18},{18,... | collective-permute-start | bytes 368648 | tf_op jit(solution)/shard_map/ppermute | solution.py:859
  59.1 7.2 %collective-permute-start.9 = (bf16[160,384]{1,0:T(8,128)(2,1)S(1)}, bf16[160,384]{1,0:T(8,128)(2,1)S(1)}, u32[]{:S(2)}, u32[]{:S(2)}) collective-permute-start(bf16[160,384]{1,0:T(8,128)(2,1)S(1)} %get-tuple-element.81), channel_id=1, source_target_pairs={{0,4},{2,6},{4,0},{6,2},{8,12},{10,14},{12,8},{14,10},{16,20},{18,... | collective-permute-start | bytes 368648 | tf_op jit(solution)/shard_map/ppermute | solution.py:859
  59.8 6.5 %collective-permute-start.10 = (bf16[160,384]{1,0:T(8,128)(2,1)S(1)}, bf16[160,384]{1,0:T(8,128)(2,1)S(1)}, u32[]{:S(2)}, u32[]{:S(2)}) collective-permute-start(bf16[160,384]{1,0:T(8,128)(2,1)S(1)} %get-tuple-element.82), channel_id=1, source_target_pairs={{0,6},{2,4},{4,2},{6,0},{8,14},{10,12},{12,10},{14,8},{16,22},{18,... | collective-permute-start | bytes 368648 | tf_op jit(solution)/shard_map/ppermute | solution.py:859
  61.5 9.9 %collective-permute-start.14 = (bf16[2,128,384]{2,1,0:T(8,128)(2,1)S(1)}, bf16[2,128,384]{2,1,0:T(8,128)(2,1)S(1)}, u32[]{:S(2)}, u32[]{:S(2)}) collective-permute-start(bf16[2,128,384]{2,1,0:T(8,128)(2,1)S(1)} %get-tuple-element.89), channel_id=1, source_target_pairs={{0,1},{1,0},{2,3},{3,2},{4,5},{5,4},{6,7},{7,6},{8,9},{9,8},{10,11... | collective-permute-start | bytes 589832 | tf_op jit(solution)/shard_map/ppermute | solution.py:815
  67.0 7.5 %collective-permute-start.11 = (bf16[216,384]{1,0:T(8,128)(2,1)S(1)}, bf16[216,384]{1,0:T(8,128)(2,1)S(1)}, u32[]{:S(2)}, u32[]{:S(2)}) collective-permute-start(bf16[216,384]{1,0:T(8,128)(2,1)S(1)} %get-tuple-element.85), channel_id=1, source_target_pairs={{0,8},{2,10},{4,12},{6,14},{8,0},{10,2},{12,4},{14,6},{16,24},{18,... | collective-permute-start | bytes 497672 | tf_op jit(solution)/shard_map/ppermute | solution.py:859
  67.5 14.0 %collective-permute-start.12 = (bf16[216,384]{1,0:T(8,128)(2,1)S(1)}, bf16[216,384]{1,0:T(8,128)(2,1)S(1)}, u32[]{:S(2)}, u32[]{:S(2)}) collective-permute-start(bf16[216,384]{1,0:T(8,128)(2,1)S(1)} %get-tuple-element.86), channel_id=1, source_target_pairs={{0,16},{2,18},{4,20},{6,22},{8,24},{10,26},{12,28},{14,30},{16,0},... | collective-permute-start | bytes 497672 | tf_op jit(solution)/shard_map/ppermute | solution.py:859
  68.5 13.0 %collective-permute-start.13 = (bf16[216,384]{1,0:T(8,128)(2,1)S(1)}, bf16[216,384]{1,0:T(8,128)(2,1)S(1)}, u32[]{:S(2)}, u32[]{:S(2)}) collective-permute-start(bf16[216,384]{1,0:T(8,128)(2,1)S(1)} %get-tuple-element.87), channel_id=1, source_target_pairs={{0,24},{2,26},{4,28},{6,30},{8,16},{10,18},{12,20},{14,22},{16,8},... | collective-permute-start | bytes 497672 | tf_op jit(solution)/shard_map/ppermute | solution.py:859
  81.5 4.7 %copy-start = (bf16[2,384]{1,0:T(2,128)(2,1)S(1)}, bf16[2,384]{1,0:T(2,128)(2,1)}, u32[]{:S(2)}) copy-start(bf16[2,384]{1,0:T(2,128)(2,1)} %own_cond_ref.1) | copy-start | bytes 4612
  85.0 1.2 %collective-permute-start.15 = (f32[8,384]{1,0:T(8,128)S(1)}, f32[8,384]{1,0:T(8,128)S(1)}, u32[]{:S(2)}, u32[]{:S(2)}) collective-permute-start(f32[8,384]{1,0:T(8,128)S(1)} %get-tuple-element.95), channel_id=1, source_target_pairs={{0,1},{1,0},{2,3},{3,2},{4,5},{5,4},{6,7},{7,6},{8,9},{9,8},{10,11... | collective-permute-start | bytes 36872 | tf_op jit(solution)/shard_map/ppermute | solution.py:815

commit v2 on v1

v2 whole, which is shorter than its diff:
```python
from functools import partial

import jax
import jax.numpy as jnp
from jax import lax
from jax.experimental import pallas as pl
from jax.experimental.pallas import tpu as pltpu
from jax.sharding import PartitionSpec as P

HEADS = 6
HEAD_DIM = 64
PAIR = 2 * HEAD_DIM
CORE_SWAP = ((0, 1), (1, 0))
CHUNK = 256
LANES = 128
GROUPS_PER_RANK = 2
GENERAL = False
F32 = jnp.float32
LOW = jnp.bfloat16


def nn(left, right):
    return lax.dot_general(left, right, (((1,), (0,)), ((), ())), preferred_element_type=F32)


def nt(left, right):
    return lax.dot_general(left, right, (((1,), (1,)), ((), ())), preferred_element_type=F32)


def tn(left, right):
    return lax.dot_general(left, right, (((0,), (0,)), ((), ())), preferred_element_type=F32)


def normalize(values):
    center = values - jnp.mean(values, axis=-1, keepdims=True)
    spread = jnp.mean(center * center, axis=-1, keepdims=True)
    inverse = lax.rsqrt(spread + 1e-06)
    return center * inverse, inverse


def norm_back(grad, normed, inverse):
    return inverse * (
        grad
        - jnp.mean(grad, axis=-1, keepdims=True)
        - normed * jnp.mean(grad * normed, axis=-1, keepdims=True)
    )


def column_sum(values):
    return jnp.sum(values, axis=0, keepdims=True)


def head_masks(rows):
    lane = lax.broadcasted_iota(jnp.int32, (rows, PAIR), 1)
    return lane < HEAD_DIM, lane >= HEAD_DIM


def masked(values, mask):
    return jnp.where(mask, values, jnp.zeros_like(values))


def softmax_rows(queries, keys, penalty):
    scores = nt(queries, keys) + penalty
    exps = jnp.exp(scores - jnp.max(scores, axis=-1, keepdims=True))
    return exps / jnp.sum(exps, axis=-1, keepdims=True)


def fetch(pairs, sems):
    copies = []
    for index, (source, target) in enumerate(pairs):
        copy = pltpu.make_async_copy(source, target, sems.at[index])
        copy.start()
        copies.append(copy)
    return copies


def own_images(near_ref, far_ref, target_ref, first_image):
    half_len = near_ref.shape[1]
    pairs = []
    for image in range(target_ref.shape[0]):
        slot = first_image + image
        pairs.append((near_ref.at[slot], target_ref.at[image, pl.ds(0, half_len)]))
        pairs.append((far_ref.at[slot], target_ref.at[image, pl.ds(half_len, half_len)]))
    return pairs


def own_marks(mask_ref, counts_ref, core, image, image_count, half_len):
    slot = core * image_count + image
    live = jnp.where(slot < counts_ref[0], 1.0, 0.0)
    marks = mask_ref[pl.ds(slot, 1), :].astype(F32) * live
    low_marks, high_marks = marks[:, :half_len], marks[:, half_len:]
    return jnp.concatenate(
        [
            jnp.where(core == 0, low_marks, high_marks),
            jnp.where(core == 0, high_marks, low_marks),
        ],
        axis=1,
    )


def as_row(ref):
    return ref[...].astype(F32).reshape(1, ref.shape[0])


def load_kernel(
    tokens_hbm,
    tokens_far_ref,
    cot_hbm,
    cot_far_ref,
    ids_hbm,
    counts_hbm,
    mask_hbm,
    qv_b_hbm,
    out_b_hbm,
    up_b_hbm,
    down_b_hbm,
    ada_w_hbm,
    ada_b_hbm,
    images_ref,
    normed_ref,
    penalty_ref,
    hot_ref,
    marks_ref,
    qkv_b_ref,
    out_b_ref,
    up_b_ref,
    down_b_ref,
    ada_w_ref,
    ada_b_ref,
    cot_images_hbm,
    inverse_hbm,
    cot_ref,
    inverse_ref,
    ids_ref,
    counts_ref,
    mask_ref,
    qv_b_ref,
    out_b_raw,
    up_b_raw,
    down_b_raw,
    ada_b_raw,
    sems,
):
    core = lax.axis_index("seq")
    image_count, length, width = images_ref.shape
    half_len = length // 2
    first_image = core * image_count
    copies = fetch(
        own_images(tokens_hbm, tokens_far_ref, images_ref, first_image)
        + [
            (ids_hbm, ids_ref),
            (counts_hbm, counts_ref),
            (mask_hbm, mask_ref),
            (qv_b_hbm, qv_b_ref),
            (out_b_hbm, out_b_raw),
            (up_b_hbm, up_b_raw),
            (down_b_hbm, down_b_raw),
            (ada_b_hbm, ada_b_raw),
        ]
        + own_images(cot_hbm, cot_far_ref, cot_ref, first_image)
        + [(ada_w_hbm, ada_w_ref)],
        sems,
    )
    token_copies = 2 * image_count
    for copy in copies[: token_copies + 8]:
        copy.wait()
    row = lax.broadcasted_iota(jnp.int32, hot_ref.shape, 0)
    column = lax.broadcasted_iota(jnp.int32, hot_ref.shape, 1)
    hot = jnp.zeros(hot_ref.shape, F32)
    marks_ref[...] = jnp.zeros_like(marks_ref)
    penalty_ref[...] = jnp.zeros_like(penalty_ref)
    for image in range(image_count):
        group = ids_ref[first_image + image]
        place = 8 * (group // GROUPS_PER_RANK) + group % GROUPS_PER_RANK
        hot = jnp.where((row == image) & (column == place), 1.0, hot)
        marks_ref[image : image + 1, :] = jnp.full((1, width), group.astype(F32), F32)
        marks = own_marks(mask_ref, counts_ref, core, image, image_count, half_len)
        penalty_ref[image : image + 1, :] = (marks - 1.0) * 30000.0
        rows = slice(image * length, (image + 1) * length)
        normed, inverse = normalize(images_ref[image].astype(F32))
        normed_ref[rows, :] = normed
        inverse_ref[rows, :] = jnp.broadcast_to(inverse, (length, LANES))
    hot_ref[...] = hot.astype(LOW)
    qkv_b_ref[...] = jnp.concatenate(
        [qv_b_ref[0:1, :], jnp.zeros((1, width), LOW), qv_b_ref[1:2, :]], axis=1
    ).astype(F32)
    for raw, target in (
        (out_b_raw, out_b_ref),
        (up_b_raw, up_b_ref),
        (down_b_raw, down_b_ref),
        (ada_b_raw, ada_b_ref),
    ):
        target[...] = as_row(raw)
    for copy in copies[token_copies + 8 :]:
        copy.wait()
    for copy in fetch([(cot_ref, cot_images_hbm), (inverse_ref, inverse_hbm)], sems):
        copy.wait()


def attention_pair(step, qkv_ref, penalty_ref, length, width):
    image, pair = divmod(step, HEADS // 2)
    rows = slice(image * length, (image + 1) * length)

    def lanes(which):
        start = which * width + pair * PAIR
        return slice(start, start + PAIR)

    queries = qkv_ref[rows, lanes(0)] * jnp.asarray(HEAD_DIM**-0.5, LOW)
    return rows, lanes, queries, qkv_ref[rows, lanes(1)], qkv_ref[rows, lanes(2)]


def forward_kernel(
    lead_rows,
    cond_ref,
    images_ref,
    normed_ref,
    penalty_ref,
    hot_ref,
    marks_ref,
    qkv_b_ref,
    out_b_ref,
    up_b_ref,
    down_b_ref,
    ada_w_ref,
    ada_b_ref,
    cot_hbm,
    qkv_w_hbm,
    out_w_hbm,
    up_w_hbm,
    down_w_hbm,
    output_ref,
    qkv_ref,
    h1_ref,
    grad_att_ref,
    grad_mid_ref,
    mod_ref,
    lead_ref,
    qkv_w_ref,
    keep_ref,
    send_ref,
    small_ref,
    cond_rows_ref,
    turned_ref,
    att_ref,
    mid_ref,
    attn_ref,
    h2_ref,
    gffn_ref,
    act_ref,
    gpre_ref,
    valid_ref,
    cot_ref,
    out_w_ref,
    up_w_ref,
    down_w_ref,
    sems,
):
    core = lax.axis_index("seq")
    image_count, length, width = images_ref.shape
    half_len = length // 2
    half = width // 2
    ff_width = up_w_ref.shape[1]
    copies = fetch(
        [
            (qkv_w_hbm, qkv_w_ref),
            (out_w_hbm, out_w_ref),
            (cot_hbm, cot_ref),
            (up_w_hbm, up_w_ref),
            (down_w_hbm, down_w_ref),
        ],
        sems,
    )
    block_count, block_rows = cond_ref.shape[:2]
    cond_rows_ref[...] = jnp.zeros_like(cond_rows_ref)
    for block in range(block_count):
        cond_rows_ref[8 * block : 8 * block + block_rows, :] = cond_ref[block].astype(F32)
    cond = cond_rows_ref[...]
    silu = cond / (1.0 + jnp.exp(-cond))
    image_silu = nn(hot_ref[...], silu.astype(LOW)).astype(LOW)
    mod_ref[...] = (nn(image_silu, ada_w_ref[...]) + ada_b_ref[...]).astype(LOW)

    def part(image, which):
        return mod_ref[image : image + 1, which * width : (which + 1) * width].astype(F32)

    def rows_of(image):
        return slice(image * length, (image + 1) * length)

    def valid_of(image):
        column = valid_ref[rows_of(image), :]
        return jnp.concatenate([column] * (width // LANES), axis=1)

    copies[0].wait()
    for image in range(image_count):
        rows = rows_of(image)
        marks = jnp.where(penalty_ref[image : image + 1, :] < 0.0, 0.0, 1.0)
        valid_ref[rows, :] = jnp.broadcast_to(marks, (LANES, length)).T
        h1 = (normed_ref[rows, :] * (1.0 + part(image, 1)) + part(image, 0)).astype(LOW)
        h1_ref[rows, :] = h1
        qkv_ref[rows, :] = (nn(h1, qkv_w_ref[...]) + qkv_b_ref[...]).astype(LOW)

    first, second = head_masks(length)
    for step in range(image_count * (HEADS // 2)):
        rows, lanes, queries, keys, values = attention_pair(
            step, qkv_ref, penalty_ref, length, width
        )
        image = step // (HEADS // 2)
        penalty = penalty_ref[image : image + 1, :]
        total = jnp.zeros((length, PAIR), F32)
        for mask in (first, second):
            probs = softmax_rows(masked(queries, mask), keys, penalty).astype(LOW)
            total = total + nn(probs, masked(values, mask))
        att_ref[rows, lanes(0)] = total.astype(LOW)

    for copy in copies[1:]:
        copy.wait()
    if lead_rows:
        turned_ref[...] = silu.T
        start = pl.multiple_of(lax.axis_index("dp") * lead_rows, 8)
        lead_ref[...] = turned_ref[pl.ds(start, lead_rows), :].astype(LOW)
    else:
        lead_ref[...] = jnp.zeros_like(lead_ref)
    small_ref[...] = jnp.zeros_like(small_ref)
    small_ref[14:16, :] = marks_ref[:2, :]
    down_bias_grad = jnp.zeros((1, width), F32)
    for image in range(image_count):
        rows = rows_of(image)
        valid = valid_of(image)
        attn = nn(att_ref[rows, :], out_w_ref[...]) + out_b_ref[...]
        attn_ref[rows, :] = attn
        middle = images_ref[image].astype(F32) + valid * part(image, 2) * attn
        mid_ref[rows, :] = middle
        normed, _ = normalize(middle)
        h2_ref[rows, :] = (normed * (1.0 + part(image, 4)) + part(image, 3)).astype(LOW)
        grad_ffn = (valid * part(image, 5) * cot_ref[image].astype(F32)).astype(LOW)
        gffn_ref[rows, :] = grad_ffn
        down_bias_grad = down_bias_grad + column_sum(grad_ffn.astype(F32))
    small_ref[13:14, :] = down_bias_grad

    for chunk in range(ff_width // CHUNK):
        columns = slice(chunk * CHUNK, (chunk + 1) * CHUNK)
        up_w = up_w_ref[:, columns]
        down_w = down_w_ref[columns, :]
        bias = jnp.zeros((1, CHUNK), F32)
        for image in range(image_count):
            rows = rows_of(image)
            pre = nn(h2_ref[rows, :], up_w) + up_b_ref[:, columns]
            square = pre * pre
            inner = jnp.tanh(pre * (0.7978845608028654 + 0.035677408136300125 * square))
            cdf = 0.5 * inner + 0.5
            act_ref[rows, columns] = (pre * cdf).astype(LOW)
            slope = 0.5 * (pre * (0.7978845608028654 + 0.10703222440890037 * square)) * (
                1.0 - inner * inner
            ) + cdf
            grad_pre = (nt(gffn_ref[rows, :], down_w) * slope).astype(LOW)
            gpre_ref[rows, columns] = grad_pre
            bias = bias + column_sum(grad_pre.astype(F32))
        for tile in range(CHUNK // LANES):
            start = chunk * CHUNK + tile * LANES
            small_ref[9 + start // width : 10 + start // width, start % width : start % width + LANES] = (
                bias[:, tile * LANES : (tile + 1) * LANES]
            )

    first_half = gffn_ref[:, :half]
    second_half = gffn_ref[:, half:]
    gffn_keep = jnp.where(core == 0, first_half, second_half)
    gffn_send = jnp.where(core == 0, second_half, first_half)
    side_chunks = ff_width // CHUNK // 2
    for step in range(side_chunks):
        low = slice(step * CHUNK, (step + 1) * CHUNK)
        high = slice((step + side_chunks) * CHUNK, (step + side_chunks + 1) * CHUNK)
        up_low = tn(h2_ref[...], gpre_ref[:, low])
        up_high = tn(h2_ref[...], gpre_ref[:, high])
        up_keep = jnp.where(core == 0, up_low, up_high)
        up_send = jnp.where(core == 0, up_high, up_low).astype(LOW)
        for tile in range(CHUNK // LANES):
            start = step * CHUNK + tile * LANES
            rows = slice(start // width * width, (start // width + 1) * width)
            columns = slice(start % width, start % width + LANES)
            keep_ref[rows, columns] = up_keep[:, tile * LANES : (tile + 1) * LANES]
            send_ref[rows, columns] = up_send[:, tile * LANES : (tile + 1) * LANES]
        rows = slice(2 * width + step * CHUNK, 2 * width + (step + 1) * CHUNK)
        for target, side in ((keep_ref, gffn_keep), (send_ref, gffn_send)):
            target[rows, :] = jnp.concatenate(
                [tn(act_ref[:, low], side), tn(act_ref[:, high], side)], axis=1
            ).astype(target.dtype)

    out_bias_grad = jnp.zeros((1, width), F32)
    for image in range(image_count):
        rows = rows_of(image)
        valid = valid_of(image)
        upstream = cot_ref[image].astype(F32)
        middle = mid_ref[rows, :]
        ffn = nn(act_ref[rows, :], down_w_ref[...]) + down_b_ref[...]
        output_ref[image] = (middle + valid * part(image, 5) * ffn).astype(LOW)
        small_ref[6 + image : 7 + image, :] = column_sum(valid * ffn * upstream)
        normed, inverse = normalize(middle)
        grad_h2 = nt(gpre_ref[rows, :], up_w_ref[...])
        small_ref[2 + image : 3 + image, :] = column_sum(grad_h2)
        small_ref[4 + image : 5 + image, :] = column_sum(grad_h2 * normed)
        grad_mid = upstream + norm_back(grad_h2 * (1.0 + part(image, 4)), normed, inverse)
        grad_mid_ref[rows, :] = grad_mid
        small_ref[image : image + 1, :] = column_sum(valid * attn_ref[rows, :] * grad_mid)
        grad_attn = (valid * part(image, 2) * grad_mid).astype(LOW)
        h2_ref[rows, :] = grad_attn
        out_bias_grad = out_bias_grad + column_sum(grad_attn.astype(F32))
        grad_att_ref[rows, :] = nt(grad_attn, out_w_ref[...]).astype(LOW)
    small_ref[8:9, :] = out_bias_grad
    out_term = tn(att_ref[...], h2_ref[...])
    out_first = jnp.concatenate([out_term[:half, :half], out_term[half:, :half]], axis=1)
    out_second = jnp.concatenate([out_term[:half, half:], out_term[half:, half:]], axis=1)
    rows = slice(2 * width + ff_width // 2, 2 * width + ff_width // 2 + half)
    keep_ref[rows, :] = jnp.where(core == 0, out_first, out_second)
    send_ref[rows, :] = jnp.where(core == 0, out_second, out_first).astype(LOW)
    start = keep_ref.shape[0] + 16
    send_ref[start - 16 : start, :] = small_ref[...].astype(LOW)
    for image in range(image_count):
        rows = slice(start + image * half_len, start + (image + 1) * half_len)
        send_ref[rows, :] = output_ref[image, half_len:, :]


def backward_kernel(
    normed_ref,
    inverse_hbm,
    penalty_ref,
    qkv_w_ref,
    qkv_ref,
    h1_ref,
    grad_att_ref,
    grad_mid_ref,
    mod_ref,
    after_ref,
    grad_tokens_ref,
    keep_ref,
    send_ref,
    other_ref,
    small_ref,
    gqkv_ref,
    inverse_ref,
    sems,
):
    core = lax.axis_index("seq")
    copies = fetch([(inverse_hbm, inverse_ref)], sems)
    image_count, length, width = grad_tokens_ref.shape
    half_len = length // 2
    half = width // 2
    first, second = head_masks(length)
    for step in range(image_count * (HEADS // 2)):
        rows, lanes, queries, keys, values = attention_pair(
            step, qkv_ref, penalty_ref, length, width
        )
        image = step // (HEADS // 2)
        penalty = penalty_ref[image : image + 1, :]
        grad_att = grad_att_ref[rows, lanes(0)]
        grad_q = jnp.zeros((length, PAIR), F32)
        grad_k = jnp.zeros((length, PAIR), F32)
        grad_v = jnp.zeros((length, PAIR), F32)
        for mask in (first, second):
            own_queries = masked(queries, mask)
            own_grad = masked(grad_att, mask)
            probs = softmax_rows(own_queries, keys, penalty)
            grad_probs = nt(own_grad, values)
            dots = jnp.sum(probs * grad_probs, axis=-1, keepdims=True)
            grad_scores = (probs * (grad_probs - dots)).astype(LOW)
            grad_v = grad_v + tn(probs.astype(LOW), own_grad)
            grad_q = grad_q + nn(grad_scores, masked(keys, mask))
            grad_k = grad_k + tn(grad_scores, own_queries)
        gqkv_ref[rows, lanes(0)] = (grad_q * HEAD_DIM**-0.5).astype(LOW)
        gqkv_ref[rows, lanes(1)] = grad_k.astype(LOW)
        gqkv_ref[rows, lanes(2)] = grad_v.astype(LOW)

    def part(image, which):
        return mod_ref[image : image + 1, which * width : (which + 1) * width].astype(F32)

    small_ref[...] = jnp.zeros_like(small_ref)
    copies[0].wait()
    small_ref[4:5, :] = column_sum(gqkv_ref[:, :width].astype(F32))
    small_ref[5:6, :] = column_sum(gqkv_ref[:, 2 * width :].astype(F32))
    for image in range(image_count):
        rows = slice(image * length, (image + 1) * length)
        normed = normed_ref[rows, :]
        inverse = jnp.concatenate([inverse_ref[rows, :]] * (width // LANES), axis=1)
        grad_h1 = nt(gqkv_ref[rows, :], qkv_w_ref[...])
        small_ref[image : image + 1, :] = column_sum(grad_h1)
        small_ref[2 + image : 3 + image, :] = column_sum(grad_h1 * normed)
        grad_in = norm_back(grad_h1 * (1.0 + part(image, 1)), normed, inverse)
        grad_tokens_ref[image] = (grad_mid_ref[rows, :] + grad_in).astype(LOW)
    low_term = tn(h1_ref[...], gqkv_ref[:, :width])
    high_term = tn(h1_ref[...], gqkv_ref[:, 2 * width :])
    keep_ref[:width, :] = jnp.where(core == 0, low_term, high_term)
    pair = jnp.where(core == 0, high_term, low_term).astype(LOW)
    term = tn(h1_ref[...], gqkv_ref[:, width : 2 * width])
    low_unit = jnp.concatenate([term[:half, :half], term[half:, :half]], axis=1)
    high_unit = jnp.concatenate([term[:half, half:], term[half:, half:]], axis=1)
    keep_ref[width:, :] = jnp.where(core == 0, low_unit, high_unit)
    cut = width // 4 * 3
    send_ref[:cut, :] = pair[:cut]
    start = width - cut
    other_ref[:start, :] = pair[cut:]
    other_ref[start : start + half, :] = jnp.where(core == 0, high_unit, low_unit).astype(LOW)
    start += half
    other_ref[start : start + 8, :] = small_ref[...].astype(LOW)
    for index, (target, start) in enumerate(((send_ref, cut), (other_ref, start + 8))):
        target[start:, :] = grad_tokens_ref[index, half_len:, :]


def by_core(core, near, far):
    return [jnp.where(core == 0, near, far), jnp.where(core == 0, far, near)]


def split_kernel(
    keep_ref, recv_ref, small_ref, own_ref, one_ref, two_ref, three_ref, early_ref
):
    core = lax.axis_index("seq")
    width = keep_ref.shape[1]
    piece = width // 16
    long = 4 * piece
    start = keep_ref.shape[0]
    near = small_ref[...].astype(LOW).astype(F32)
    far = recv_ref[start : start + 16, :].astype(F32)
    first, second = by_core(core, near, far)
    mods = []
    for row in range(0, 6, 2):
        low_kind = [first[:2], second[:2]] if row == 0 else [jnp.zeros((4, width), F32)]
        high_kind = [first[row + 2 : row + 4], second[row + 2 : row + 4]]
        mods.append(
            jnp.where(
                core == 0, jnp.concatenate(low_kind, axis=0), jnp.concatenate(high_kind, axis=0)
            )
        )
    early_ref[...] = jnp.concatenate(
        mods + [first[8:14] + second[8:14], jnp.zeros((6, width), F32)], axis=0
    )
    lane = lax.broadcasted_iota(jnp.int32, (8, width), 1)
    ids = jnp.zeros((8, width), F32)
    for slot, block in enumerate((first[14:15], first[15:16], second[14:15], second[15:16])):
        ids = jnp.where(lane == slot, block, ids)
    for step, target in enumerate((own_ref, one_ref, two_ref, three_ref)):
        who = (lax.axis_index("dp") & 3) ^ step

        def move(start, size, to):
            rows = pl.ds(pl.multiple_of(start, 8), size)
            target[to : to + size, :] = (
                keep_ref[rows, :] + recv_ref[rows, :].astype(F32)
            ).astype(target.dtype)

        for z in range(4):
            for side in range(2):
                move(side * width + piece * (4 * z + who), piece, (2 * z + side) * piece)
        for z in range(2):
            move(2 * width + long * (4 * z + who), long, 8 * piece + z * long)
            move(2 * width + 8 * long + piece * (4 * z + who), piece, 16 * piece + z * piece)
        target[18 * piece :, :] = ids.astype(target.dtype)


def split_qkv_kernel(keep_ref, recv_ref, other_ref, small_ref, early_ref, *refs):
    core = lax.axis_index("seq")
    width = keep_ref.shape[1]
    piece = width // 16
    cut = width // 4 * 3
    near = small_ref[...].astype(LOW).astype(F32)
    start = keep_ref.shape[0] - cut
    far = other_ref[start : start + 8, :].astype(F32)
    first, second = by_core(core, near, far)
    early = early_ref[...]
    late = jnp.concatenate([first[0:2], second[0:2], first[2:4], second[2:4], early[:4]], axis=0)
    small = jnp.concatenate(
        [
            jnp.where(core == 0, late, early[:12]),
            early[12:18],
            first[4:6] + second[4:6],
            jnp.zeros((4, width), F32),
        ],
        axis=0,
    ).astype(LOW)
    total_ref = refs[-1]
    total_ref[:cut, :] = keep_ref[:cut, :] + recv_ref[:cut, :].astype(F32)
    total_ref[cut:, :] = keep_ref[cut:, :] + other_ref[:start, :].astype(F32)
    for step, target in enumerate(refs[-5:-1]):
        who = (lax.axis_index("dp") & 3) ^ step
        for z in range(6):
            start = width + piece * (4 * (z - 4) + who) if z >= 4 else piece * (4 * z + who)
            rows = pl.ds(pl.multiple_of(start, 8), piece)
            target[piece * z : piece * (z + 1), :] = total_ref[rows, :].astype(target.dtype)
        target[6 * piece :, :] = small.astype(target.dtype)


def summed(sources, rows):
    return sum((source[rows, :].astype(F32) for source in sources[1:]), sources[0][rows, :])


def fold_kernel(*refs):
    parts, after = refs[:4], refs[4]
    kept_ref, rest_ref, rest_small_ref = refs[5:8]
    sends = refs[8:11]
    total_ref, group_ref = refs[11:]
    width = total_ref.shape[1]
    piece = width // 16
    long = 4 * piece
    half = width // 2
    total_ref[...] = summed(parts, slice(0, 16 * piece))
    for step, part in enumerate(parts):
        group_ref[(lax.axis_index("dp") & 3) ^ step] = part[18 * piece :, :].astype(F32)
    kept_ref[...] = summed(parts, slice(16 * piece, 18 * piece))
    ids = [group_ref[q, 0:1] for q in range(4)] + [jnp.zeros((4, width), F32)]
    small = jnp.concatenate(ids, axis=0).astype(LOW)
    rest_small_ref[...] = small
    for step, target in enumerate((rest_ref,) + tuple(sends)):
        who = (lax.axis_index("dp") >> 2) ^ step
        rows = pl.ds(pl.multiple_of(2 * piece * who, 8), 2 * piece)
        target[: 2 * piece, :] = total_ref[rows, :].astype(target.dtype)
        rows = pl.ds(pl.multiple_of(8 * piece + long * (who % 2), 8), long)
        down = total_ref[rows, :]
        down = jnp.where(who < 2, down[:, :half], down[:, half:])
        down = jnp.concatenate([down[: 2 * piece], down[2 * piece :]], axis=1)
        target[2 * piece : 4 * piece, :] = down.astype(target.dtype)
        if step:
            target[4 * piece :, :] = small


def fold_qkv_kernel(*refs):
    parts, kept_ref = refs[:4], refs[4]
    rest_ref, rest_small_ref = refs[5:7]
    sends = refs[7:10]
    total_ref, late_ref = refs[10:]
    width = total_ref.shape[1]
    piece = width // 16
    half = width // 2
    total_ref[: 6 * piece, :] = summed(parts, slice(0, 6 * piece))
    total_ref[6 * piece :, :] = kept_ref[...]
    for step, part in enumerate(parts):
        late_ref[(lax.axis_index("dp") & 3) ^ step] = part[6 * piece :, :].astype(F32)
    rows = [late_ref[q, :12] for q in range(4)]
    rows.append(late_ref[0, 12:20] + late_ref[1, 12:20] + late_ref[2, 12:20] + late_ref[3, 12:20])
    small = jnp.concatenate(rows, axis=0).astype(LOW)
    rest_small_ref[...] = small
    for step, target in enumerate((rest_ref,) + tuple(sends)):
        who = (lax.axis_index("dp") >> 2) ^ step

        def side(start):
            value = total_ref[pl.ds(pl.multiple_of(piece * (start + who % 2), 8), piece), :]
            return jnp.where(who < 2, value[:, :half], value[:, half:])

        target[:piece, :] = jnp.concatenate([side(6), side(4)], axis=1).astype(target.dtype)
        pair = total_ref[pl.ds(pl.multiple_of(piece * who, 8), piece), :]
        target[piece : 2 * piece, :] = pair.astype(target.dtype)
        if step:
            target[2 * piece :, :] = small


def one_hot(ids, lead):
    place = lax.broadcasted_iota(jnp.int32, (lead.shape[1], ids.shape[1]), 0)
    wanted = (ids // GROUPS_PER_RANK) * 8 + ids % GROUPS_PER_RANK
    return jnp.where(place == wanted, 1.0, 0.0).astype(LOW)


def group_parts(silu_rows, own_groups, kinds, kind_of):
    zeros = jnp.zeros_like(kind_of, F32)
    blocks = [masked(silu_rows, kind_of == kind) for kind in kinds]
    rows = []
    for kind in kinds:
        for one in own_groups:
            rows.append(jnp.where((kind_of == kind) & one, 1.0, zeros))
    for kind in kinds:
        rows.append(jnp.where(kind_of == kind, 1.0, zeros))
    while len(rows) % 8:
        rows.append(zeros)
    return blocks, jnp.concatenate(rows, axis=0).astype(LOW)


def split_dot(values, weight):
    high = values.astype(LOW)
    low = (values - high.astype(F32)).astype(LOW)
    return nt(high, weight) + nt(low, weight)


def finish_kernel(
    own_ref,
    own_small_ref,
    one_ref,
    two_ref,
    three_ref,
    lead_ref,
    recv_one_ref,
    recv_two_ref,
    recv_other_ref,
    output_ref,
    grad_tokens_ref,
    output_to,
    grad_tokens_to,
    up_ref,
    down_ref,
    silu_ref,
    ids_ref,
    stack_ref,
    sems,
):
    core = lax.axis_index("seq")
    width = own_ref.shape[1]
    piece = width // 16
    half = width // 2
    slots, half_len = output_to.shape[:2]
    count = slots // 2
    pairs = []
    for index, source in enumerate((recv_two_ref, recv_other_ref)):
        slot = (1 - core) * count + index
        start = recv_one_ref.shape[0] - (count - index) * half_len
        pairs.append((recv_one_ref.at[pl.ds(start, half_len)], output_to.at[slot]))
        start = source.shape[0] - half_len
        pairs.append((source.at[pl.ds(start, half_len)], grad_tokens_to.at[slot]))
        slot = core * count + index
        pairs.append((output_ref.at[index, pl.ds(0, half_len)], output_to.at[slot]))
        pairs.append((grad_tokens_ref.at[index, pl.ds(0, half_len)], grad_tokens_to.at[slot]))
    copies = fetch(pairs, sems)
    parts = (own_ref, one_ref, two_ref, three_ref)
    total = summed(parts, slice(0, 4 * piece))
    up_ref[...] = jnp.concatenate([total[:piece], total[piece : 2 * piece]], axis=1)
    down = total[2 * piece :]
    down_ref[...] = jnp.concatenate([down[:, :half], down[:, half:]], axis=0)
    line = lax.axis_index("dp") >> 2
    smalls = (own_small_ref[...],) + tuple(part[4 * piece :, :] for part in parts[1:])
    for step, small in enumerate(smalls):
        stack_ref[line ^ step] = small[:, :LANES].astype(F32)
    stack = stack_ref[...].reshape(32, LANES).astype(LOW)
    count = 192
    row = lax.broadcasted_iota(jnp.int32, (32, count), 0)
    chip = lax.broadcasted_iota(jnp.int32, (32, count), 1) // 12
    spread = tn(stack, jnp.where(row == chip + 4 * (chip // 4), 1.0, 0.0).astype(LOW))[:8]
    slot = lax.broadcasted_iota(jnp.int32, (8, count), 0)
    wanted = lax.broadcasted_iota(jnp.int32, (8, count), 1) % 4
    ids = column_sum(jnp.where(slot == wanted, spread, 0.0)).astype(jnp.int32)
    ids_ref[...] = ids
    lead = lead_ref[...]
    silu_ref[...] = nn(lead, one_hot(ids, lead)).astype(LOW)
    for copy in copies:
        copy.wait()


def late_kernel(
    own_ref,
    own_small_ref,
    one_ref,
    two_ref,
    three_ref,
    silu_ref,
    ids_ref,
    ada_ref,
    out_ref,
    qkv_ref,
    ada_out_ref,
    own_sums_ref,
    send_ref,
    out_bias_ref,
    up_bias_ref,
    down_bias_ref,
    qv_ref,
    stack_ref,
    bias_ref,
):
    core = lax.axis_index("seq")
    width = own_ref.shape[1]
    piece = width // 16
    half = width // 2
    parts = (own_ref, one_ref, two_ref, three_ref)
    line = lax.axis_index("dp") >> 2
    smalls = (own_small_ref[...],) + tuple(part[2 * piece :, :] for part in parts[1:])
    for step, small in enumerate(smalls):
        stack_ref[line ^ step] = small[:48]
        bias_ref[line ^ step] = small[48:].astype(F32)
    stack = stack_ref[...].reshape(192, width)
    ids = ids_ref[...]
    item = lax.broadcasted_iota(jnp.int32, (1, 192), 1) % 12
    base = GROUPS_PER_RANK * lax.axis_index("dp")
    own = [ids == base + index for index in range(GROUPS_PER_RANK)]
    blocks, rows = group_parts(silu_ref[...], own, range(3), item // 4)
    sums = nn(rows, stack)
    for kind in range(3):
        ada_out_ref[:, kind * width : (kind + 1) * width] = nn(blocks[kind], stack)
    weight = ada_ref[:, pl.ds(pl.multiple_of(core * 3 * width, LANES), 3 * width)]
    own_sum = jnp.concatenate(
        [
            jnp.concatenate([sums[2 * kind : 2 * kind + 2] for kind in range(3)], axis=1),
            jnp.zeros((6, 3 * width), F32),
        ],
        axis=0,
    )
    cond = split_dot(own_sum, weight)
    low_cond, high_cond = cond[:2, :half], cond[:2, half:]
    kept = jnp.where(core == 0, low_cond, high_cond)
    sent = jnp.where(core == 0, high_cond, low_cond)
    zeros = jnp.zeros((2, half), F32)
    pad = jnp.zeros((3, width), F32)
    own_sums_ref[...] = jnp.concatenate(
        [jnp.concatenate([kept, zeros], axis=1), sums[6:9], pad], axis=0
    )
    send_ref[...] = jnp.concatenate(
        [jnp.concatenate([sent, zeros], axis=1), sums[6:9], pad], axis=0
    )
    bias = bias_ref[0] + bias_ref[1] + bias_ref[2] + bias_ref[3]
    out_bias_ref[...] = bias[0:1].reshape(width)
    up_bias_ref[...] = jnp.concatenate([bias[1 + row : 2 + row] for row in range(4)], axis=1).reshape(
        4 * width
    )
    down_bias_ref[...] = bias[5:6].reshape(width)
    qv_ref[...] = bias[6:8]
    total = summed(parts, slice(0, 2 * piece))
    out_ref[...] = total[:piece, :half]
    unit, pair = total[:piece, half:], total[piece:]
    qkv_ref[...] = jnp.where(
        core == 0,
        jnp.concatenate([pair, unit], axis=1),
        jnp.concatenate([unit, pair], axis=1),
    )


def final_kernel(own_ref, recv_ref, own_cond_ref, cond_ref, bias_ref):
    core = lax.axis_index("seq")
    width = own_ref.shape[1]
    half = width // 2
    near, far = own_ref[...], recv_ref[...]
    values = own_cond_ref[...].astype(F32)
    values = jnp.where(core == 0, values[:, :half], values[:, half:])
    gate = 1.0 / (1.0 + jnp.exp(-values))
    cond_ref[...] = (near[:2, :half] + far[:2, :half]) * (gate * (1.0 + values * (1.0 - gate)))
    rows = [block[row : row + 1] for block in by_core(core, near, far) for row in range(2, 5)]
    bias_ref[...] = jnp.concatenate(rows, axis=1).reshape(6 * width)


def silu_slope(values):
    sigmoid_val = jax.nn.sigmoid(values)
    return sigmoid_val * (1.0 + values * (1.0 - sigmoid_val))


def swap_cores(values):
    return lax.ppermute(values, "seq", CORE_SWAP)


def pick(core, first, second):
    return jnp.where(core == 0, first, second)


def to_patches(images, far, core):
    half_len = images.shape[1] // 2
    return pick(
        core,
        jnp.concatenate([images[:, :half_len], far], axis=0),
        jnp.concatenate([far, images[:, :half_len]], axis=0),
    )


def call(kernel, name, shapes, scratch, limit, spaces, *operands, aliases=None):
    chosen = {
        "s": pl.BlockSpec(memory_space=pltpu.SMEM),
        "v": pl.BlockSpec(memory_space=pltpu.VMEM),
        "V": pl.BlockSpec(memory_space=pltpu.VMEM),
        "a": pl.BlockSpec(memory_space=pl.ANY),
        "h": pl.BlockSpec(memory_space=pltpu.HBM),
    }
    pinned = {"h": pltpu.HBM, "V": pltpu.VMEM}
    into, out_of = spaces
    operands = [
        pltpu.with_memory_space_constraint(item, pinned[kind]) if kind in pinned else item
        for kind, item in zip(into, operands)
    ]
    return pl.pallas_call(
        kernel,
        out_shape=tuple(
            pinned.get(kind, jax.ShapeDtypeStruct)(shape, dtype)
            for kind, (shape, dtype) in zip(out_of, shapes)
        ),
        in_specs=[chosen[kind] for kind in into],
        out_specs=[chosen[kind] for kind in out_of],
        scratch_shapes=scratch,
        compiler_params=pltpu.CompilerParams(vmem_limit_bytes=limit << 20),
        cost_estimate=pl.CostEstimate(flops=1, bytes_accessed=1, transcendentals=0),
        input_output_aliases=aliases or {},
        name=name,
    )(*operands)


def rank_swap(values, step, count):
    return lax.ppermute(values, "dp", [(rank, rank ^ step) for rank in range(count)])


def owner_total(term, dp_count):
    blocks = term.astype(LOW).reshape(dp_count, term.shape[0] // dp_count, term.shape[1])
    return jnp.sum(lax.all_to_all(blocks, "dp", 0, 0, tiled=True).astype(F32), axis=0)


def general_tail(
    core, dp_count, dp_rank, sides, smalls, heads, cond_rows, cond, own_ids, ada_weight
):
    highest = lax.Precision.HIGHEST
    width, mod_width = ada_weight.shape
    half = width // 2
    (keep_one, send_one), (keep_two, send_two, send_other) = sides
    output, grad_tokens = heads
    small_one, small_two = smalls
    half_len = output.shape[1] // 2
    recv_one = swap_cores(send_one)
    first_sum = keep_one + recv_one[: keep_one.shape[0]].astype(F32)
    recv_two, recv_other = swap_cores(send_two), swap_cores(send_other)
    cut = width // 4 * 3
    second_sum = keep_two + jnp.concatenate(
        [recv_two[:cut], recv_other[: keep_two.shape[0] - cut]], axis=0
    ).astype(F32)
    output_far = recv_one[keep_one.shape[0] + 16 :].reshape(-1, half_len, width)
    grad_far = jnp.stack([item[-half_len:] for item in (recv_two, recv_other)])
    ff_half = first_sum.shape[0] - 2 * width - half
    up = jnp.concatenate([first_sum[:width], first_sum[width : 2 * width]], axis=1)
    down = first_sum[2 * width : 2 * width + ff_half]
    down = jnp.concatenate([down[:, :half], down[:, half:]], axis=0)
    out = first_sum[2 * width + ff_half :]
    out = jnp.concatenate([out[:, :half], out[:, half:]], axis=0)
    pair, unit = second_sum[:width], second_sum[width:]
    unit = jnp.concatenate([unit[:, :half], unit[:, half:]], axis=0)
    qkv = pick(
        core, jnp.concatenate([pair, unit], axis=1), jnp.concatenate([unit, pair], axis=1)
    )
    sums = [owner_total(term, dp_count) for term in (qkv, out, up, down)]
    image_grad = jnp.concatenate(
        [small_two[0:2], small_two[2:4], small_one[0:2], small_one[2:4], small_one[4:6], small_one[6:8]],
        axis=1,
    )
    biases = jnp.concatenate([small_two[4:6], small_one[8:14]], axis=0)
    marks = jnp.broadcast_to(own_ids.astype(F32)[:, None], (own_ids.shape[0], width))
    packed = jnp.concatenate([image_grad.reshape(-1, width), biases, marks], axis=0)
    gathered = lax.all_to_all(
        jnp.broadcast_to(packed[None], (2 * dp_count,) + packed.shape),
        ("dp", "seq"),
        0,
        0,
        tiled=True,
    )
    grad_rows = gathered[:, :12].reshape(-1, mod_width)
    bias_sums = jnp.sum(gathered[:, 12:20], axis=0)
    all_ids = gathered[:, 20:, 0].reshape(-1).astype(jnp.int32)
    group_count = cond_rows.shape[0]
    all_hot = (all_ids[:, None] == jnp.arange(group_count, dtype=jnp.int32)[None, :]).astype(F32)
    group_grad = jnp.dot(all_hot.T, grad_rows, precision=highest)
    own_rows = width // dp_count
    silu_rows = lax.reduce_precision(jax.nn.silu(cond_rows.astype(F32)), 8, 7)
    silu_part = lax.dynamic_slice_in_dim(silu_rows, dp_rank * own_rows, own_rows, 1)
    grad_half = pick(core, group_grad[:, : mod_width // 2], group_grad[:, mod_width // 2 :])
    ada_sum = jnp.dot(silu_part.T, grad_half, precision=highest)
    own_grad = lax.dynamic_slice_in_dim(
        group_grad, dp_rank * GROUPS_PER_RANK, GROUPS_PER_RANK, 0
    )
    ada_half = lax.dynamic_slice_in_dim(ada_weight, core * half, half, 0).astype(F32)
    cond_half = pick(core, cond[:, :half], cond[:, half:]).astype(F32)
    grad_cond = silu_slope(cond_half) * jnp.dot(own_grad, ada_half.T, precision=highest)
    return (
        to_patches(output, output_far, core),
        to_patches(grad_tokens, grad_far, core),
        grad_cond,
        sums[0],
        bias_sums[:2],
        sums[1],
        bias_sums[2],
        sums[2],
        bias_sums[3:7].reshape(-1),
        sums[3],
        bias_sums[7],
        ada_sum,
        jnp.sum(grad_rows, axis=0),
    )


def body(
    tokens,
    cotangent,
    cond,
    group_ids,
    image_counts,
    patch_mask,
    qkv_weight,
    qv_bias,
    out_weight,
    out_bias,
    up_weight,
    up_bias,
    down_weight,
    down_bias,
    ada_weight,
    ada_bias,
):
    slot_count, half_len, width = tokens.shape
    ff_width = up_weight.shape[1]
    mod_width = ada_weight.shape[1]
    dp_count = lax.axis_size("dp")
    core = lax.axis_index("seq").astype(jnp.int32)
    dp_rank = lax.axis_index("dp").astype(jnp.int32)
    image_count = slot_count // 2
    length = 2 * half_len
    row_count = image_count * length
    half = width // 2
    piece = width // dp_count
    fast = dp_count == 16 and not GENERAL
    cond_blocks = lax.all_to_all(
        jnp.broadcast_to(cond[None], (dp_count,) + cond.shape), "dp", 0, 0, tiled=True
    )
    tokens_far = swap_cores(tokens)
    cot_far = swap_cores(cotangent)
    image_shape = (image_count, length, width)
    packed_rows = 2 * width + ff_width // 2 + half
    vmem = pltpu.VMEM
    (
        images,
        normed,
        penalty,
        hot,
        marks,
        qkv_b_row,
        out_b_row,
        up_b_row,
        down_b_row,
        ada_weight_near,
        ada_b_row,
        cot_images,
        inverse,
    ) = call(
        load_kernel,
        "load",
        (
            (image_shape, LOW),
            ((row_count, width), F32),
            ((8, length), F32),
            ((8, 8 * dp_count), LOW),
            ((8, width), F32),
            ((1, 3 * width), F32),
            ((1, width), F32),
            ((1, ff_width), F32),
            ((1, width), F32),
            (ada_weight.shape, LOW),
            ((1, mod_width), F32),
            (image_shape, LOW),
            ((row_count, LANES), F32),
        ),
        [
            vmem(image_shape, LOW),
            vmem((row_count, LANES), F32),
            pltpu.SMEM(group_ids.shape, jnp.int32),
            pltpu.SMEM(image_counts.shape, jnp.int32),
            vmem(patch_mask.shape, jnp.int32),
            vmem(qv_bias.shape, LOW),
            vmem(out_bias.shape, LOW),
            vmem(up_bias.shape, LOW),
            vmem(down_bias.shape, LOW),
            vmem(ada_bias.shape, LOW),
            pltpu.SemaphoreType.DMA((9 + 4 * image_count,)),
        ],
        12,
        ("hVhaha" + "h" * 7, "VV" + "V" * 9 + "hh"),
        tokens,
        tokens_far,
        cotangent,
        cot_far,
        group_ids,
        image_counts,
        patch_mask,
        qv_bias,
        out_bias,
        up_bias,
        down_bias,
        ada_weight,
        ada_bias,
    )
    (
        output,
        qkv,
        h1,
        grad_att,
        grad_mid,
        image_mod,
        lead,
        qkv_weight_near,
        keep_one,
        send_one,
        small_one,
    ) = call(
        partial(forward_kernel, piece if fast else 0),
        "forward_and_ffn_back",
        (
            (image_shape, LOW),
            ((row_count, 3 * width), LOW),
            ((row_count, width), LOW),
            ((row_count, width), LOW),
            ((row_count, width), F32),
            ((8, mod_width), LOW),
            ((24, 8 * dp_count), LOW),
            (qkv_weight.shape, LOW),
            ((packed_rows, width), F32),
            ((packed_rows + 16 + row_count // 2, width), LOW),
            ((16, width), F32),
        ),
        [
            vmem((8 * dp_count, width), F32),
            vmem((width, 8 * dp_count), F32),
            vmem((row_count, width), LOW),
            vmem((row_count, width), F32),
            vmem((row_count, width), F32),
            vmem((row_count, width), LOW),
            vmem((row_count, width), LOW),
            vmem((row_count, ff_width), LOW),
            vmem((row_count, ff_width), LOW),
            vmem((row_count, LANES), F32),
            vmem(image_shape, LOW),
            vmem(out_weight.shape, LOW),
            vmem(up_weight.shape, LOW),
            vmem(down_weight.shape, LOW),
            pltpu.SemaphoreType.DMA((5,)),
        ],
        30,
        ("V" * 12 + "h" * 5, "V" * 11),
        cond_blocks,
        images,
        normed,
        penalty,
        hot,
        marks,
        qkv_b_row,
        out_b_row,
        up_b_row,
        down_b_row,
        ada_weight_near,
        ada_b_row,
        cot_images,
        qkv_weight,
        out_weight,
        up_weight,
        down_weight,
    )

    def attention_back(after):
        return call(
            backward_kernel,
            "attention_back",
            (
                (image_shape, LOW),
                ((width + half, width), F32),
                ((width // 4 * 3 + half_len, width), LOW),
                ((width // 4 + half + 8 + half_len, width), LOW),
                ((8, width), F32),
            ),
            [
                vmem((row_count, 3 * width), LOW),
                vmem((row_count, LANES), F32),
                pltpu.SemaphoreType.DMA((1,)),
            ],
            24,
            ("VhVVVVVVVa", "VVVVV"),
            normed,
            inverse,
            penalty,
            qkv_weight_near,
            qkv,
            h1,
            grad_att,
            grad_mid,
            image_mod,
            after,
        )

    if not fast:
        grad_tokens, keep_two, send_two, send_other, small_two = attention_back(small_one)
        own_ids = lax.dynamic_slice_in_dim(group_ids, core * image_count, image_count, 0)
        return general_tail(
            core,
            dp_count,
            dp_rank,
            ((keep_one, send_one), (keep_two, send_two, send_other)),
            (small_one, small_two),
            (output, grad_tokens),
            cond_blocks.reshape(-1, width),
            cond,
            own_ids,
            ada_weight,
        )

    recv_one = swap_cores(send_one)
    split_rows = 18 * piece + 8
    own_part, *sent_parts, early = call(
        split_kernel,
        "split_plane",
        (((split_rows, width), F32),)
        + (((split_rows, width), LOW),) * 3
        + (((24, width), F32),),
        [],
        16,
        ("VVV", "VVVVV"),
        keep_one,
        recv_one,
        small_one,
    )
    near_parts = [rank_swap(item, step + 1, 16) for step, item in enumerate(sent_parts)]
    grad_tokens, keep_two, send_two, send_other, small_two = attention_back(sent_parts[2])
    recv_two, recv_other = swap_cores(send_two), swap_cores(send_other)
    split_rows = 6 * piece + 24
    own_qkv, *sent_qkv = call(
        split_qkv_kernel,
        "split_qkv_plane",
        (((split_rows, width), F32),) + (((split_rows, width), LOW),) * 3,
        [vmem((width + half, width), F32)],
        16,
        ("VVVVVaaa", "VVVV"),
        keep_two,
        recv_two,
        recv_other,
        small_two,
        early,
        *near_parts,
    )
    near_qkv = [rank_swap(item, step + 1, 16) for step, item in enumerate(sent_qkv)]
    line_rows = 4 * piece + 8
    kept_rows, rest, rest_ids, *lines = call(
        fold_kernel,
        "fold_plane",
        (((2 * piece, width), F32), ((4 * piece, width), F32), ((8, width), LOW))
        + (((line_rows, width), LOW),) * 3,
        [vmem((16 * piece, width), F32), vmem((4, 8, width), F32)],
        16,
        ("VVVVa", "VVVVVV"),
        own_part,
        *near_parts,
        sent_qkv[2],
    )
    lines = [rank_swap(item, 4 * (step + 1), 16) for step, item in enumerate(lines)]
    line_rows = 2 * piece + 56
    rest_qkv, rest_small, *lines_qkv = call(
        fold_qkv_kernel,
        "fold_qkv_plane",
        (((2 * piece, width), F32), ((56, width), LOW)) + (((line_rows, width), LOW),) * 3,
        [vmem((8 * piece, width), F32), vmem((4, 24, width), F32)],
        16,
        ("VVVVV", "VVVVV"),
        own_qkv,
        *near_qkv,
        kept_rows,
    )
    lines_qkv = [rank_swap(item, 4 * (step + 1), 16) for step, item in enumerate(lines_qkv)]
    output, grad_tokens, up_sum, down_sum, silu_rows, all_ids = call(
        finish_kernel,
        "finish_line",
        (
            (tokens.shape, LOW),
            (tokens.shape, LOW),
            ((piece, ff_width // 2), F32),
            ((4 * piece, half), F32),
            ((piece, 192), LOW),
            ((1, 192), jnp.int32),
        ),
        [vmem((4, 8, LANES), F32), pltpu.SemaphoreType.DMA((4 * image_count,))],
        16,
        ("V" * 11, "hhvvVV"),
        rest,
        rest_ids,
        *lines,
        lead,
        recv_one,
        recv_two,
        recv_other,
        output,
        grad_tokens,
    )
    (
        out_sum,
        qkv_sum,
        ada_sum,
        own_sums,
        send_sums,
        out_bias_sum,
        up_bias_sum,
        down_bias_sum,
        qv_sum,
    ) = call(
        late_kernel,
        "late_groups",
        (
            ((piece, half), F32),
            ((piece, 3 * half), F32),
            ((piece, mod_width // 2), F32),
            ((8, width), F32),
            ((8, width), F32),
            ((width,), F32),
            ((ff_width,), F32),
            ((width,), F32),
            ((2, width), F32),
        ),
        [vmem((4, 48, width), LOW), vmem((4, 8, width), F32)],
        16,
        ("V" * 8, "vvvVVvvvv"),
        rest_qkv,
        rest_small,
        *lines_qkv,
        silu_rows,
        all_ids,
        ada_weight_near,
    )
    grad_cond, ada_bias_sum = call(
        final_kernel,
        "final_groups",
        (((GROUPS_PER_RANK, half), F32), ((mod_width,), F32)),
        [],
        16,
        ("VVv", "vv"),
        own_sums,
        swap_cores(send_sums),
        cond,
    )
    return (
        output,
        grad_tokens,
        grad_cond,
        qkv_sum,
        qv_sum,
        out_sum,
        out_bias_sum,
        up_sum,
        up_bias_sum,
        down_sum,
        down_bias_sum,
        ada_sum,
        ada_bias_sum,
    )


def solution(mesh):
    placed = (
        P("dp", "seq", None),
        P("dp", "seq", None),
        P("dp", None),
        P("dp"),
        P("dp"),
        P("dp", None),
        P(),
        P(),
        P(),
        P(),
        P(),
        P(),
        P(),
        P(),
        P(),
        P(),
    )
    return jax.shard_map(
        body,
        mesh=mesh,
        in_specs=placed,
        out_specs=(
            P("dp", "seq", None),
            P("dp", "seq", None),
            P("dp", "seq"),
            P("dp", "seq"),
            P(),
            P("dp", "seq"),
            P(),
            P("dp", "seq"),
            P(),
            P("dp", "seq"),
            P(),
            P("dp", "seq"),
            P(),
        ),
        check_vma=False,
    )
```

time: 87.2 us -> 75.2 us (0.86)
  waiting for transfers between devices: 30.7 us -> 17.2 us
  starting transfers between devices: 21.2 us -> 25.8 us
  Pallas kernels: 31.5 us -> 27.3 us
  local copies, waits for them, and re-layouts: 1.44 us -> 3.04 us
    ppermute x9 -> x12, waiting for transfers between devices: 17.8 us -> 9.21 us  [rank_swap(): lax.ppermute(values, 'dp', [(rank, rank ^ step) for rank in range(count)])]
    all_to_all x1, waiting for transfers between devices: 7.02 us -> 1.94 us  [body(): lax.all_to_all(jnp.broadcast_to(cond[None], (dp_count,) + cond.shape), 'd...]
    ppermute x9 -> x12, starting transfers between devices: 11.6 us -> 16.3 us  [rank_swap(): lax.ppermute(values, 'dp', [(rank, rank ^ step) for rank in range(count)])]
    pallas_call x8 -> x10, Pallas kernels: 31.5 us -> 27.3 us  [call(): pl.pallas_call(kernel, out_shape=tuple((pinned.get(kind, jax.ShapeDtypeSt...]
    broadcast_in_dim x0 -> x1, local copies, waits for them, and re-layouts: none -> 1.3 us  [body(): jnp.broadcast_to(cond[None], (dp_count,) + cond.shape)]
    unnamed x6, local copies, waits for them, and re-layouts: 0.66 us -> 1.74 us
    ppermute x7 -> x6, waiting for transfers between devices: 5.81 us -> 6.1 us  [swap_cores(): return lax.ppermute(values, 'seq', CORE_SWAP)]
  transfers between devices with their start and end apart: 17 -> 19, of which waited for: 9 -> 7; matrix products, arithmetic and copies ran while one was open for 2% -> 2% of each run, Pallas kernels for 12% -> 17%
where the time goes in v2:
time: 75.2 us; the launch traced here: 74.9 us
  Pallas kernels  27.3 us (36%)
  starting transfers between devices  25.8 us (34%)
  waiting for transfers between devices  17.2 us (23%)
  local copies, waits for them, and re-layouts  3.04 us (4%)
  between operations  1.43 us (2%)
    pallas_call x10, Pallas kernels, call(): pl.pallas_call(kernel, out_shape=tuple((pinned.get(kind, jax.ShapeDtypeSt...  27.3 us
    ppermute x12, starting transfers between devices, rank_swap(): lax.ppermute(values, 'dp', [(rank, rank ^ step) for rank in range(count)])  16.3 us
    ppermute x12, waiting for transfers between devices, rank_swap(): lax.ppermute(values, 'dp', [(rank, rank ^ step) for rank in range(count)])  9.21 us
    all_to_all x1, starting transfers between devices, body(): lax.all_to_all(jnp.broadcast_to(cond[None], (dp_count,) + cond.shape), 'd...  8.29 us
    ppermute x6, waiting for transfers between devices, swap_cores(): return lax.ppermute(values, 'seq', CORE_SWAP)  6.1 us
    all_to_all x1, waiting for transfers between devices, body(): lax.all_to_all(jnp.broadcast_to(cond[None], (dp_count,) + cond.shape), 'd...  1.94 us
    unnamed x6, local copies, waits for them, and re-layouts  1.74 us
  transfers between devices with their start and end apart: 19, of which 7 were waited for; matrix products, arithmetic and copies ran while one was open for 2% of the time, Pallas kernels for 17%

profile of v2, /device:TPU:0, one launch (start us, length us, event | category | flops | bytes accessed | tf_op | source)
XLA Modules:
  0.0 74.9 jit_solution(10145102850533933099)
XLA Ops:
  0.6 0.5 collective-permute-start
  1.2 0.1 collective-permute-start.1
  1.2 1.3 %broadcast_in_dim.2 = bf16[16,2,384]{2,1,0:T(2,128)(2,1)} broadcast(bf16[2,384]{1,0:T(2,128)(2,1)} %own_cond_ref.1), dimensions={1,2} | broadcast | bytes 26112 | tf_op jit(solution)/shard_map/broadcast_in_dim | solution.py:999
  2.5 8.3 %all-to-all-start = ((bf16[16,2,384]{2,1,0:T(2,128)(2,1)}), bf16[16,2,384]{2,1,0:T(2,128)(2,1)S(1)}, u32[]{:S(2)}, u32[]{:S(2)}) async-start(bf16[16,2,384]{2,1,0:T(2,128)(2,1)} %broadcast_in_dim.2), calls=%async_computation | async-start | bytes 49152 | tf_op jit(solution)/shard_map/all_to_all | solution.py:998
  11.5 0.0 collective-permute-done.tokens_far_ref
  11.5 0.0 collective-permute-done.1.cot_far_ref
  11.5 0.0 copy-start
  11.5 0.7 copy-done
  12.3 1.0 %copy-done.1 = bf16[4,128,384]{2,1,0:T(8,128)(2,1)S(1)} copy-done((bf16[4,128,384]{2,1,0:T(8,128)(2,1)S(1)}, bf16[4,128,384]{2,1,0:T(8,128)(2,1)}, u32[]{:S(2)}) %copy-start.1) | copy-done | bytes 393240
  13.3 3.0 %load.1 = (bf16[2,256,384]{2,1,0:T(8,128)(2,1)S(1)}, f32[512,384]{1,0:T(8,128)S(1)}, f32[8,256]{1,0:T(8,128)S(1)}, bf16[8,128]{1,0:T(8,128)(2,1)S(1)}, f32[8,384...) custom-call(bf16[4,128,384]{2,1,0:T(8,128)(2,1)} %tokens_hbm.1, ...), custom_call_target="tpu_custom_call" | custom-call | flops 1 | bytes 1 | tf_op jit(solution)/shard_map/load/pallas_call | solution.py:864
  16.3 1.9 %all-to-all-done.cond_ref = bf16[16,2,384]{2,1,0:T(2,128)(2,1)S(1)} async-done(((bf16[16,2,384]{2,1,0:T(2,128)(2,1)}), bf16[16,2,384]{2,1,0:T(2,128)(2,1)S(1)}, u32[]{:S(2)}, u32[]{:S(2)}) %all-to-all-start) | async-done | bytes 24608 | tf_op jit(solution)/shard_map/all_to_all | solution.py:998
  18.2 12.1 %forward_and_ffn_back.1 = (bf16[2,256,384]{2,1,0:T(8,128)(2,1)S(1)}, bf16[512,1152]{1,0:T(8,128)(2,1)S(1)}, bf16[512,384]{1,0:T(8,128)(2,1)S(1)}, bf16[512,384]{...) custom-call(bf16[16,2,384]{2,1,0:T(2,128)(2,1)S(1)} %all-to-all-done, ...), custom_call_target="tpu_custom_call" | custom-call | flops 1 | bytes 1 | tf_op jit(solution)/shard_map/forward_and_ffn_back/pallas_call | solution.py:864
  30.4 0.1 collective-permute-start.2
  30.4 3.3 %collective-permute-done.2.recv_ref.recv_one_ref = bf16[2000,384]{1,0:T(8,128)(2,1)S(1)} collective-permute-done((bf16[2000,384]{1,0:T(8,128)(2,1)S(1)}, bf16[2000,384]{1,0:T(8,128)(2,1)S(1)}, u32[]{:S(2)}, u32[]{:S(2)}) %collective-permute-start.2) | collective-permute-done | bytes 1536032 | tf_op jit(solution)/shard_map/ppermute | solution.py:834
  33.8 0.3 split_plane.1
  34.1 0.8 %collective-permute-start.3 = (bf16[440,384]{1,0:T(8,128)(2,1)S(1)}, bf16[440,384]{1,0:T(8,128)(2,1)S(1)}, u32[]{:S(2)}, u32[]{:S(2)}) collective-permute-start(bf16[440,384]{1,0:T(8,128)(2,1)S(1)} %get-tuple-element.95), channel_id=1, source_target_pairs={{0,2},{2,0},{4,6},{6,4},{8,10},{10,8},{12,14},{14,12},{16,18},{18,... | collective-permute-start | bytes 1013768 | tf_op jit(solution)/shard_map/ppermute | solution.py:881
  34.8 0.8 %collective-permute-start.4 = (bf16[440,384]{1,0:T(8,128)(2,1)S(1)}, bf16[440,384]{1,0:T(8,128)(2,1)S(1)}, u32[]{:S(2)}, u32[]{:S(2)}) collective-permute-start(bf16[440,384]{1,0:T(8,128)(2,1)S(1)} %get-tuple-element.96), channel_id=1, source_target_pairs={{0,4},{2,6},{4,0},{6,2},{8,12},{10,14},{12,8},{14,10},{16,20},{18,... | collective-permute-start | bytes 1013768 | tf_op jit(solution)/shard_map/ppermute | solution.py:881
  35.6 2.0 %collective-permute-start.5 = (bf16[440,384]{1,0:T(8,128)(2,1)S(1)}, bf16[440,384]{1,0:T(8,128)(2,1)S(1)}, u32[]{:S(2)}, u32[]{:S(2)}) collective-permute-start(bf16[440,384]{1,0:T(8,128)(2,1)S(1)} %get-tuple-element.97.after_ref), channel_id=1, source_target_pairs={{0,6},{2,4},{4,2},{6,0},{8,14},{10,12},{12,10},{14,8},{16,22},{18,... | collective-permute-start | bytes 1013768 | tf_op jit(solution)/shard_map/ppermute | solution.py:881
  37.6 7.1 %attention_back.1 = (bf16[2,256,384]{2,1,0:T(8,128)(2,1)S(1)}, f32[576,384]{1,0:T(8,128)S(1)}, bf16[416,384]{1,0:T(8,128)(2,1)S(1)}, bf16[424,384]{1,0:T(8,128)(2,1)S(1)}, f32[8,384]{1,0:T(8,128)S(1)}) custom-call(f32[512,384]{1,0:T(8,128)S(1)} %get-tuple-element.80.normed_ref, f32[512,128]{1,0:T(8,128)} %get-tuple-element.98.inverse_hbm, ...), custom_call_target="tpu_custom_call" | custom-call | flops 1 | bytes 1 | tf_op jit(solution)/shard_map/attention_back/pallas_call | solution.py:864
  44.7 0.1 collective-permute-start.7
  44.8 0.5 collective-permute-start.6
  45.3 1.6 %collective-permute-done.6.recv_ref.recv_two_ref = bf16[416,384]{1,0:T(8,128)(2,1)S(1)} collective-permute-done((bf16[416,384]{1,0:T(8,128)(2,1)S(1)}, bf16[416,384]{1,0:T(8,128)(2,1)S(1)}, u32[]{:S(2)}, u32[]{:S(2)}) %collective-permute-start.6) | collective-permute-done | bytes 319520 | tf_op jit(solution)/shard_map/ppermute | solution.py:834
  46.9 0.0 collective-permute-done.7.other_ref.recv_other_ref
  46.9 4.9 %collective-permute-done.4.refs_1_.refs_2_ = bf16[440,384]{1,0:T(8,128)(2,1)S(1)} collective-permute-done((bf16[440,384]{1,0:T(8,128)(2,1)S(1)}, bf16[440,384]{1,0:T(8,128)(2,1)S(1)}, u32[]{:S(2)}, u32[]{:S(2)}) %collective-permute-start.4) | collective-permute-done | bytes 337952 | tf_op jit(solution)/shard_map/ppermute | solution.py:881
  51.8 0.0 collective-permute-done.5.refs_2_.refs_3_
  51.8 0.2 split_qkv_plane.1
  52.0 1.4 %collective-permute-start.11 = (bf16[168,384]{1,0:T(8,128)(2,1)S(1)}, bf16[168,384]{1,0:T(8,128)(2,1)S(1)}, u32[]{:S(2)}, u32[]{:S(2)}) collective-permute-start(bf16[168,384]{1,0:T(8,128)(2,1)S(1)} %get-tuple-element.122), channel_id=1, source_target_pairs={{0,2},{2,0},{4,6},{6,4},{8,10},{10,8},{12,14},{14,12},{16,18},{18,... | collective-permute-start | bytes 387080 | tf_op jit(solution)/shard_map/ppermute | solution.py:881
  53.4 0.6 collective-permute-start.12
  54.0 1.6 %collective-permute-start.13 = (bf16[168,384]{1,0:T(8,128)(2,1)S(1)}, bf16[168,384]{1,0:T(8,128)(2,1)S(1)}, u32[]{:S(2)}, u32[]{:S(2)}) collective-permute-start(bf16[168,384]{1,0:T(8,128)(2,1)S(1)} %get-tuple-element.110.refs_4_), channel_id=1, source_target_pairs={{0,6},{2,4},{4,2},{6,0},{8,14},{10,12},{12,10},{14,8},{16,22},{18,... | collective-permute-start | bytes 387080 | tf_op jit(solution)/shard_map/ppermute | solution.py:881
  55.5 0.4 fold_plane.1
  55.9 0.9 %collective-permute-start.8 = (bf16[104,384]{1,0:T(8,128)(2,1)S(1)}, bf16[104,384]{1,0:T(8,128)(2,1)S(1)}, u32[]{:S(2)}, u32[]{:S(2)}) collective-permute-start(bf16[104,384]{1,0:T(8,128)(2,1)S(1)} %get-tuple-element.113), channel_id=1, source_target_pairs={{0,8},{2,10},{4,12},{6,14},{8,0},{10,2},{12,4},{14,6},{16,24},{18,... | collective-permute-start | bytes 239624 | tf_op jit(solution)/shard_map/ppermute | solution.py:881
  56.8 2.4 %collective-permute-start.9 = (bf16[104,384]{1,0:T(8,128)(2,1)S(1)}, bf16[104,384]{1,0:T(8,128)(2,1)S(1)}, u32[]{:S(2)}, u32[]{:S(2)}) collective-permute-start(bf16[104,384]{1,0:T(8,128)(2,1)S(1)} %get-tuple-element.114), channel_id=1, source_target_pairs={{0,16},{2,18},{4,20},{6,22},{8,24},{10,26},{12,28},{14,30},{16,0},... | collective-permute-start | bytes 239624 | tf_op jit(solution)/shard_map/ppermute | solution.py:881
  59.2 1.5 %collective-permute-start.10 = (bf16[104,384]{1,0:T(8,128)(2,1)S(1)}, bf16[104,384]{1,0:T(8,128)(2,1)S(1)}, u32[]{:S(2)}, u32[]{:S(2)}) collective-permute-start(bf16[104,384]{1,0:T(8,128)(2,1)S(1)} %get-tuple-element.115), channel_id=1, source_target_pairs={{0,24},{2,26},{4,28},{6,30},{8,16},{10,18},{12,20},{14,22},{16,8},... | collective-permute-start | bytes 239624 | tf_op jit(solution)/shard_map/ppermute | solution.py:881
  60.7 0.3 fold_qkv_plane.1
  60.9 0.6 collective-permute-start.14
  61.5 2.4 %collective-permute-start.15 = (bf16[104,384]{1,0:T(8,128)(2,1)S(1)}, bf16[104,384]{1,0:T(8,128)(2,1)S(1)}, u32[]{:S(2)}, u32[]{:S(2)}) collective-permute-start(bf16[104,384]{1,0:T(8,128)(2,1)S(1)} %get-tuple-element.128), channel_id=1, source_target_pairs={{0,16},{2,18},{4,20},{6,22},{8,24},{10,26},{12,28},{14,30},{16,0},... | collective-permute-start | bytes 239624 | tf_op jit(solution)/shard_map/ppermute | solution.py:881
  63.9 0.0 collective-permute-done.8.one_ref
  63.9 1.5 %collective-permute-start.16 = (bf16[104,384]{1,0:T(8,128)(2,1)S(1)}, bf16[104,384]{1,0:T(8,128)(2,1)S(1)}, u32[]{:S(2)}, u32[]{:S(2)}) collective-permute-start(bf16[104,384]{1,0:T(8,128)(2,1)S(1)} %get-tuple-element.129), channel_id=1, source_target_pairs={{0,24},{2,26},{4,28},{6,30},{8,16},{10,18},{12,20},{14,22},{16,8},... | collective-permute-start | bytes 239624 | tf_op jit(solution)/shard_map/ppermute | solution.py:881
  65.4 1.1 %collective-permute-done.9.two_ref = bf16[104,384]{1,0:T(8,128)(2,1)S(1)} collective-permute-done((bf16[104,384]{1,0:T(8,128)(2,1)S(1)}, bf16[104,384]{1,0:T(8,128)(2,1)S(1)}, u32[]{:S(2)}, u32[]{:S(2)}) %collective-permute-start.9) | collective-permute-done | bytes 79904 | tf_op jit(solution)/shard_map/ppermute | solution.py:881
  66.4 1.8 %finish_line.1 = (bf16[4,128,384]{2,1,0:T(8,128)(2,1)}, bf16[4,128,384]{2,1,0:T(8,128)(2,1)}, f32[24,768]{1,0:T(8,128)}, f32[96,192]{1,0:T(8,128)}, bf16[24,192]{1,0:T(8,128)(2,1)S(1)}, /*index=5*/s32[1,192]{1,0:T(1,128)S(1)}) custom-call(f32[96,384]{1,0:T(8,128)S(1)} %get-tuple-element.111.own_ref, bf16[8,384]{1,0:T(8,128)(2,1)S(1)} %get-tuple-element.112.own_small_ref, ...), custom_call_target="tpu_custom_call" | custom-call | flops 1 | bytes 1 | tf_op jit(solution)/shard_map/finish_line/pallas_call | solution.py:864
  68.3 0.0 copy-start.2
  68.3 0.0 collective-permute-done.14.one_ref
  68.3 3.2 %collective-permute-done.15.two_ref = bf16[104,384]{1,0:T(8,128)(2,1)S(1)} collective-permute-done((bf16[104,384]{1,0:T(8,128)(2,1)S(1)}, bf16[104,384]{1,0:T(8,128)(2,1)S(1)}, u32[]{:S(2)}, u32[]{:S(2)}) %collective-permute-start.15) | collective-permute-done | bytes 79904 | tf_op jit(solution)/shard_map/ppermute | solution.py:881
  71.5 0.0 collective-permute-done.16.three_ref
  71.5 1.5 %late_groups.1 = (f32[24,192]{1,0:T(8,128)}, f32[24,576]{1,0:T(8,128)}, f32[24,1152]{1,0:T(8,128)}, f32[8,384]{1,0:T(8,128)S(1)}, f32[8,384]{1,0:T(8,128)S(1)}, ...) custom-call(f32[48,384]{1,0:T(8,128)S(1)} %get-tuple-element.125.own_ref, ...), custom_call_target="tpu_custom_call" | custom-call | flops 1 | bytes 1 | tf_op jit(solution)/shard_map/late_groups/pallas_call | solution.py:864
  73.0 0.0 collective-permute-start.17
  73.0 1.2 %collective-permute-done.17.recv_ref = f32[8,384]{1,0:T(8,128)S(1)} collective-permute-done((f32[8,384]{1,0:T(8,128)S(1)}, f32[8,384]{1,0:T(8,128)S(1)}, u32[]{:S(2)}, u32[]{:S(2)}) %collective-permute-start.17) | collective-permute-done | bytes 12320 | tf_op jit(solution)/shard_map/ppermute | solution.py:834
  74.2 0.7 final_groups.1
  (7 shorter events, 0.0 us)
Async XLA Ops:
  0.6 10.8 %collective-permute-start = (bf16[4,128,384]{2,1,0:T(8,128)(2,1)}, bf16[4,128,384]{2,1,0:T(8,128)(2,1)S(1)}, u32[]{:S(2)}, u32[]{:S(2)}) collective-permute-start(bf16[4,128,384]{2,1,0:T(8,128)(2,1)} %tokens_hbm.1), channel_id=1, source_target_pairs={{0,1},{1,0},{2,3},{3,2},{4,5},{5,4},{6,7},{7,6},{8,9},{9,8},{10,11... | collective-permute-start | bytes 1179656 | tf_op jit(solution)/shard_map/ppermute | solution.py:834
  1.2 10.3 %collective-permute-start.1 = (bf16[4,128,384]{2,1,0:T(8,128)(2,1)}, bf16[4,128,384]{2,1,0:T(8,128)(2,1)S(1)}, u32[]{:S(2)}, u32[]{:S(2)}) collective-permute-start(bf16[4,128,384]{2,1,0:T(8,128)(2,1)} %cot_hbm.1), channel_id=1, source_target_pairs={{0,1},{1,0},{2,3},{3,2},{4,5},{5,4},{6,7},{7,6},{8,9},{9,8},{10,11... | collective-permute-start | bytes 1179656 | tf_op jit(solution)/shard_map/ppermute | solution.py:834
  2.5 15.7 %all-to-all-start = ((bf16[16,2,384]{2,1,0:T(2,128)(2,1)}), bf16[16,2,384]{2,1,0:T(2,128)(2,1)S(1)}, u32[]{:S(2)}, u32[]{:S(2)}) async-start(bf16[16,2,384]{2,1,0:T(2,128)(2,1)} %broadcast_in_dim.2), calls=%async_computation | async-start | bytes 49152 | tf_op jit(solution)/shard_map/all_to_all | solution.py:998
  11.5 0.7 copy-start
  12.3 1.0 %copy-start.1 = (bf16[4,128,384]{2,1,0:T(8,128)(2,1)S(1)}, bf16[4,128,384]{2,1,0:T(8,128)(2,1)}, u32[]{:S(2)}) copy-start(bf16[4,128,384]{2,1,0:T(8,128)(2,1)} %copy-done) | copy-start | bytes 1179652
  30.4 3.4 %collective-permute-start.2 = (bf16[2000,384]{1,0:T(8,128)(2,1)S(1)}, bf16[2000,384]{1,0:T(8,128)(2,1)S(1)}, u32[]{:S(2)}, u32[]{:S(2)}) collective-permute-start(bf16[2000,384]{1,0:T(8,128)(2,1)S(1)} %get-tuple-element.92), channel_id=1, source_target_pairs={{0,1},{1,0},{2,3},{3,2},{4,5},{5,4},{6,7},{7,6},{8,9},{9,8},{10,11... | collective-permute-start | bytes 4608008 | tf_op jit(solution)/shard_map/ppermute | solution.py:834
  34.1 12.8 %collective-permute-start.3 = (bf16[440,384]{1,0:T(8,128)(2,1)S(1)}, bf16[440,384]{1,0:T(8,128)(2,1)S(1)}, u32[]{:S(2)}, u32[]{:S(2)}) collective-permute-start(bf16[440,384]{1,0:T(8,128)(2,1)S(1)} %get-tuple-element.95), channel_id=1, source_target_pairs={{0,2},{2,0},{4,6},{6,4},{8,10},{10,8},{12,14},{14,12},{16,18},{18,... | collective-permute-start | bytes 1013768 | tf_op jit(solution)/shard_map/ppermute | solution.py:881
  34.8 16.9 %collective-permute-start.4 = (bf16[440,384]{1,0:T(8,128)(2,1)S(1)}, bf16[440,384]{1,0:T(8,128)(2,1)S(1)}, u32[]{:S(2)}, u32[]{:S(2)}) collective-permute-start(bf16[440,384]{1,0:T(8,128)(2,1)S(1)} %get-tuple-element.96), channel_id=1, source_target_pairs={{0,4},{2,6},{4,0},{6,2},{8,12},{10,14},{12,8},{14,10},{16,20},{18,... | collective-permute-start | bytes 1013768 | tf_op jit(solution)/shard_map/ppermute | solution.py:881
  35.6 16.1 %collective-permute-start.5 = (bf16[440,384]{1,0:T(8,128)(2,1)S(1)}, bf16[440,384]{1,0:T(8,128)(2,1)S(1)}, u32[]{:S(2)}, u32[]{:S(2)}) collective-permute-start(bf16[440,384]{1,0:T(8,128)(2,1)S(1)} %get-tuple-element.97.after_ref), channel_id=1, source_target_pairs={{0,6},{2,4},{4,2},{6,0},{8,14},{10,12},{12,10},{14,8},{16,22},{18,... | collective-permute-start | bytes 1013768 | tf_op jit(solution)/shard_map/ppermute | solution.py:881
  44.7 2.2 %collective-permute-start.7 = (bf16[424,384]{1,0:T(8,128)(2,1)S(1)}, bf16[424,384]{1,0:T(8,128)(2,1)S(1)}, u32[]{:S(2)}, u32[]{:S(2)}) collective-permute-start(bf16[424,384]{1,0:T(8,128)(2,1)S(1)} %get-tuple-element.107), channel_id=1, source_target_pairs={{0,1},{1,0},{2,3},{3,2},{4,5},{5,4},{6,7},{7,6},{8,9},{9,8},{10,11... | collective-permute-start | bytes 976904 | tf_op jit(solution)/shard_map/ppermute | solution.py:834
  44.8 2.1 %collective-permute-start.6 = (bf16[416,384]{1,0:T(8,128)(2,1)S(1)}, bf16[416,384]{1,0:T(8,128)(2,1)S(1)}, u32[]{:S(2)}, u32[]{:S(2)}) collective-permute-start(bf16[416,384]{1,0:T(8,128)(2,1)S(1)} %get-tuple-element.106), channel_id=1, source_target_pairs={{0,1},{1,0},{2,3},{3,2},{4,5},{5,4},{6,7},{7,6},{8,9},{9,8},{10,11... | collective-permute-start | bytes 958472 | tf_op jit(solution)/shard_map/ppermute | solution.py:834
  52.0 7.2 %collective-permute-start.11 = (bf16[168,384]{1,0:T(8,128)(2,1)S(1)}, bf16[168,384]{1,0:T(8,128)(2,1)S(1)}, u32[]{:S(2)}, u32[]{:S(2)}) collective-permute-start(bf16[168,384]{1,0:T(8,128)(2,1)S(1)} %get-tuple-element.122), channel_id=1, source_target_pairs={{0,2},{2,0},{4,6},{6,4},{8,10},{10,8},{12,14},{14,12},{16,18},{18,... | collective-permute-start | bytes 387080 | tf_op jit(solution)/shard_map/ppermute | solution.py:881
  53.4 7.3 %collective-permute-start.12 = (bf16[168,384]{1,0:T(8,128)(2,1)S(1)}, bf16[168,384]{1,0:T(8,128)(2,1)S(1)}, u32[]{:S(2)}, u32[]{:S(2)}) collective-permute-start(bf16[168,384]{1,0:T(8,128)(2,1)S(1)} %get-tuple-element.123), channel_id=1, source_target_pairs={{0,4},{2,6},{4,0},{6,2},{8,12},{10,14},{12,8},{14,10},{16,20},{18,... | collective-permute-start | bytes 387080 | tf_op jit(solution)/shard_map/ppermute | solution.py:881
  54.0 6.7 %collective-permute-start.13 = (bf16[168,384]{1,0:T(8,128)(2,1)S(1)}, bf16[168,384]{1,0:T(8,128)(2,1)S(1)}, u32[]{:S(2)}, u32[]{:S(2)}) collective-permute-start(bf16[168,384]{1,0:T(8,128)(2,1)S(1)} %get-tuple-element.110.refs_4_), channel_id=1, source_target_pairs={{0,6},{2,4},{4,2},{6,0},{8,14},{10,12},{12,10},{14,8},{16,22},{18,... | collective-permute-start | bytes 387080 | tf_op jit(solution)/shard_map/ppermute | solution.py:881
  55.9 8.0 %collective-permute-start.8 = (bf16[104,384]{1,0:T(8,128)(2,1)S(1)}, bf16[104,384]{1,0:T(8,128)(2,1)S(1)}, u32[]{:S(2)}, u32[]{:S(2)}) collective-permute-start(bf16[104,384]{1,0:T(8,128)(2,1)S(1)} %get-tuple-element.113), channel_id=1, source_target_pairs={{0,8},{2,10},{4,12},{6,14},{8,0},{10,2},{12,4},{14,6},{16,24},{18,... | collective-permute-start | bytes 239624 | tf_op jit(solution)/shard_map/ppermute | solution.py:881
  56.8 9.6 %collective-permute-start.9 = (bf16[104,384]{1,0:T(8,128)(2,1)S(1)}, bf16[104,384]{1,0:T(8,128)(2,1)S(1)}, u32[]{:S(2)}, u32[]{:S(2)}) collective-permute-start(bf16[104,384]{1,0:T(8,128)(2,1)S(1)} %get-tuple-element.114), channel_id=1, source_target_pairs={{0,16},{2,18},{4,20},{6,22},{8,24},{10,26},{12,28},{14,30},{16,0},... | collective-permute-start | bytes 239624 | tf_op jit(solution)/shard_map/ppermute | solution.py:881
  59.2 7.3 %collective-permute-start.10 = (bf16[104,384]{1,0:T(8,128)(2,1)S(1)}, bf16[104,384]{1,0:T(8,128)(2,1)S(1)}, u32[]{:S(2)}, u32[]{:S(2)}) collective-permute-start(bf16[104,384]{1,0:T(8,128)(2,1)S(1)} %get-tuple-element.115), channel_id=1, source_target_pairs={{0,24},{2,26},{4,28},{6,30},{8,16},{10,18},{12,20},{14,22},{16,8},... | collective-permute-start | bytes 239624 | tf_op jit(solution)/shard_map/ppermute | solution.py:881
  60.9 7.4 %collective-permute-start.14 = (bf16[104,384]{1,0:T(8,128)(2,1)S(1)}, bf16[104,384]{1,0:T(8,128)(2,1)S(1)}, u32[]{:S(2)}, u32[]{:S(2)}) collective-permute-start(bf16[104,384]{1,0:T(8,128)(2,1)S(1)} %get-tuple-element.127), channel_id=1, source_target_pairs={{0,8},{2,10},{4,12},{6,14},{8,0},{10,2},{12,4},{14,6},{16,24},{18,... | collective-permute-start | bytes 239624 | tf_op jit(solution)/shard_map/ppermute | solution.py:881
  61.5 10.0 %collective-permute-start.15 = (bf16[104,384]{1,0:T(8,128)(2,1)S(1)}, bf16[104,384]{1,0:T(8,128)(2,1)S(1)}, u32[]{:S(2)}, u32[]{:S(2)}) collective-permute-start(bf16[104,384]{1,0:T(8,128)(2,1)S(1)} %get-tuple-element.128), channel_id=1, source_target_pairs={{0,16},{2,18},{4,20},{6,22},{8,24},{10,26},{12,28},{14,30},{16,0},... | collective-permute-start | bytes 239624 | tf_op jit(solution)/shard_map/ppermute | solution.py:881
  63.9 7.6 %collective-permute-start.16 = (bf16[104,384]{1,0:T(8,128)(2,1)S(1)}, bf16[104,384]{1,0:T(8,128)(2,1)S(1)}, u32[]{:S(2)}, u32[]{:S(2)}) collective-permute-start(bf16[104,384]{1,0:T(8,128)(2,1)S(1)} %get-tuple-element.129), channel_id=1, source_target_pairs={{0,24},{2,26},{4,28},{6,30},{8,16},{10,18},{12,20},{14,22},{16,8},... | collective-permute-start | bytes 239624 | tf_op jit(solution)/shard_map/ppermute | solution.py:881
  68.3 5.9 %copy-start.2 = (bf16[2,384]{1,0:T(2,128)(2,1)S(1)}, bf16[2,384]{1,0:T(2,128)(2,1)}, u32[]{:S(2)}) copy-start(bf16[2,384]{1,0:T(2,128)(2,1)} %own_cond_ref.1) | copy-start | bytes 4612
  73.0 1.2 %collective-permute-start.17 = (f32[8,384]{1,0:T(8,128)S(1)}, f32[8,384]{1,0:T(8,128)S(1)}, u32[]{:S(2)}, u32[]{:S(2)}) collective-permute-start(f32[8,384]{1,0:T(8,128)S(1)} %get-tuple-element.133), channel_id=1, source_target_pairs={{0,1},{1,0},{2,3},{3,2},{4,5},{5,4},{6,7},{7,6},{8,9},{9,8},{10,11... | collective-permute-start | bytes 36872 | tf_op jit(solution)/shard_map/ppermute | solution.py:834

commit v3 on v2

--- a/solution.py
+++ b/solution.py
@@ -15,6 +15,7 @@
 LANES = 128
 GROUPS_PER_RANK = 2
 GENERAL = False
+PIECE_ROWS = 288
 F32 = jnp.float32
 LOW = jnp.bfloat16
 
@@ -105,8 +106,6 @@
 def load_kernel(
     tokens_hbm,
     tokens_far_ref,
-    cot_hbm,
-    cot_far_ref,
     ids_hbm,
     counts_hbm,
     mask_hbm,
@@ -117,7 +116,6 @@
     ada_w_hbm,
     ada_b_hbm,
     images_ref,
-    normed_ref,
     penalty_ref,
     hot_ref,
     marks_ref,
@@ -127,10 +125,6 @@
     down_b_ref,
     ada_w_ref,
     ada_b_ref,
-    cot_images_hbm,
-    inverse_hbm,
-    cot_ref,
-    inverse_ref,
     ids_ref,
     counts_ref,
     mask_ref,
@@ -146,8 +140,7 @@
     half_len = length // 2
     first_image = core * image_count
     copies = fetch(
-        own_images(tokens_hbm, tokens_far_ref, images_ref, first_image)
-        + [
+        [
             (ids_hbm, ids_ref),
             (counts_hbm, counts_ref),
             (mask_hbm, mask_ref),
@@ -156,30 +149,28 @@
             (up_b_hbm, up_b_raw),
             (down_b_hbm, down_b_raw),
             (ada_b_hbm, ada_b_raw),
+            (ada_w_hbm, ada_w_ref),
         ]
-        + own_images(cot_hbm, cot_far_ref, cot_ref, first_image)
-        + [(ada_w_hbm, ada_w_ref)],
+        + own_images(tokens_hbm, tokens_far_ref, images_ref, first_image),
         sems,
     )
-    token_copies = 2 * image_count
-    for copy in copies[: token_copies + 8]:
+    for copy in copies[:8]:
         copy.wait()
     row = lax.broadcasted_iota(jnp.int32, hot_ref.shape, 0)
     column = lax.broadcasted_iota(jnp.int32, hot_ref.shape, 1)
+    lane = lax.broadcasted_iota(jnp.int32, marks_ref.shape, 1)
     hot = jnp.zeros(hot_ref.shape, F32)
-    marks_ref[...] = jnp.zeros_like(marks_ref)
+    marks = jnp.zeros(marks_ref.shape, F32)
+    for slot in range(2 * image_count):
+        marks = jnp.where(lane == slot, ids_ref[slot].astype(F32), marks)
+    marks_ref[...] = marks
     penalty_ref[...] = jnp.zeros_like(penalty_ref)
     for image in range(image_count):
         group = ids_ref[first_image + image]
         place = 8 * (group // GROUPS_PER_RANK) + group % GROUPS_PER_RANK
         hot = jnp.where((row == image) & (column == place), 1.0, hot)
-        marks_ref[image : image + 1, :] = jnp.full((1, width), group.astype(F32), F32)
-        marks = own_marks(mask_ref, counts_ref, core, image, image_count, half_len)
-        penalty_ref[image : image + 1, :] = (marks - 1.0) * 30000.0
-        rows = slice(image * length, (image + 1) * length)
-        normed, inverse = normalize(images_ref[image].astype(F32))
-        normed_ref[rows, :] = normed
-        inverse_ref[rows, :] = jnp.broadcast_to(inverse, (length, LANES))
+        own = own_marks(mask_ref, counts_ref, core, image, image_count, half_len)
+        penalty_ref[image : image + 1, :] = (own - 1.0) * 30000.0
     hot_ref[...] = hot.astype(LOW)
     qkv_b_ref[...] = jnp.concatenate(
         [qv_b_ref[0:1, :], jnp.zeros((1, width), LOW), qv_b_ref[1:2, :]], axis=1
@@ -191,9 +182,7 @@
         (ada_b_raw, ada_b_ref),
     ):
         target[...] = as_row(raw)
-    for copy in copies[token_copies + 8 :]:
-        copy.wait()
-    for copy in fetch([(cot_ref, cot_images_hbm), (inverse_ref, inverse_hbm)], sems):
+    for copy in copies[8:]:
         copy.wait()
 
 
@@ -207,20 +196,30 @@
 
     queries = qkv_ref[rows, lanes(0)] * jnp.asarray(HEAD_DIM**-0.5, LOW)
     return rows, lanes, queries, qkv_ref[rows, lanes(1)], qkv_ref[rows, lanes(2)]
+
+
+def image_rows(image, length):
+    return slice(image * length, (image + 1) * length)
+
+
+def mod_part(mod_ref, image, which, width):
+    return mod_ref[image : image + 1, which * width : (which + 1) * width].astype(F32)
+
+
+def wide_column(column_ref, rows, width):
+    return jnp.concatenate([column_ref[rows, :]] * (width // LANES), axis=1)
 
 
 def forward_kernel(
     lead_rows,
     cond_ref,
     images_ref,
-    normed_ref,
+    cot_far_ref,
     penalty_ref,
     hot_ref,
-    marks_ref,
     qkv_b_ref,
     out_b_ref,
     up_b_ref,
-    down_b_ref,
     ada_w_ref,
     ada_b_ref,
     cot_hbm,
@@ -228,31 +227,30 @@
     out_w_hbm,
     up_w_hbm,
     down_w_hbm,
-    output_ref,
     qkv_ref,
     h1_ref,
-    grad_att_ref,
-    grad_mid_ref,
+    normed_ref,
+    inverse_ref,
     mod_ref,
     lead_ref,
+    att_ref,
+    mid_ref,
+    attn_ref,
+    act_ref,
+    gpre_ref,
+    valid_ref,
+    cot_ref,
     qkv_w_ref,
+    out_w_ref,
+    up_w_ref,
+    down_w_ref,
     keep_ref,
     send_ref,
     small_ref,
     cond_rows_ref,
     turned_ref,
-    att_ref,
-    mid_ref,
-    attn_ref,
     h2_ref,
     gffn_ref,
-    act_ref,
-    gpre_ref,
-    valid_ref,
-    cot_ref,
-    out_w_ref,
-    up_w_ref,
-    down_w_ref,
     sems,
 ):
     core = lax.axis_index("seq")
@@ -264,10 +262,10 @@
         [
             (qkv_w_hbm, qkv_w_ref),
             (out_w_hbm, out_w_ref),
-            (cot_hbm, cot_ref),
             (up_w_hbm, up_w_ref),
             (down_w_hbm, down_w_ref),
-        ],
+        ]
+        + own_images(cot_hbm, cot_far_ref, cot_ref, core * image_count),
         sems,
     )
     block_count, block_rows = cond_ref.shape[:2]
@@ -280,21 +278,17 @@
     mod_ref[...] = (nn(image_silu, ada_w_ref[...]) + ada_b_ref[...]).astype(LOW)
 
     def part(image, which):
-        return mod_ref[image : image + 1, which * width : (which + 1) * width].astype(F32)
-
-    def rows_of(image):
-        return slice(image * length, (image + 1) * length)
-
-    def valid_of(image):
-        column = valid_ref[rows_of(image), :]
-        return jnp.concatenate([column] * (width // LANES), axis=1)
+        return mod_part(mod_ref, image, which, width)
 
     copies[0].wait()
     for image in range(image_count):
-        rows = rows_of(image)
+        rows = image_rows(image, length)
+        normed, inverse = normalize(images_ref[image].astype(F32))
+        normed_ref[rows, :] = normed
+        inverse_ref[rows, :] = jnp.broadcast_to(inverse, (length, LANES))
         marks = jnp.where(penalty_ref[image : image + 1, :] < 0.0, 0.0, 1.0)
         valid_ref[rows, :] = jnp.broadcast_to(marks, (LANES, length)).T
-        h1 = (normed_ref[rows, :] * (1.0 + part(image, 1)) + part(image, 0)).astype(LOW)
+        h1 = (normed * (1.0 + part(image, 1)) + part(image, 0)).astype(LOW)
         h1_ref[rows, :] = h1
         qkv_ref[rows, :] = (nn(h1, qkv_w_ref[...]) + qkv_b_ref[...]).astype(LOW)
 
@@ -320,11 +314,10 @@
     else:
         lead_ref[...] = jnp.zeros_like(lead_ref)
     small_ref[...] = jnp.zeros_like(small_ref)
-    small_ref[14:16, :] = marks_ref[:2, :]
     down_bias_grad = jnp.zeros((1, width), F32)
     for image in range(image_count):
-        rows = rows_of(image)
-        valid = valid_of(image)
+        rows = image_rows(image, length)
+        valid = wide_column(valid_ref, rows, width)
         attn = nn(att_ref[rows, :], out_w_ref[...]) + out_b_ref[...]
         attn_ref[rows, :] = attn
         middle = images_ref[image].astype(F32) + valid * part(image, 2) * attn
@@ -342,7 +335,7 @@
         down_w = down_w_ref[columns, :]
         bias = jnp.zeros((1, CHUNK), F32)
         for image in range(image_count):
-            rows = rows_of(image)
+            rows = image_rows(image, length)
             pre = nn(h2_ref[rows, :], up_w) + up_b_ref[:, columns]
             square = pre * pre
             inner = jnp.tanh(pre * (0.7978845608028654 + 0.035677408136300125 * square))
@@ -384,10 +377,42 @@
                 [tn(act_ref[:, low], side), tn(act_ref[:, high], side)], axis=1
             ).astype(target.dtype)
 
+
+def finish_forward_kernel(
+    mod_ref,
+    att_ref,
+    mid_ref,
+    attn_ref,
+    act_ref,
+    gpre_ref,
+    valid_ref,
+    cot_ref,
+    out_w_ref,
+    up_w_ref,
+    down_w_ref,
+    down_b_ref,
+    early_ref,
+    output_ref,
+    grad_att_ref,
+    grad_mid_ref,
+    keep_ref,
+    send_ref,
+    small_ref,
+    gattn_ref,
+):
+    core = lax.axis_index("seq")
+    image_count, length, width = cot_ref.shape
+    half_len = length // 2
+    half = width // 2
+    small_ref[...] = early_ref[...]
+
+    def part(image, which):
+        return mod_part(mod_ref, image, which, width)
+
     out_bias_grad = jnp.zeros((1, width), F32)
     for image in range(image_count):
-        rows = rows_of(image)
-        valid = valid_of(image)
+        rows = image_rows(image, length)
+        valid = wide_column(valid_ref, rows, width)
         upstream = cot_ref[image].astype(F32)
         middle = mid_ref[rows, :]
         ffn = nn(act_ref[rows, :], down_w_ref[...]) + down_b_ref[...]
@@ -401,26 +426,24 @@
         grad_mid_ref[rows, :] = grad_mid
         small_ref[image : image + 1, :] = column_sum(valid * attn_ref[rows, :] * grad_mid)
         grad_attn = (valid * part(image, 2) * grad_mid).astype(LOW)
-        h2_ref[rows, :] = grad_attn
+        gattn_ref[rows, :] = grad_attn
         out_bias_grad = out_bias_grad + column_sum(grad_attn.astype(F32))
         grad_att_ref[rows, :] = nt(grad_attn, out_w_ref[...]).astype(LOW)
     small_ref[8:9, :] = out_bias_grad
-    out_term = tn(att_ref[...], h2_ref[...])
+    out_term = tn(att_ref[...], gattn_ref[...])
     out_first = jnp.concatenate([out_term[:half, :half], out_term[half:, :half]], axis=1)
     out_second = jnp.concatenate([out_term[:half, half:], out_term[half:, half:]], axis=1)
-    rows = slice(2 * width + ff_width // 2, 2 * width + ff_width // 2 + half)
-    keep_ref[rows, :] = jnp.where(core == 0, out_first, out_second)
-    send_ref[rows, :] = jnp.where(core == 0, out_second, out_first).astype(LOW)
-    start = keep_ref.shape[0] + 16
-    send_ref[start - 16 : start, :] = small_ref[...].astype(LOW)
+    keep_ref[...] = jnp.where(core == 0, out_first, out_second)
+    send_ref[:half, :] = jnp.where(core == 0, out_second, out_first).astype(LOW)
+    send_ref[half : half + 16, :] = small_ref[...].astype(LOW)
     for image in range(image_count):
-        rows = slice(start + image * half_len, start + (image + 1) * half_len)
-        send_ref[rows, :] = output_ref[image, half_len:, :]
+        start = half + 16 + image * half_len
+        send_ref[start : start + half_len, :] = output_ref[image, half_len:, :]
 
 
 def backward_kernel(
     normed_ref,
-    inverse_hbm,
+    inverse_ref,
     penalty_ref,
     qkv_w_ref,
     qkv_ref,
@@ -429,17 +452,16 @@
     grad_mid_ref,
     mod_ref,
     after_ref,
+    after_too_ref,
+    after_all_ref,
     grad_tokens_ref,
     keep_ref,
     send_ref,
     other_ref,
     small_ref,
     gqkv_ref,
-    inverse_ref,
-    sems,
 ):
     core = lax.axis_index("seq")
-    copies = fetch([(inverse_hbm, inverse_ref)], sems)
     image_count, length, width = grad_tokens_ref.shape
     half_len = length // 2
     half = width // 2
@@ -472,7 +494,6 @@
         return mod_ref[image : image + 1, which * width : (which + 1) * width].astype(F32)
 
     small_ref[...] = jnp.zeros_like(small_ref)
-    copies[0].wait()
     small_ref[4:5, :] = column_sum(gqkv_ref[:, :width].astype(F32))
     small_ref[5:6, :] = column_sum(gqkv_ref[:, 2 * width :].astype(F32))
     for image in range(image_count):
@@ -492,15 +513,15 @@
     low_unit = jnp.concatenate([term[:half, :half], term[half:, :half]], axis=1)
     high_unit = jnp.concatenate([term[:half, half:], term[half:, half:]], axis=1)
     keep_ref[width:, :] = jnp.where(core == 0, low_unit, high_unit)
-    cut = width // 4 * 3
+    cut = send_ref.shape[0] - half_len
     send_ref[:cut, :] = pair[:cut]
+    send_ref[cut:, :] = grad_tokens_ref[0, half_len:, :]
     start = width - cut
     other_ref[:start, :] = pair[cut:]
     other_ref[start : start + half, :] = jnp.where(core == 0, high_unit, low_unit).astype(LOW)
     start += half
     other_ref[start : start + 8, :] = small_ref[...].astype(LOW)
-    for index, (target, start) in enumerate(((send_ref, cut), (other_ref, start + 8))):
-        target[start:, :] = grad_tokens_ref[index, half_len:, :]
+    other_ref[start + 8 :, :] = grad_tokens_ref[1, half_len:, :]
 
 
 def by_core(core, near, far):
@@ -508,80 +529,100 @@
 
 
 def split_kernel(
-    keep_ref, recv_ref, small_ref, own_ref, one_ref, two_ref, three_ref, early_ref
+    keep_ref, recv_ref, marks_ref, own_up_ref, own_down_ref, send_up_ref, send_down_ref
+):
+    width = keep_ref.shape[1]
+    piece = width // 16
+    long = 4 * piece
+    block = 8 * piece
+    plane = lax.axis_index("dp") & 3
+
+    def move(target, start, size, to):
+        rows = pl.ds(pl.multiple_of(start, 8), size)
+        target[to : to + size, :] = (keep_ref[rows, :] + recv_ref[rows, :].astype(F32)).astype(
+            target.dtype
+        )
+
+    for target, steps in ((own_up_ref, (0, 2)), (send_up_ref, (1, 3))):
+        for index, step in enumerate(steps):
+            who = plane ^ step
+            for z in range(4):
+                for side in range(2):
+                    start = side * width + piece * (4 * z + who)
+                    move(target, start, piece, index * block + (2 * z + side) * piece)
+    for target, steps in ((own_down_ref, (0, 1)), (send_down_ref, (2, 3))):
+        for index, step in enumerate(steps):
+            who = plane ^ step
+            for z in range(2):
+                start = 2 * width + long * (4 * z + who)
+                move(target, start, long, index * block + z * long)
+    send_up_ref[2 * block :, :] = marks_ref[...].astype(LOW)
+
+
+def cross_kernel(
+    own_up_ref,
+    own_down_ref,
+    recv_up_ref,
+    recv_down_ref,
+    marks_ref,
+    after_ref,
+    kept_ref,
+    send_up_ref,
+    send_down_ref,
+):
+    block = own_up_ref.shape[0] // 2
+    first, second = slice(0, block), slice(block, 2 * block)
+    kept_ref[first, :] = own_up_ref[first, :] + recv_up_ref[first, :].astype(F32)
+    kept_ref[second, :] = own_down_ref[first, :] + recv_down_ref[first, :].astype(F32)
+    kept_ref[2 * block : 2 * block + 8, :] = marks_ref[...].astype(LOW).astype(F32)
+    kept_ref[2 * block + 8 :, :] = recv_up_ref[2 * block :, :].astype(F32)
+    send_up_ref[first, :] = (own_up_ref[second, :] + recv_up_ref[second, :].astype(F32)).astype(LOW)
+    send_up_ref[block : block + 8, :] = marks_ref[...].astype(LOW)
+    send_up_ref[block + 8 :, :] = recv_up_ref[2 * block :, :]
+    send_down_ref[...] = (own_down_ref[second, :] + recv_down_ref[second, :].astype(F32)).astype(LOW)
+
+
+def split_qkv_kernel(
+    keep_ref, recv_ref, other_ref, small_ref, keep_out_ref, recv_out_ref, early_ref, *refs
 ):
     core = lax.axis_index("seq")
     width = keep_ref.shape[1]
     piece = width // 16
-    long = 4 * piece
-    start = keep_ref.shape[0]
+    half = width // 2
+    cut = PIECE_ROWS
+    start = keep_ref.shape[0] - cut
     near = small_ref[...].astype(LOW).astype(F32)
-    far = recv_ref[start : start + 16, :].astype(F32)
+    far = other_ref[start : start + 8, :].astype(F32)
     first, second = by_core(core, near, far)
-    mods = []
-    for row in range(0, 6, 2):
-        low_kind = [first[:2], second[:2]] if row == 0 else [jnp.zeros((4, width), F32)]
-        high_kind = [first[row + 2 : row + 4], second[row + 2 : row + 4]]
-        mods.append(
+    near_early = early_ref[...].astype(LOW).astype(F32)
+    far_early = recv_out_ref[half : half + 16, :].astype(F32)
+    early, early_too = by_core(core, near_early, far_early)
+    rows = []
+    for kind in range(3):
+        low_rows = [first, second] if kind < 2 else [early, early_too]
+        low_start = 2 * kind if kind < 2 else 0
+        low_rows = [block[low_start : low_start + 2] for block in low_rows]
+        high_rows = [block[2 * kind + 2 : 2 * kind + 4] for block in (early, early_too)]
+        rows.append(
             jnp.where(
-                core == 0, jnp.concatenate(low_kind, axis=0), jnp.concatenate(high_kind, axis=0)
+                core == 0, jnp.concatenate(low_rows, axis=0), jnp.concatenate(high_rows, axis=0)
             )
         )
-    early_ref[...] = jnp.concatenate(
-        mods + [first[8:14] + second[8:14], jnp.zeros((6, width), F32)], axis=0
-    )
-    lane = lax.broadcasted_iota(jnp.int32, (8, width), 1)
-    ids = jnp.zeros((8, width), F32)
-    for slot, block in enumerate((first[14:15], first[15:16], second[14:15], second[15:16])):
-        ids = jnp.where(lane == slot, block, ids)
-    for step, target in enumerate((own_ref, one_ref, two_ref, three_ref)):
-        who = (lax.axis_index("dp") & 3) ^ step
-
-        def move(start, size, to):
-            rows = pl.ds(pl.multiple_of(start, 8), size)
-            target[to : to + size, :] = (
-                keep_ref[rows, :] + recv_ref[rows, :].astype(F32)
-            ).astype(target.dtype)
-
-        for z in range(4):
-            for side in range(2):
-                move(side * width + piece * (4 * z + who), piece, (2 * z + side) * piece)
-        for z in range(2):
-            move(2 * width + long * (4 * z + who), long, 8 * piece + z * long)
-            move(2 * width + 8 * long + piece * (4 * z + who), piece, 16 * piece + z * piece)
-        target[18 * piece :, :] = ids.astype(target.dtype)
-
-
-def split_qkv_kernel(keep_ref, recv_ref, other_ref, small_ref, early_ref, *refs):
-    core = lax.axis_index("seq")
-    width = keep_ref.shape[1]
-    piece = width // 16
-    cut = width // 4 * 3
-    near = small_ref[...].astype(LOW).astype(F32)
-    start = keep_ref.shape[0] - cut
-    far = other_ref[start : start + 8, :].astype(F32)
-    first, second = by_core(core, near, far)
-    early = early_ref[...]
-    late = jnp.concatenate([first[0:2], second[0:2], first[2:4], second[2:4], early[:4]], axis=0)
-    small = jnp.concatenate(
-        [
-            jnp.where(core == 0, late, early[:12]),
-            early[12:18],
-            first[4:6] + second[4:6],
-            jnp.zeros((4, width), F32),
-        ],
-        axis=0,
-    ).astype(LOW)
+    rows += [early[8:14] + early_too[8:14], first[4:6] + second[4:6], jnp.zeros((4, width), F32)]
+    small = jnp.concatenate(rows, axis=0).astype(LOW)
     total_ref = refs[-1]
     total_ref[:cut, :] = keep_ref[:cut, :] + recv_ref[:cut, :].astype(F32)
-    total_ref[cut:, :] = keep_ref[cut:, :] + other_ref[:start, :].astype(F32)
+    total_ref[cut : width + half, :] = keep_ref[cut:, :] + other_ref[:start, :].astype(F32)
+    total_ref[width + half :, :] = keep_out_ref[...] + recv_out_ref[:half, :].astype(F32)
     for step, target in enumerate(refs[-5:-1]):
         who = (lax.axis_index("dp") & 3) ^ step
-        for z in range(6):
-            start = width + piece * (4 * (z - 4) + who) if z >= 4 else piece * (4 * z + who)
-            rows = pl.ds(pl.multiple_of(start, 8), piece)
+        for z in range(8):
+            begin = piece * (4 * z + who)
+            if z >= 4:
+                begin = width + (z - 4) // 2 * half + piece * (4 * (z % 2) + who)
+            rows = pl.ds(pl.multiple_of(begin, 8), piece)
             target[piece * z : piece * (z + 1), :] = total_ref[rows, :].astype(target.dtype)
-        target[6 * piece :, :] = small.astype(target.dtype)
+        target[8 * piece :, :] = small.astype(target.dtype)
 
 
 def summed(sources, rows):
@@ -589,18 +630,23 @@
 
 
 def fold_kernel(*refs):
-    parts, after = refs[:4], refs[4]
-    kept_ref, rest_ref, rest_small_ref = refs[5:8]
-    sends = refs[8:11]
-    total_ref, group_ref = refs[11:]
+    kept_ref, up_ref, down_ref = refs[:3]
+    rest_ref, rest_small_ref = refs[4:6]
+    sends = refs[6:9]
+    total_ref, group_ref = refs[9:]
     width = total_ref.shape[1]
     piece = width // 16
     long = 4 * piece
     half = width // 2
-    total_ref[...] = summed(parts, slice(0, 16 * piece))
-    for step, part in enumerate(parts):
-        group_ref[(lax.axis_index("dp") & 3) ^ step] = part[18 * piece :, :].astype(F32)
-    kept_ref[...] = summed(parts, slice(16 * piece, 18 * piece))
+    block = 8 * piece
+    total_ref[:block, :] = kept_ref[:block, :] + up_ref[:block, :].astype(F32)
+    total_ref[block:, :] = kept_ref[block : 2 * block, :] + down_ref[...].astype(F32)
+    plane = lax.axis_index("dp") & 3
+    for index in range(2):
+        start = 2 * block + 8 * index
+        group_ref[plane ^ index] = kept_ref[start : start + 8, :]
+        start = block + 8 * index
+        group_ref[plane ^ (2 + index)] = up_ref[start : start + 8, :].astype(F32)
     ids = [group_ref[q, 0:1] for q in range(4)] + [jnp.zeros((4, width), F32)]
     small = jnp.concatenate(ids, axis=0).astype(LOW)
     rest_small_ref[...] = small
@@ -618,17 +664,16 @@
 
 
 def fold_qkv_kernel(*refs):
-    parts, kept_ref = refs[:4], refs[4]
-    rest_ref, rest_small_ref = refs[5:7]
-    sends = refs[7:10]
-    total_ref, late_ref = refs[10:]
+    parts = refs[:4]
+    rest_ref, rest_small_ref = refs[4:6]
+    sends = refs[6:9]
+    total_ref, late_ref = refs[9:]
     width = total_ref.shape[1]
     piece = width // 16
     half = width // 2
-    total_ref[: 6 * piece, :] = summed(parts, slice(0, 6 * piece))
-    total_ref[6 * piece :, :] = kept_ref[...]
+    total_ref[...] = summed(parts, slice(0, 8 * piece))
     for step, part in enumerate(parts):
-        late_ref[(lax.axis_index("dp") & 3) ^ step] = part[6 * piece :, :].astype(F32)
+        late_ref[(lax.axis_index("dp") & 3) ^ step] = part[8 * piece :, :].astype(F32)
     rows = [late_ref[q, :12] for q in range(4)]
     rows.append(late_ref[0, 12:20] + late_ref[1, 12:20] + late_ref[2, 12:20] + late_ref[3, 12:20])
     small = jnp.concatenate(rows, axis=0).astype(LOW)
@@ -680,7 +725,7 @@
     two_ref,
     three_ref,
     lead_ref,
-    recv_one_ref,
+    recv_out_ref,
     recv_two_ref,
     recv_other_ref,
     output_ref,
@@ -701,10 +746,11 @@
     slots, half_len = output_to.shape[:2]
     count = slots // 2
     pairs = []
-    for index, source in enumerate((recv_two_ref, recv_other_ref)):
+    for index in range(count):
         slot = (1 - core) * count + index
-        start = recv_one_ref.shape[0] - (count - index) * half_len
-        pairs.append((recv_one_ref.at[pl.ds(start, half_len)], output_to.at[slot]))
+        start = recv_out_ref.shape[0] - (count - index) * half_len
+        pairs.append((recv_out_ref.at[pl.ds(start, half_len)], output_to.at[slot]))
+        source = (recv_two_ref, recv_other_ref)[index]
         start = source.shape[0] - half_len
         pairs.append((source.at[pl.ds(start, half_len)], grad_tokens_to.at[slot]))
         slot = core * count + index
@@ -736,7 +782,6 @@
 
 
 def late_kernel(
-    own_ref,
     own_small_ref,
     one_ref,
     two_ref,
@@ -744,8 +789,6 @@
     silu_ref,
     ids_ref,
     ada_ref,
-    out_ref,
-    qkv_ref,
     ada_out_ref,
     own_sums_ref,
     send_ref,
@@ -757,12 +800,13 @@
     bias_ref,
 ):
     core = lax.axis_index("seq")
-    width = own_ref.shape[1]
+    width = own_small_ref.shape[1]
     piece = width // 16
     half = width // 2
-    parts = (own_ref, one_ref, two_ref, three_ref)
     line = lax.axis_index("dp") >> 2
-    smalls = (own_small_ref[...],) + tuple(part[2 * piece :, :] for part in parts[1:])
+    smalls = (own_small_ref[...],) + tuple(
+        part[2 * piece :, :] for part in (one_ref, two_ref, three_ref)
+    )
     for step, small in enumerate(smalls):
         stack_ref[line ^ step] = small[:48]
         bias_ref[line ^ step] = small[48:].astype(F32)
@@ -802,7 +846,14 @@
     )
     down_bias_ref[...] = bias[5:6].reshape(width)
     qv_ref[...] = bias[6:8]
-    total = summed(parts, slice(0, 2 * piece))
+
+
+def rest_kernel(own_ref, one_ref, two_ref, three_ref, after_ref, out_ref, qkv_ref):
+    core = lax.axis_index("seq")
+    width = own_ref.shape[1]
+    piece = width // 16
+    half = width // 2
+    total = summed((own_ref, one_ref, two_ref, three_ref), slice(0, 2 * piece))
     out_ref[...] = total[:piece, :half]
     unit, pair = total[:piece, half:], total[piece:]
     qkv_ref[...] = jnp.where(
@@ -892,18 +943,23 @@
     highest = lax.Precision.HIGHEST
     width, mod_width = ada_weight.shape
     half = width // 2
-    (keep_one, send_one), (keep_two, send_two, send_other) = sides
+    (keep_one, send_one), (keep_out, send_out), (keep_two, send_two, send_other) = sides
     output, grad_tokens = heads
     small_one, small_two = smalls
     half_len = output.shape[1] // 2
-    recv_one = swap_cores(send_one)
-    first_sum = keep_one + recv_one[: keep_one.shape[0]].astype(F32)
+    recv_out = swap_cores(send_out)
+    first_sum = jnp.concatenate(
+        [
+            keep_one + swap_cores(send_one).astype(F32),
+            keep_out + recv_out[:half].astype(F32),
+        ],
+        axis=0,
+    )
     recv_two, recv_other = swap_cores(send_two), swap_cores(send_other)
-    cut = width // 4 * 3
     second_sum = keep_two + jnp.concatenate(
-        [recv_two[:cut], recv_other[: keep_two.shape[0] - cut]], axis=0
+        [recv_two[:PIECE_ROWS], recv_other[: keep_two.shape[0] - PIECE_ROWS]], axis=0
     ).astype(F32)
-    output_far = recv_one[keep_one.shape[0] + 16 :].reshape(-1, half_len, width)
+    output_far = recv_out[half + 16 :].reshape(-1, half_len, width)
     grad_far = jnp.stack([item[-half_len:] for item in (recv_two, recv_other)])
     ff_half = first_sum.shape[0] - 2 * width - half
     up = jnp.concatenate([first_sum[:width], first_sum[width : 2 * width]], axis=1)
@@ -1001,11 +1057,10 @@
     tokens_far = swap_cores(tokens)
     cot_far = swap_cores(cotangent)
     image_shape = (image_count, length, width)
-    packed_rows = 2 * width + ff_width // 2 + half
+    half_shape = (image_count, half_len, width)
     vmem = pltpu.VMEM
     (
         images,
-        normed,
         penalty,
         hot,
         marks,
@@ -1015,14 +1070,11 @@
         down_b_row,
         ada_weight_near,
         ada_b_row,
-        cot_images,
-        inverse,
     ) = call(
         load_kernel,
         "load",
         (
             (image_shape, LOW),
-            ((row_count, width), F32),
             ((8, length), F32),
             ((8, 8 * dp_count), LOW),
             ((8, width), F32),
@@ -1032,12 +1084,8 @@
             ((1, width), F32),
             (ada_weight.shape, LOW),
             ((1, mod_width), F32),
-            (image_shape, LOW),
-            ((row_count, LANES), F32),
         ),
         [
-            vmem(image_shape, LOW),
-            vmem((row_count, LANES), F32),
             pltpu.SMEM(group_ids.shape, jnp.int32),
             pltpu.SMEM(image_counts.shape, jnp.int32),
             vmem(patch_mask.shape, jnp.int32),
@@ -1046,14 +1094,12 @@
             vmem(up_bias.shape, LOW),
             vmem(down_bias.shape, LOW),
             vmem(ada_bias.shape, LOW),
-            pltpu.SemaphoreType.DMA((9 + 4 * image_count,)),
+            pltpu.SemaphoreType.DMA((9 + 2 * image_count,)),
         ],
         12,
-        ("hVhaha" + "h" * 7, "VV" + "V" * 9 + "hh"),
+        ("hVha" + "h" * 7, "V" * 10),
         tokens,
         tokens_far,
-        cotangent,
-        cot_far,
         group_ids,
         image_counts,
         patch_mask,
@@ -1065,89 +1111,119 @@
         ada_bias,
     )
     (
-        output,
         qkv,
         h1,
-        grad_att,
-        grad_mid,
+        normed,
+        inverse,
         image_mod,
         lead,
+        att,
+        middle,
+        attn,
+        act,
+        grad_pre,
+        valid,
+        cot_images,
         qkv_weight_near,
+        out_weight_near,
+        up_weight_near,
+        down_weight_near,
         keep_one,
         send_one,
-        small_one,
+        small_early,
     ) = call(
         partial(forward_kernel, piece if fast else 0),
-        "forward_and_ffn_back",
+        "forward_and_ffn_grads",
         (
-            (image_shape, LOW),
             ((row_count, 3 * width), LOW),
             ((row_count, width), LOW),
+            ((row_count, width), F32),
+            ((row_count, LANES), F32),
+            ((8, mod_width), LOW),
+            ((24, 8 * dp_count), LOW),
             ((row_count, width), LOW),
             ((row_count, width), F32),
-            ((8, mod_width), LOW),
-            ((24, 8 * dp_count), LOW),
+            ((row_count, width), F32),
+            ((row_count, ff_width), LOW),
+            ((row_count, ff_width), LOW),
+            ((row_count, LANES), F32),
+            (image_shape, LOW),
             (qkv_weight.shape, LOW),
-            ((packed_rows, width), F32),
-            ((packed_rows + 16 + row_count // 2, width), LOW),
+            (out_weight.shape, LOW),
+            (up_weight.shape, LOW),
+            (down_weight.shape, LOW),
+            ((2 * width + ff_width // 2, width), F32),
+            ((2 * width + ff_width // 2, width), LOW),
             ((16, width), F32),
         ),
         [
             vmem((8 * dp_count, width), F32),
             vmem((width, 8 * dp_count), F32),
             vmem((row_count, width), LOW),
-            vmem((row_count, width), F32),
-            vmem((row_count, width), F32),
             vmem((row_count, width), LOW),
-            vmem((row_count, width), LOW),
-            vmem((row_count, ff_width), LOW),
-            vmem((row_count, ff_width), LOW),
-            vmem((row_count, LANES), F32),
-            vmem(image_shape, LOW),
-            vmem(out_weight.shape, LOW),
-            vmem(up_weight.shape, LOW),
-            vmem(down_weight.shape, LOW),
-            pltpu.SemaphoreType.DMA((5,)),
+            pltpu.SemaphoreType.DMA((4 + 2 * image_count,)),
         ],
-        30,
-        ("V" * 12 + "h" * 5, "V" * 11),
+        24,
+        ("V" * 10 + "h" * 5, "V" * 20),
         cond_blocks,
         images,
-        normed,
+        cot_far,
         penalty,
         hot,
-        marks,
         qkv_b_row,
         out_b_row,
         up_b_row,
-        down_b_row,
         ada_weight_near,
         ada_b_row,
-        cot_images,
+        cotangent,
         qkv_weight,
         out_weight,
         up_weight,
         down_weight,
     )
-
-    def attention_back(after):
+    output, grad_att, grad_mid, keep_out, send_out, small_one = call(
+        finish_forward_kernel,
+        "norm_back",
+        (
+            (image_shape, LOW),
+            ((row_count, width), LOW),
+            ((row_count, width), F32),
+            ((half, width), F32),
+            ((half + 16 + row_count // 2, width), LOW),
+            ((16, width), F32),
+        ),
+        [vmem((row_count, width), LOW)],
+        16,
+        ("V" * 13, "V" * 6),
+        image_mod,
+        att,
+        middle,
+        attn,
+        act,
+        grad_pre,
+        valid,
+        cot_images,
+        out_weight_near,
+        up_weight_near,
+        down_weight_near,
+        down_b_row,
+        small_early,
+    )
+
+    def attention_back(*after):
         return call(
             backward_kernel,
             "attention_back",
             (
                 (image_shape, LOW),
                 ((width + half, width), F32),
-                ((width // 4 * 3 + half_len, width), LOW),
-                ((width // 4 + half + 8 + half_len, width), LOW),
+                ((PIECE_ROWS + half_len, width), LOW),
+                ((width + half + 8 - PIECE_ROWS + half_len, width), LOW),
                 ((8, width), F32),
             ),
-            [
-                vmem((row_count, 3 * width), LOW),
-                vmem((row_count, LANES), F32),
-                pltpu.SemaphoreType.DMA((1,)),
-            ],
+            [vmem((row_count, 3 * width), LOW)],
             24,
-            ("VhVVVVVVVa", "VVVVV"),
+            ("V" * 9 + "aaa", "VVVVV"),
             normed,
             inverse,
             penalty,
@@ -1157,17 +1233,19 @@
             grad_att,
             grad_mid,
             image_mod,
-            after,
+            *after,
         )
 
     if not fast:
-        grad_tokens, keep_two, send_two, send_other, small_two = attention_back(small_one)
+        grad_tokens, keep_two, send_two, send_other, small_two = attention_back(
+            small_one, keep_one, keep_out
+        )
         own_ids = lax.dynamic_slice_in_dim(group_ids, core * image_count, image_count, 0)
         return general_tail(
             core,
             dp_count,
             dp_rank,
-            ((keep_one, send_one), (keep_two, send_two, send_other)),
+            ((keep_one, send_one), (keep_out, send_out), (keep_two, send_two, send_other)),
             (small_one, small_two),
             (output, grad_tokens),
             cond_blocks.reshape(-1, width),
@@ -1177,50 +1255,77 @@
         )
 
     recv_one = swap_cores(send_one)
-    split_rows = 18 * piece + 8
-    own_part, *sent_parts, early = call(
+    recv_out = swap_cores(send_out)
+    block_rows = 8 * piece
+    own_up, own_down, sent_up, sent_down = call(
         split_kernel,
         "split_plane",
-        (((split_rows, width), F32),)
-        + (((split_rows, width), LOW),) * 3
-        + (((24, width), F32),),
+        (
+            ((2 * block_rows, width), F32),
+            ((2 * block_rows, width), F32),
+            ((2 * block_rows + 8, width), LOW),
+            ((2 * block_rows, width), LOW),
+        ),
         [],
         16,
-        ("VVV", "VVVVV"),
+        ("VVV", "VVVV"),
         keep_one,
         recv_one,
-        small_one,
-    )
-    near_parts = [rank_swap(item, step + 1, 16) for step, item in enumerate(sent_parts)]
-    grad_tokens, keep_two, send_two, send_other, small_two = attention_back(sent_parts[2])
+        marks,
+    )
+    near_up, near_down = rank_swap(sent_up, 1, 16), rank_swap(sent_down, 2, 16)
+    grad_tokens, keep_two, send_two, send_other, small_two = attention_back(
+        sent_up, sent_down, recv_out
+    )
+    kept, cross_up, cross_down = call(
+        cross_kernel,
+        "cross_plane",
+        (
+            ((2 * block_rows + 16, width), F32),
+            ((block_rows + 16, width), LOW),
+            ((block_rows, width), LOW),
+        ),
+        [],
+        16,
+        ("VVVVVa", "VVV"),
+        own_up,
+        own_down,
+        near_up,
+        near_down,
+        marks,
+        small_two,
+    )
+    near_up, near_down = rank_swap(cross_up, 2, 16), rank_swap(cross_down, 1, 16)
     recv_two, recv_other = swap_cores(send_two), swap_cores(send_other)
-    split_rows = 6 * piece + 24
+    split_rows = 8 * piece + 24
     own_qkv, *sent_qkv = call(
         split_qkv_kernel,
         "split_qkv_plane",
         (((split_rows, width), F32),) + (((split_rows, width), LOW),) * 3,
-        [vmem((width + half, width), F32)],
+        [vmem((2 * width, width), F32)],
         16,
-        ("VVVVVaaa", "VVVV"),
+        ("VVVVVVVa", "VVVV"),
         keep_two,
         recv_two,
         recv_other,
         small_two,
-        early,
-        *near_parts,
+        keep_out,
+        recv_out,
+        small_one,
+        cross_up,
     )
     near_qkv = [rank_swap(item, step + 1, 16) for step, item in enumerate(sent_qkv)]
     line_rows = 4 * piece + 8
-    kept_rows, rest, rest_ids, *lines = call(
+    rest, rest_ids, *lines = call(
         fold_kernel,
         "fold_plane",
-        (((2 * piece, width), F32), ((4 * piece, width), F32), ((8, width), LOW))
-        + (((line_rows, width), LOW),) * 3,
+        (((4 * piece, width), F32), ((8, width), LOW)) + (((line_rows, width), LOW),) * 3,
         [vmem((16 * piece, width), F32), vmem((4, 8, width), F32)],
         16,
-        ("VVVVa", "VVVVVV"),
-        own_part,
-        *near_parts,
+        ("VVVa", "VVVVV"),
+        kept,
+        near_up,
+        near_down,
         sent_qkv[2],
     )
     lines = [rank_swap(item, 4 * (step + 1), 16) for step, item in enumerate(lines)]
@@ -1231,10 +1336,9 @@
         (((2 * piece, width), F32), ((56, width), LOW)) + (((line_rows, width), LOW),) * 3,
         [vmem((8 * piece, width), F32), vmem((4, 24, width), F32)],
         16,
-        ("VVVVV", "VVVVV"),
+        ("VVVV", "VVVVV"),
         own_qkv,
         *near_qkv,
-        kept_rows,
     )
     lines_qkv = [rank_swap(item, 4 * (step + 1), 16) for step, item in enumerate(lines_qkv)]
     output, grad_tokens, up_sum, down_sum, silu_rows, all_ids = call(
@@ -1255,15 +1359,13 @@
         rest_ids,
         *lines,
         lead,
-        recv_one,
+        recv_out,
         recv_two,
         recv_other,
         output,
         grad_tokens,
     )
     (
-        out_sum,
-        qkv_sum,
         ada_sum,
         own_sums,
         send_sums,
@@ -1275,8 +1377,6 @@
         late_kernel,
         "late_groups",
         (
-            ((piece, half), F32),
-            ((piece, 3 * half), F32),
             ((piece, mod_width // 2), F32),
             ((8, width), F32),
             ((8, width), F32),
@@ -1287,13 +1387,23 @@
         ),
         [vmem((4, 48, width), LOW), vmem((4, 8, width), F32)],
         16,
-        ("V" * 8, "vvvVVvvvv"),
-        rest_qkv,
+        ("V" * 7, "vVVvvvv"),
         rest_small,
         *lines_qkv,
         silu_rows,
         all_ids,
         ada_weight_near,
+    )
+    out_sum, qkv_sum = call(
+        rest_kernel,
+        "rest_sums",
+        (((piece, half), F32), ((piece, 3 * half), F32)),
+        [],
+        16,
+        ("VVVVa", "vv"),
+        rest_qkv,
+        *lines_qkv,
+        send_sums,
     )
     grad_cond, ada_bias_sum = call(
         final_kernel,

time: 75.2 us -> 67.7 us (0.900)
  waiting for transfers between devices: 17.2 us -> 13.9 us
  starting transfers between devices: 25.8 us -> 24 us
  local copies, waits for them, and re-layouts: 3.04 us -> 1.31 us
    ppermute x6 -> x7, waiting for transfers between devices: 6.1 us -> 0.47 us  [swap_cores(): return lax.ppermute(values, 'seq', CORE_SWAP)]
    all_to_all x1, waiting for transfers between devices: 1.94 us -> 5 us  [body(): lax.all_to_all(jnp.broadcast_to(cond[None], (dp_count,) + cond.shape), 'd...]
    ppermute x12 -> x13, starting transfers between devices: 16.3 us -> 13.9 us  [rank_swap(): lax.ppermute(values, 'dp', [(rank, rank ^ step) for rank in range(count)])]
    unnamed x6 -> x2, local copies, waits for them, and re-layouts: 1.74 us -> 0.01 us
    ppermute x12 -> x13, waiting for transfers between devices: 9.21 us -> 8.4 us  [rank_swap(): lax.ppermute(values, 'dp', [(rank, rank ^ step) for rank in range(count)])]
    ppermute x6 -> x7, starting transfers between devices: 1.24 us -> 1.8 us  [swap_cores(): return lax.ppermute(values, 'seq', CORE_SWAP)]
    pallas_call x10 -> x13, Pallas kernels: 27.3 us -> 26.9 us  [call(): pl.pallas_call(kernel, out_shape=tuple((pinned.get(kind, jax.ShapeDtypeSt...]
  transfers between devices with their start and end apart: 19 -> 21, of which waited for: 7 -> 8; matrix products, arithmetic and copies ran while one was open for 2% -> 2% of each run, Pallas kernels for 17% -> 22%
where the time goes in v3:
time: 67.7 us; the launch traced here: 67.5 us
  Pallas kernels  26.9 us (40%)
  starting transfers between devices  24 us (35%)
  waiting for transfers between devices  13.9 us (21%)
  between operations  1.41 us (2%)
  local copies, waits for them, and re-layouts  1.31 us (2%)
    pallas_call x13, Pallas kernels, call(): pl.pallas_call(kernel, out_shape=tuple((pinned.get(kind, jax.ShapeDtypeSt...  26.9 us
    ppermute x13, starting transfers between devices, rank_swap(): lax.ppermute(values, 'dp', [(rank, rank ^ step) for rank in range(count)])  13.9 us
    ppermute x13, waiting for transfers between devices, rank_swap(): lax.ppermute(values, 'dp', [(rank, rank ^ step) for rank in range(count)])  8.4 us
    all_to_all x1, starting transfers between devices, body(): lax.all_to_all(jnp.broadcast_to(cond[None], (dp_count,) + cond.shape), 'd...  8.29 us
    all_to_all x1, waiting for transfers between devices, body(): lax.all_to_all(jnp.broadcast_to(cond[None], (dp_count,) + cond.shape), 'd...  5 us
    ppermute x7, starting transfers between devices, swap_cores(): return lax.ppermute(values, 'seq', CORE_SWAP)  1.8 us
  transfers between devices with their start and end apart: 21, of which 8 were waited for; matrix products, arithmetic and copies ran while one was open for 2% of the time, Pallas kernels for 22%

profile of v3, /device:TPU:0, one launch (start us, length us, event | category | flops | bytes accessed | tf_op | source)
XLA Modules:
  0.0 67.5 jit_solution(6733813309541397417)
XLA Ops:
  0.6 0.5 collective-permute-start
  1.2 0.1 collective-permute-start.1
  1.2 1.3 %broadcast_in_dim.2 = bf16[16,2,384]{2,1,0:T(2,128)(2,1)} broadcast(bf16[2,384]{1,0:T(2,128)(2,1)} %own_cond_ref.1), dimensions={1,2} | broadcast | bytes 26112 | tf_op jit(solution)/shard_map/broadcast_in_dim | solution.py:1055
  2.5 8.3 %all-to-all-start = ((bf16[16,2,384]{2,1,0:T(2,128)(2,1)}), bf16[16,2,384]{2,1,0:T(2,128)(2,1)S(1)}, u32[]{:S(2)}, u32[]{:S(2)}) async-start(bf16[16,2,384]{2,1,0:T(2,128)(2,1)} %broadcast_in_dim.2), calls=%async_computation | async-start | bytes 49152 | tf_op jit(solution)/shard_map/all_to_all | solution.py:1054
  11.5 1.7 %load.1 = (bf16[2,256,384]{2,1,0:T(8,128)(2,1)S(1)}, f32[8,256]{1,0:T(8,128)S(1)}, bf16[8,128]{1,0:T(8,128)(2,1)S(1)}, f32[8,384]{1,0:T(8,128)S(1)}, f32[1,1152]...) custom-call(bf16[4,128,384]{2,1,0:T(8,128)(2,1)} %tokens_hbm.1, ...), custom_call_target="tpu_custom_call" | custom-call | flops 1 | bytes 1 | tf_op jit(solution)/shard_map/load/pallas_call | solution.py:915
  13.2 5.0 %all-to-all-done.cond_ref = bf16[16,2,384]{2,1,0:T(2,128)(2,1)S(1)} async-done(((bf16[16,2,384]{2,1,0:T(2,128)(2,1)}), bf16[16,2,384]{2,1,0:T(2,128)(2,1)S(1)}, u32[]{:S(2)}, u32[]{:S(2)}) %all-to-all-start) | async-done | bytes 24608 | tf_op jit(solution)/shard_map/all_to_all | solution.py:1054
  18.2 0.0 collective-permute-done.1.cot_far_ref
  18.2 9.7 %forward_and_ffn_grads.1 = (bf16[512,1152]{1,0:T(8,128)(2,1)S(1)}, bf16[512,384]{1,0:T(8,128)(2,1)S(1)}, f32[512,384]{1,0:T(8,128)S(1)}, f32[512,128]{1,0:T(8,12...) custom-call(bf16[16,2,384]{2,1,0:T(2,128)(2,1)S(1)} %all-to-all-done, ...), custom_call_target="tpu_custom_call" | custom-call | flops 1 | bytes 1 | tf_op jit(solution)/shard_map/forward_and_ffn_grads/pallas_call | solution.py:915
  27.9 0.1 collective-permute-start.2
  28.0 2.9 %norm_back.1 = (bf16[2,256,384]{2,1,0:T(8,128)(2,1)S(1)}, bf16[512,384]{1,0:T(8,128)(2,1)S(1)}, f32[512,384]{1,0:T(8,128)S(1)}, f32[192,384]{1,0:T(8,128)S(1)}, ...) custom-call(bf16[8,2304]{1,0:T(8,128)(2,1)S(1)} %get-tuple-element.112.mod_ref, ...), custom_call_target="tpu_custom_call" | custom-call | flops 1 | bytes 1 | tf_op jit(solution)/shard_map/norm_back/pallas_call | solution.py:915
  30.9 0.6 collective-permute-start.5
  31.5 0.0 collective-permute-done.2.recv_ref
  31.5 0.2 split_plane.1
  31.7 0.7 %collective-permute-start.3 = (bf16[392,384]{1,0:T(8,128)(2,1)S(1)}, bf16[392,384]{1,0:T(8,128)(2,1)S(1)}, u32[]{:S(2)}, u32[]{:S(2)}) collective-permute-start(bf16[392,384]{1,0:T(8,128)(2,1)S(1)} %get-tuple-element.105.after_ref), channel_id=1, source_target_pairs={{0,2},{2,0},{4,6},{6,4},{8,10},{10,8},{12,14},{14,12},{16,18},{18,... | collective-permute-start | bytes 903176 | tf_op jit(solution)/shard_map/ppermute | solution.py:932
  32.4 0.5 collective-permute-start.4
  32.9 6.8 %attention_back.1 = (bf16[2,256,384]{2,1,0:T(8,128)(2,1)S(1)}, f32[576,384]{1,0:T(8,128)S(1)}, bf16[416,384]{1,0:T(8,128)(2,1)S(1)}, bf16[424,384]{1,0:T(8,128)(2,1)S(1)}, f32[8,384]{1,0:T(8,128)S(1)}) custom-call(f32[512,384]{1,0:T(8,128)S(1)} %get-tuple-element.107.normed_ref, f32[512,128]{1,0:T(8,128)S(1)} %get-tuple-element.108.inverse_ref, ...), custom_call_target="tpu_custom_call" | custom-call | flops 1 | bytes 1 | tf_op jit(solution)/shard_map/attention_back/pallas_call | solution.py:915
  39.8 0.2 collective-permute-start.9
  40.0 0.3 collective-permute-start.8
  40.4 0.7 %collective-permute-done.4.recv_down_ref = bf16[384,384]{1,0:T(8,128)(2,1)S(1)} collective-permute-done((bf16[384,384]{1,0:T(8,128)(2,1)S(1)}, bf16[384,384]{1,0:T(8,128)(2,1)S(1)}, u32[]{:S(2)}, u32[]{:S(2)}) %collective-permute-start.4) | collective-permute-done | bytes 294944 | tf_op jit(solution)/shard_map/ppermute | solution.py:932
  41.1 0.1 cross_plane.1
  41.2 0.8 %collective-permute-start.6 = (bf16[208,384]{1,0:T(8,128)(2,1)S(1)}, bf16[208,384]{1,0:T(8,128)(2,1)S(1)}, u32[]{:S(2)}, u32[]{:S(2)}) collective-permute-start(bf16[208,384]{1,0:T(8,128)(2,1)S(1)} %get-tuple-element.130.refs_0_), channel_id=1, source_target_pairs={{0,4},{2,6},{4,0},{6,2},{8,12},{10,14},{12,8},{14,10},{16,20},{18,... | collective-permute-start | bytes 479240 | tf_op jit(solution)/shard_map/ppermute | solution.py:932
  42.1 1.4 %collective-permute-start.7 = (bf16[192,384]{1,0:T(8,128)(2,1)S(1)}, bf16[192,384]{1,0:T(8,128)(2,1)S(1)}, u32[]{:S(2)}, u32[]{:S(2)}) collective-permute-start(bf16[192,384]{1,0:T(8,128)(2,1)S(1)} %get-tuple-element.131), channel_id=1, source_target_pairs={{0,2},{2,0},{4,6},{6,4},{8,10},{10,8},{12,14},{14,12},{16,18},{18,... | collective-permute-start | bytes 442376 | tf_op jit(solution)/shard_map/ppermute | solution.py:932
  43.4 0.0 collective-permute-done.8.recv_ref.recv_two_ref
  43.5 0.2 split_qkv_plane.1
  43.7 0.7 %collective-permute-start.13 = (bf16[216,384]{1,0:T(8,128)(2,1)S(1)}, bf16[216,384]{1,0:T(8,128)(2,1)S(1)}, u32[]{:S(2)}, u32[]{:S(2)}) collective-permute-start(bf16[216,384]{1,0:T(8,128)(2,1)S(1)} %get-tuple-element.149), channel_id=1, source_target_pairs={{0,2},{2,0},{4,6},{6,4},{8,10},{10,8},{12,14},{14,12},{16,18},{18,... | collective-permute-start | bytes 497672 | tf_op jit(solution)/shard_map/ppermute | solution.py:932
  44.4 1.3 %collective-permute-start.14 = (bf16[216,384]{1,0:T(8,128)(2,1)S(1)}, bf16[216,384]{1,0:T(8,128)(2,1)S(1)}, u32[]{:S(2)}, u32[]{:S(2)}) collective-permute-start(bf16[216,384]{1,0:T(8,128)(2,1)S(1)} %get-tuple-element.150), channel_id=1, source_target_pairs={{0,4},{2,6},{4,0},{6,2},{8,12},{10,14},{12,8},{14,10},{16,20},{18,... | collective-permute-start | bytes 497672 | tf_op jit(solution)/shard_map/ppermute | solution.py:932
  45.6 1.6 %collective-permute-start.15 = (bf16[216,384]{1,0:T(8,128)(2,1)S(1)}, bf16[216,384]{1,0:T(8,128)(2,1)S(1)}, u32[]{:S(2)}, u32[]{:S(2)}) collective-permute-start(bf16[216,384]{1,0:T(8,128)(2,1)S(1)} %get-tuple-element.137.refs_3_), channel_id=1, source_target_pairs={{0,6},{2,4},{4,2},{6,0},{8,14},{10,12},{12,10},{14,8},{16,22},{18,... | collective-permute-start | bytes 497672 | tf_op jit(solution)/shard_map/ppermute | solution.py:932
  47.2 1.6 %collective-permute-done.7.refs_2_ = bf16[192,384]{1,0:T(8,128)(2,1)S(1)} collective-permute-done((bf16[192,384]{1,0:T(8,128)(2,1)S(1)}, bf16[192,384]{1,0:T(8,128)(2,1)S(1)}, u32[]{:S(2)}, u32[]{:S(2)}) %collective-permute-start.7) | collective-permute-done | bytes 147488 | tf_op jit(solution)/shard_map/ppermute | solution.py:932
  48.8 0.3 fold_plane.1
  49.1 0.6 collective-permute-start.10
  49.7 0.7 collective-permute-start.11
  50.3 2.0 %collective-permute-done.13.refs_1_ = bf16[216,384]{1,0:T(8,128)(2,1)S(1)} collective-permute-done((bf16[216,384]{1,0:T(8,128)(2,1)S(1)}, bf16[216,384]{1,0:T(8,128)(2,1)S(1)}, u32[]{:S(2)}, u32[]{:S(2)}) %collective-permute-start.13) | collective-permute-done | bytes 165920 | tf_op jit(solution)/shard_map/ppermute | solution.py:932
  52.4 1.2 %collective-permute-start.12 = (bf16[104,384]{1,0:T(8,128)(2,1)S(1)}, bf16[104,384]{1,0:T(8,128)(2,1)S(1)}, u32[]{:S(2)}, u32[]{:S(2)}) collective-permute-start(bf16[104,384]{1,0:T(8,128)(2,1)S(1)} %get-tuple-element.142), channel_id=1, source_target_pairs={{0,24},{2,26},{4,28},{6,30},{8,16},{10,18},{12,20},{14,22},{16,8},... | collective-permute-start | bytes 239624 | tf_op jit(solution)/shard_map/ppermute | solution.py:932
  53.6 0.0 collective-permute-done.14.refs_2_
  53.6 1.2 %collective-permute-done.15.refs_3_ = bf16[216,384]{1,0:T(8,128)(2,1)S(1)} collective-permute-done((bf16[216,384]{1,0:T(8,128)(2,1)S(1)}, bf16[216,384]{1,0:T(8,128)(2,1)S(1)}, u32[]{:S(2)}, u32[]{:S(2)}) %collective-permute-start.15) | collective-permute-done | bytes 165920 | tf_op jit(solution)/shard_map/ppermute | solution.py:932
  54.8 0.3 fold_qkv_plane.1
  55.1 0.7 collective-permute-start.16
  55.7 1.4 %collective-permute-start.17 = (bf16[104,384]{1,0:T(8,128)(2,1)S(1)}, bf16[104,384]{1,0:T(8,128)(2,1)S(1)}, u32[]{:S(2)}, u32[]{:S(2)}) collective-permute-start(bf16[104,384]{1,0:T(8,128)(2,1)S(1)} %get-tuple-element.153), channel_id=1, source_target_pairs={{0,16},{2,18},{4,20},{6,22},{8,24},{10,26},{12,28},{14,30},{16,0},... | collective-permute-start | bytes 239624 | tf_op jit(solution)/shard_map/ppermute | solution.py:932
  57.1 0.0 collective-permute-done.10.one_ref
  57.1 2.4 %collective-permute-start.18 = (bf16[104,384]{1,0:T(8,128)(2,1)S(1)}, bf16[104,384]{1,0:T(8,128)(2,1)S(1)}, u32[]{:S(2)}, u32[]{:S(2)}) collective-permute-start(bf16[104,384]{1,0:T(8,128)(2,1)S(1)} %get-tuple-element.154), channel_id=1, source_target_pairs={{0,24},{2,26},{4,28},{6,30},{8,16},{10,18},{12,20},{14,22},{16,8},... | collective-permute-start | bytes 239624 | tf_op jit(solution)/shard_map/ppermute | solution.py:932
  59.5 1.8 %finish_line.1 = (bf16[4,128,384]{2,1,0:T(8,128)(2,1)}, bf16[4,128,384]{2,1,0:T(8,128)(2,1)}, f32[24,768]{1,0:T(8,128)}, f32[96,192]{1,0:T(8,128)}, bf16[24,192]{1,0:T(8,128)(2,1)S(1)}, /*index=5*/s32[1,192]{1,0:T(1,128)S(1)}) custom-call(f32[96,384]{1,0:T(8,128)S(1)} %get-tuple-element.138.own_ref, bf16[8,384]{1,0:T(8,128)(2,1)S(1)} %get-tuple-element.139.own_small_ref, ...), custom_call_target="tpu_custom_call" | custom-call | flops 1 | bytes 1 | tf_op jit(solution)/shard_map/finish_line/pallas_call | solution.py:915
  61.3 0.1 collective-permute-done.16.one_ref
  61.5 2.7 %collective-permute-done.17.two_ref = bf16[104,384]{1,0:T(8,128)(2,1)S(1)} collective-permute-done((bf16[104,384]{1,0:T(8,128)(2,1)S(1)}, bf16[104,384]{1,0:T(8,128)(2,1)S(1)}, u32[]{:S(2)}, u32[]{:S(2)}) %collective-permute-start.17) | collective-permute-done | bytes 79904 | tf_op jit(solution)/shard_map/ppermute | solution.py:932
  64.2 0.0 collective-permute-done.18.three_ref
  64.2 1.4 %late_groups.1 = (f32[24,1152]{1,0:T(8,128)}, f32[8,384]{1,0:T(8,128)S(1)}, f32[8,384]{1,0:T(8,128)S(1)}, f32[384]{0:T(512)}, f32[1536]{0:T(1024)}, /*index=5*/f32[384]{0:T(512)}, f32[2,384]{1,0:T(2,128)}) custom-call(bf16[56,384]{1,0:T(8,128)(2,1)S(1)} %get-tuple-element.151.own_small_ref, bf16[104,384]{1,0:T(8,128)(2,1)S(1)} %collective-permute-done.16.one_ref, ...), custom_call_target="tpu_custom_call" | custom-call | flops 1 | bytes 1 | tf_op jit(solution)/shard_map/late_groups/pallas_call | solution.py:915
  65.6 0.7 %rest_sums.1 = (f32[24,192]{1,0:T(8,128)}, f32[24,576]{1,0:T(8,128)}) custom-call(f32[48,384]{1,0:T(8,128)S(1)} %get-tuple-element.160.own_ref, bf16[104,384]{1,0:T(8,128)(2,1)S(1)} %collective-permute-done.16.one_ref, bf16[104,384]{1,0:T(8,128)(2,1)S(1)} %collective-permute-done.17.two_ref, bf16[104,384]{1,0:T(8,128)(2,1)S(1)} %collective-permute-done.18.three_ref, ...), custom_call_target="tpu_custom_call" | custom-call | flops 1 | bytes 1 | tf_op jit(solution)/shard_map/rest_sums/pallas_call | solution.py:915
  66.3 0.5 collective-permute-done.19.recv_ref
  66.8 0.7 %final_groups.1 = (f32[2,192]{1,0:T(2,128)}, f32[2304]{0:T(1024)}) custom-call(f32[8,384]{1,0:T(8,128)S(1)} %get-tuple-element.157.own_ref, f32[8,384]{1,0:T(8,128)S(1)} %collective-permute-done.19.recv_ref, bf16[2,384]{1,0:T(2,128)(2,1)S(1)} %copy-done), custom_call_target="tpu_custom_call" | custom-call | flops 1 | bytes 1 | tf_op jit(solution)/shard_map/final_groups/pallas_call | solution.py:915
  (10 shorter events, 0.0 us)
Async XLA Ops:
  0.6 10.8 %collective-permute-start = (bf16[4,128,384]{2,1,0:T(8,128)(2,1)}, bf16[4,128,384]{2,1,0:T(8,128)(2,1)S(1)}, u32[]{:S(2)}, u32[]{:S(2)}) collective-permute-start(bf16[4,128,384]{2,1,0:T(8,128)(2,1)} %tokens_hbm.1), channel_id=1, source_target_pairs={{0,1},{1,0},{2,3},{3,2},{4,5},{5,4},{6,7},{7,6},{8,9},{9,8},{10,11... | collective-permute-start | bytes 1179656 | tf_op jit(solution)/shard_map/ppermute | solution.py:885
  1.2 17.1 %collective-permute-start.1 = (bf16[4,128,384]{2,1,0:T(8,128)(2,1)}, bf16[4,128,384]{2,1,0:T(8,128)(2,1)S(1)}, u32[]{:S(2)}, u32[]{:S(2)}) collective-permute-start(bf16[4,128,384]{2,1,0:T(8,128)(2,1)} %cot_hbm.1), channel_id=1, source_target_pairs={{0,1},{1,0},{2,3},{3,2},{4,5},{5,4},{6,7},{7,6},{8,9},{9,8},{10,11... | collective-permute-start | bytes 1179656 | tf_op jit(solution)/shard_map/ppermute | solution.py:885
  2.5 15.7 %all-to-all-start = ((bf16[16,2,384]{2,1,0:T(2,128)(2,1)}), bf16[16,2,384]{2,1,0:T(2,128)(2,1)S(1)}, u32[]{:S(2)}, u32[]{:S(2)}) async-start(bf16[16,2,384]{2,1,0:T(2,128)(2,1)} %broadcast_in_dim.2), calls=%async_computation | async-start | bytes 49152 | tf_op jit(solution)/shard_map/all_to_all | solution.py:1054
  27.9 3.6 %collective-permute-start.2 = (bf16[1536,384]{1,0:T(8,128)(2,1)S(1)}, bf16[1536,384]{1,0:T(8,128)(2,1)S(1)}, u32[]{:S(2)}, u32[]{:S(2)}) collective-permute-start(bf16[1536,384]{1,0:T(8,128)(2,1)S(1)} %get-tuple-element.101), channel_id=1, source_target_pairs={{0,1},{1,0},{2,3},{3,2},{4,5},{5,4},{6,7},{7,6},{8,9},{9,8},{10,11... | collective-permute-start | bytes 3538952 | tf_op jit(solution)/shard_map/ppermute | solution.py:885
  30.9 2.0 %collective-permute-start.5 = (bf16[464,384]{1,0:T(8,128)(2,1)S(1)}, bf16[464,384]{1,0:T(8,128)(2,1)S(1)}, u32[]{:S(2)}, u32[]{:S(2)}) collective-permute-start(bf16[464,384]{1,0:T(8,128)(2,1)S(1)} %get-tuple-element.127), channel_id=1, source_target_pairs={{0,1},{1,0},{2,3},{3,2},{4,5},{5,4},{6,7},{7,6},{8,9},{9,8},{10,11... | collective-permute-start | bytes 1069064 | tf_op jit(solution)/shard_map/ppermute | solution.py:885
  31.7 9.4 %collective-permute-start.3 = (bf16[392,384]{1,0:T(8,128)(2,1)S(1)}, bf16[392,384]{1,0:T(8,128)(2,1)S(1)}, u32[]{:S(2)}, u32[]{:S(2)}) collective-permute-start(bf16[392,384]{1,0:T(8,128)(2,1)S(1)} %get-tuple-element.105.after_ref), channel_id=1, source_target_pairs={{0,2},{2,0},{4,6},{6,4},{8,10},{10,8},{12,14},{14,12},{16,18},{18,... | collective-permute-start | bytes 903176 | tf_op jit(solution)/shard_map/ppermute | solution.py:932
  32.4 8.7 %collective-permute-start.4 = (bf16[384,384]{1,0:T(8,128)(2,1)S(1)}, bf16[384,384]{1,0:T(8,128)(2,1)S(1)}, u32[]{:S(2)}, u32[]{:S(2)}) collective-permute-start(bf16[384,384]{1,0:T(8,128)(2,1)S(1)} %get-tuple-element.106.after_too_ref), channel_id=1, source_target_pairs={{0,4},{2,6},{4,0},{6,2},{8,12},{10,14},{12,8},{14,10},{16,20},{18,... | collective-permute-start | bytes 884744 | tf_op jit(solution)/shard_map/ppermute | solution.py:932
  39.8 3.7 %collective-permute-start.9 = (bf16[424,384]{1,0:T(8,128)(2,1)S(1)}, bf16[424,384]{1,0:T(8,128)(2,1)S(1)}, u32[]{:S(2)}, u32[]{:S(2)}) collective-permute-start(bf16[424,384]{1,0:T(8,128)(2,1)S(1)} %get-tuple-element.134), channel_id=1, source_target_pairs={{0,1},{1,0},{2,3},{3,2},{4,5},{5,4},{6,7},{7,6},{8,9},{9,8},{10,11... | collective-permute-start | bytes 976904 | tf_op jit(solution)/shard_map/ppermute | solution.py:885
  40.0 3.4 %collective-permute-start.8 = (bf16[416,384]{1,0:T(8,128)(2,1)S(1)}, bf16[416,384]{1,0:T(8,128)(2,1)S(1)}, u32[]{:S(2)}, u32[]{:S(2)}) collective-permute-start(bf16[416,384]{1,0:T(8,128)(2,1)S(1)} %get-tuple-element.133), channel_id=1, source_target_pairs={{0,1},{1,0},{2,3},{3,2},{4,5},{5,4},{6,7},{7,6},{8,9},{9,8},{10,11... | collective-permute-start | bytes 958472 | tf_op jit(solution)/shard_map/ppermute | solution.py:885
  41.2 7.6 %collective-permute-start.6 = (bf16[208,384]{1,0:T(8,128)(2,1)S(1)}, bf16[208,384]{1,0:T(8,128)(2,1)S(1)}, u32[]{:S(2)}, u32[]{:S(2)}) collective-permute-start(bf16[208,384]{1,0:T(8,128)(2,1)S(1)} %get-tuple-element.130.refs_0_), channel_id=1, source_target_pairs={{0,4},{2,6},{4,0},{6,2},{8,12},{10,14},{12,8},{14,10},{16,20},{18,... | collective-permute-start | bytes 479240 | tf_op jit(solution)/shard_map/ppermute | solution.py:932
  42.1 6.7 %collective-permute-start.7 = (bf16[192,384]{1,0:T(8,128)(2,1)S(1)}, bf16[192,384]{1,0:T(8,128)(2,1)S(1)}, u32[]{:S(2)}, u32[]{:S(2)}) collective-permute-start(bf16[192,384]{1,0:T(8,128)(2,1)S(1)} %get-tuple-element.131), channel_id=1, source_target_pairs={{0,2},{2,0},{4,6},{6,4},{8,10},{10,8},{12,14},{14,12},{16,18},{18,... | collective-permute-start | bytes 442376 | tf_op jit(solution)/shard_map/ppermute | solution.py:932
  43.7 8.7 %collective-permute-start.13 = (bf16[216,384]{1,0:T(8,128)(2,1)S(1)}, bf16[216,384]{1,0:T(8,128)(2,1)S(1)}, u32[]{:S(2)}, u32[]{:S(2)}) collective-permute-start(bf16[216,384]{1,0:T(8,128)(2,1)S(1)} %get-tuple-element.149), channel_id=1, source_target_pairs={{0,2},{2,0},{4,6},{6,4},{8,10},{10,8},{12,14},{14,12},{16,18},{18,... | collective-permute-start | bytes 497672 | tf_op jit(solution)/shard_map/ppermute | solution.py:932
  44.4 9.2 %collective-permute-start.14 = (bf16[216,384]{1,0:T(8,128)(2,1)S(1)}, bf16[216,384]{1,0:T(8,128)(2,1)S(1)}, u32[]{:S(2)}, u32[]{:S(2)}) collective-permute-start(bf16[216,384]{1,0:T(8,128)(2,1)S(1)} %get-tuple-element.150), channel_id=1, source_target_pairs={{0,4},{2,6},{4,0},{6,2},{8,12},{10,14},{12,8},{14,10},{16,20},{18,... | collective-permute-start | bytes 497672 | tf_op jit(solution)/shard_map/ppermute | solution.py:932
  45.6 9.1 %collective-permute-start.15 = (bf16[216,384]{1,0:T(8,128)(2,1)S(1)}, bf16[216,384]{1,0:T(8,128)(2,1)S(1)}, u32[]{:S(2)}, u32[]{:S(2)}) collective-permute-start(bf16[216,384]{1,0:T(8,128)(2,1)S(1)} %get-tuple-element.137.refs_3_), channel_id=1, source_target_pairs={{0,6},{2,4},{4,2},{6,0},{8,14},{10,12},{12,10},{14,8},{16,22},{18,... | collective-permute-start | bytes 497672 | tf_op jit(solution)/shard_map/ppermute | solution.py:932
  49.1 8.0 %collective-permute-start.10 = (bf16[104,384]{1,0:T(8,128)(2,1)S(1)}, bf16[104,384]{1,0:T(8,128)(2,1)S(1)}, u32[]{:S(2)}, u32[]{:S(2)}) collective-permute-start(bf16[104,384]{1,0:T(8,128)(2,1)S(1)} %get-tuple-element.140), channel_id=1, source_target_pairs={{0,8},{2,10},{4,12},{6,14},{8,0},{10,2},{12,4},{14,6},{16,24},{18,... | collective-permute-start | bytes 239624 | tf_op jit(solution)/shard_map/ppermute | solution.py:932
  49.7 9.8 %collective-permute-start.11 = (bf16[104,384]{1,0:T(8,128)(2,1)S(1)}, bf16[104,384]{1,0:T(8,128)(2,1)S(1)}, u32[]{:S(2)}, u32[]{:S(2)}) collective-permute-start(bf16[104,384]{1,0:T(8,128)(2,1)S(1)} %get-tuple-element.141), channel_id=1, source_target_pairs={{0,16},{2,18},{4,20},{6,22},{8,24},{10,26},{12,28},{14,30},{16,0},... | collective-permute-start | bytes 239624 | tf_op jit(solution)/shard_map/ppermute | solution.py:932
  52.4 7.2 %collective-permute-start.12 = (bf16[104,384]{1,0:T(8,128)(2,1)S(1)}, bf16[104,384]{1,0:T(8,128)(2,1)S(1)}, u32[]{:S(2)}, u32[]{:S(2)}) collective-permute-start(bf16[104,384]{1,0:T(8,128)(2,1)S(1)} %get-tuple-element.142), channel_id=1, source_target_pairs={{0,24},{2,26},{4,28},{6,30},{8,16},{10,18},{12,20},{14,22},{16,8},... | collective-permute-start | bytes 239624 | tf_op jit(solution)/shard_map/ppermute | solution.py:932
  55.1 6.4 %collective-permute-start.16 = (bf16[104,384]{1,0:T(8,128)(2,1)S(1)}, bf16[104,384]{1,0:T(8,128)(2,1)S(1)}, u32[]{:S(2)}, u32[]{:S(2)}) collective-permute-start(bf16[104,384]{1,0:T(8,128)(2,1)S(1)} %get-tuple-element.152), channel_id=1, source_target_pairs={{0,8},{2,10},{4,12},{6,14},{8,0},{10,2},{12,4},{14,6},{16,24},{18,... | collective-permute-start | bytes 239624 | tf_op jit(solution)/shard_map/ppermute | solution.py:932
  55.7 8.5 %collective-permute-start.17 = (bf16[104,384]{1,0:T(8,128)(2,1)S(1)}, bf16[104,384]{1,0:T(8,128)(2,1)S(1)}, u32[]{:S(2)}, u32[]{:S(2)}) collective-permute-start(bf16[104,384]{1,0:T(8,128)(2,1)S(1)} %get-tuple-element.153), channel_id=1, source_target_pairs={{0,16},{2,18},{4,20},{6,22},{8,24},{10,26},{12,28},{14,30},{16,0},... | collective-permute-start | bytes 239624 | tf_op jit(solution)/shard_map/ppermute | solution.py:932
  57.1 7.1 %collective-permute-start.18 = (bf16[104,384]{1,0:T(8,128)(2,1)S(1)}, bf16[104,384]{1,0:T(8,128)(2,1)S(1)}, u32[]{:S(2)}, u32[]{:S(2)}) collective-permute-start(bf16[104,384]{1,0:T(8,128)(2,1)S(1)} %get-tuple-element.154), channel_id=1, source_target_pairs={{0,24},{2,26},{4,28},{6,30},{8,16},{10,18},{12,20},{14,22},{16,8},... | collective-permute-start | bytes 239624 | tf_op jit(solution)/shard_map/ppermute | solution.py:932
  64.2 2.6 %copy-start = (bf16[2,384]{1,0:T(2,128)(2,1)S(1)}, bf16[2,384]{1,0:T(2,128)(2,1)}, u32[]{:S(2)}) copy-start(bf16[2,384]{1,0:T(2,128)(2,1)} %own_cond_ref.1) | copy-start | bytes 4612
  65.6 1.2 %collective-permute-start.19 = (f32[8,384]{1,0:T(8,128)S(1)}, f32[8,384]{1,0:T(8,128)S(1)}, u32[]{:S(2)}, u32[]{:S(2)}) collective-permute-start(f32[8,384]{1,0:T(8,128)S(1)} %get-tuple-element.158.after_ref), channel_id=1, source_target_pairs={{0,1},{1,0},{2,3},{3,2},{4,5},{5,4},{6,7},{7,6},{8,9},{9,8},{10,11... | collective-permute-start | bytes 36872 | tf_op jit(solution)/shard_map/ppermute | solution.py:885

commit v4 on v3

--- a/solution.py
+++ b/solution.py
@@ -58,12 +58,6 @@
 
 def masked(values, mask):
     return jnp.where(mask, values, jnp.zeros_like(values))
-
-
-def softmax_rows(queries, keys, penalty):
-    scores = nt(queries, keys) + penalty
-    exps = jnp.exp(scores - jnp.max(scores, axis=-1, keepdims=True))
-    return exps / jnp.sum(exps, axis=-1, keepdims=True)
 
 
 def fetch(pairs, sems):
@@ -233,6 +227,7 @@
     inverse_ref,
     mod_ref,
     lead_ref,
+    logs_ref,
     att_ref,
     mid_ref,
     attn_ref,
@@ -271,7 +266,8 @@
     block_count, block_rows = cond_ref.shape[:2]
     cond_rows_ref[...] = jnp.zeros_like(cond_rows_ref)
     for block in range(block_count):
-        cond_rows_ref[8 * block : 8 * block + block_rows, :] = cond_ref[block].astype(F32)
+        start = 8 * (block_count - 1 - block)
+        cond_rows_ref[start : start + block_rows, :] = cond_ref[block].astype(F32)
     cond = cond_rows_ref[...]
     silu = cond / (1.0 + jnp.exp(-cond))
     image_silu = nn(hot_ref[...], silu.astype(LOW)).astype(LOW)
@@ -300,9 +296,16 @@
         image = step // (HEADS // 2)
         penalty = penalty_ref[image : image + 1, :]
         total = jnp.zeros((length, PAIR), F32)
-        for mask in (first, second):
-            probs = softmax_rows(masked(queries, mask), keys, penalty).astype(LOW)
-            total = total + nn(probs, masked(values, mask))
+        for side, mask in enumerate((first, second)):
+            scores = nt(masked(queries, mask), keys) + penalty
+            top = jnp.max(scores, axis=-1, keepdims=True)
+            exps = jnp.exp(scores - top)
+            whole = jnp.sum(exps, axis=-1, keepdims=True)
+            head = 2 * (step % (HEADS // 2)) + side
+            logs_ref[rows, head * LANES : (head + 1) * LANES] = jnp.broadcast_to(
+                top + jnp.log(whole), (length, LANES)
+            )
+            total = total + nn((exps / whole).astype(LOW), masked(values, mask))
         att_ref[rows, lanes(0)] = total.astype(LOW)
 
     for copy in copies[1:]:
@@ -445,6 +448,7 @@
     normed_ref,
     inverse_ref,
     penalty_ref,
+    logs_ref,
     qkv_w_ref,
     qkv_ref,
     h1_ref,
@@ -476,10 +480,13 @@
         grad_q = jnp.zeros((length, PAIR), F32)
         grad_k = jnp.zeros((length, PAIR), F32)
         grad_v = jnp.zeros((length, PAIR), F32)
-        for mask in (first, second):
+        for side, mask in enumerate((first, second)):
             own_queries = masked(queries, mask)
             own_grad = masked(grad_att, mask)
-            probs = softmax_rows(own_queries, keys, penalty)
+            head = 2 * (step % (HEADS // 2)) + side
+            logs = logs_ref[rows, head * LANES : (head + 1) * LANES]
+            logs = jnp.concatenate([logs] * (length // LANES), axis=1)
+            probs = jnp.exp(nt(own_queries, keys) + penalty - logs)
             grad_probs = nt(own_grad, values)
             dots = jnp.sum(probs * grad_probs, axis=-1, keepdims=True)
             grad_scores = (probs * (grad_probs - dots)).astype(LOW)
@@ -698,9 +705,8 @@
     return jnp.where(place == wanted, 1.0, 0.0).astype(LOW)
 
 
-def group_parts(silu_rows, own_groups, kinds, kind_of):
+def group_rows(own_groups, kinds, kind_of):
     zeros = jnp.zeros_like(kind_of, F32)
-    blocks = [masked(silu_rows, kind_of == kind) for kind in kinds]
     rows = []
     for kind in kinds:
         for one in own_groups:
@@ -709,13 +715,14 @@
         rows.append(jnp.where(kind_of == kind, 1.0, zeros))
     while len(rows) % 8:
         rows.append(zeros)
-    return blocks, jnp.concatenate(rows, axis=0).astype(LOW)
+    return jnp.concatenate(rows, axis=0).astype(LOW)
 
 
 def split_dot(values, weight):
     high = values.astype(LOW)
     low = (values - high.astype(F32)).astype(LOW)
-    return nt(high, weight) + nt(low, weight)
+    both = nt(jnp.concatenate([high.astype(F32), low.astype(F32)], axis=0).astype(LOW), weight)
+    return both[: values.shape[0]] + both[values.shape[0] :]
 
 
 def finish_kernel(
@@ -786,17 +793,15 @@
     one_ref,
     two_ref,
     three_ref,
-    silu_ref,
     ids_ref,
     ada_ref,
-    ada_out_ref,
+    stack_out_ref,
     own_sums_ref,
     send_ref,
     out_bias_ref,
     up_bias_ref,
     down_bias_ref,
     qv_ref,
-    stack_ref,
     bias_ref,
 ):
     core = lax.axis_index("seq")
@@ -808,17 +813,14 @@
         part[2 * piece :, :] for part in (one_ref, two_ref, three_ref)
     )
     for step, small in enumerate(smalls):
-        stack_ref[line ^ step] = small[:48]
+        stack_out_ref[line ^ step] = small[:48]
         bias_ref[line ^ step] = small[48:].astype(F32)
-    stack = stack_ref[...].reshape(192, width)
+    stack = stack_out_ref[...].reshape(192, width)
     ids = ids_ref[...]
     item = lax.broadcasted_iota(jnp.int32, (1, 192), 1) % 12
     base = GROUPS_PER_RANK * lax.axis_index("dp")
     own = [ids == base + index for index in range(GROUPS_PER_RANK)]
-    blocks, rows = group_parts(silu_ref[...], own, range(3), item // 4)
-    sums = nn(rows, stack)
-    for kind in range(3):
-        ada_out_ref[:, kind * width : (kind + 1) * width] = nn(blocks[kind], stack)
+    sums = nn(group_rows(own, range(3), item // 4), stack)
     weight = ada_ref[:, pl.ds(pl.multiple_of(core * 3 * width, LANES), 3 * width)]
     own_sum = jnp.concatenate(
         [
@@ -848,7 +850,9 @@
     qv_ref[...] = bias[6:8]
 
 
-def rest_kernel(own_ref, one_ref, two_ref, three_ref, after_ref, out_ref, qkv_ref):
+def rest_kernel(
+    own_ref, one_ref, two_ref, three_ref, stack_ref, silu_ref, after_ref, out_ref, qkv_ref, ada_out_ref
+):
     core = lax.axis_index("seq")
     width = own_ref.shape[1]
     piece = width // 16
@@ -861,6 +865,12 @@
         jnp.concatenate([pair, unit], axis=1),
         jnp.concatenate([unit, pair], axis=1),
     )
+    stack = stack_ref[...].reshape(192, width)
+    kind_of = lax.broadcasted_iota(jnp.int32, (1, 192), 1) % 12 // 4
+    for kind in range(3):
+        ada_out_ref[:, kind * width : (kind + 1) * width] = nn(
+            masked(silu_ref[...], kind_of == kind), stack
+        )
 
 
 def final_kernel(own_ref, recv_ref, own_cond_ref, cond_ref, bias_ref):
@@ -1052,7 +1062,12 @@
     piece = width // dp_count
     fast = dp_count == 16 and not GENERAL
     cond_blocks = lax.all_to_all(
-        jnp.broadcast_to(cond[None], (dp_count,) + cond.shape), "dp", 0, 0, tiled=True
+        jnp.broadcast_to(cond[None], (dp_count,) + cond.shape),
+        "dp",
+        0,
+        0,
+        axis_index_groups=[list(range(dp_count))[::-1]],
+        tiled=True,
     )
     tokens_far = swap_cores(tokens)
     cot_far = swap_cores(cotangent)
@@ -1117,6 +1132,7 @@
         inverse,
         image_mod,
         lead,
+        logs,
         att,
         middle,
         attn,
@@ -1141,6 +1157,7 @@
             ((row_count, LANES), F32),
             ((8, mod_width), LOW),
             ((24, 8 * dp_count), LOW),
+            ((row_count, HEADS * LANES), F32),
             ((row_count, width), LOW),
             ((row_count, width), F32),
             ((row_count, width), F32),
@@ -1164,7 +1181,7 @@
             pltpu.SemaphoreType.DMA((4 + 2 * image_count,)),
         ],
         24,
-        ("V" * 10 + "h" * 5, "V" * 20),
+        ("V" * 10 + "h" * 5, "V" * 21),
         cond_blocks,
         images,
         cot_far,
@@ -1223,10 +1240,11 @@
             ),
             [vmem((row_count, 3 * width), LOW)],
             24,
-            ("V" * 9 + "aaa", "VVVVV"),
+            ("V" * 10 + "aaa", "VVVVV"),
             normed,
             inverse,
             penalty,
+            logs,
             qkv_weight_near,
             qkv,
             h1,
@@ -1248,7 +1266,7 @@
             ((keep_one, send_one), (keep_out, send_out), (keep_two, send_two, send_other)),
             (small_one, small_two),
             (output, grad_tokens),
-            cond_blocks.reshape(-1, width),
+            cond_blocks[::-1].reshape(-1, width),
             cond,
             own_ids,
             ada_weight,
@@ -1366,7 +1384,7 @@
         grad_tokens,
     )
     (
-        ada_sum,
+        stack,
         own_sums,
         send_sums,
         out_bias_sum,
@@ -1377,7 +1395,7 @@
         late_kernel,
         "late_groups",
         (
-            ((piece, mod_width // 2), F32),
+            ((4, 48, width), LOW),
             ((8, width), F32),
             ((8, width), F32),
             ((width,), F32),
@@ -1385,24 +1403,25 @@
             ((width,), F32),
             ((2, width), F32),
         ),
-        [vmem((4, 48, width), LOW), vmem((4, 8, width), F32)],
+        [vmem((4, 8, width), F32)],
         16,
-        ("V" * 7, "vVVvvvv"),
+        ("V" * 6, "VVVvvvv"),
         rest_small,
         *lines_qkv,
-        silu_rows,
         all_ids,
         ada_weight_near,
     )
-    out_sum, qkv_sum = call(
+    out_sum, qkv_sum, ada_sum = call(
         rest_kernel,
         "rest_sums",
-        (((piece, half), F32), ((piece, 3 * half), F32)),
+        (((piece, half), F32), ((piece, 3 * half), F32), ((piece, mod_width // 2), F32)),
         [],
         16,
-        ("VVVVa", "vv"),
+        ("VVVVVVa", "vvv"),
         rest_qkv,
         *lines_qkv,
+        stack,
+        silu_rows,
         send_sums,
     )
     grad_cond, ada_bias_sum = call(

time: 67.7 us -> 66.5 us (0.982)
  waiting for transfers between devices: 13.9 us -> 6.75 us
  starting transfers between devices: 24 us -> 30.9 us
  Pallas kernels: 26.9 us -> 25.9 us
    ppermute x13, starting transfers between devices: 13.9 us -> 18.8 us  [rank_swap(): lax.ppermute(values, 'dp', [(rank, rank ^ step) for rank in range(count)])]
    all_to_all x1, waiting for transfers between devices: 5 us -> 0.1 us  [body(): lax.all_to_all(jnp.broadcast_to(cond[None], (dp_count,) + cond.shape), 'd...]
    ppermute x13, waiting for transfers between devices: 8.4 us -> 6.32 us  [rank_swap(): lax.ppermute(values, 'dp', [(rank, rank ^ step) for rank in range(count)])]
    all_to_all x1, starting transfers between devices: 8.29 us -> 10.3 us  [body(): lax.all_to_all(jnp.broadcast_to(cond[None], (dp_count,) + cond.shape), 'd...]
    pallas_call x13, Pallas kernels: 26.9 us -> 25.9 us  [call(): pl.pallas_call(kernel, out_shape=tuple((pinned.get(kind, jax.ShapeDtypeSt...]
  transfers between devices with their start and end apart: 21 -> 21, of which waited for: 8 -> 6; matrix products, arithmetic and copies ran while one was open for 2% -> 2% of each run, Pallas kernels for 22% -> 22%
where the time goes in v4:
time: 66.5 us; the launch traced here: 66.3 us
  starting transfers between devices  30.9 us (46%)
  Pallas kernels  25.9 us (39%)
  waiting for transfers between devices  6.75 us (10%)
  between operations  1.41 us (2%)
  local copies, waits for them, and re-layouts  1.31 us (2%)
    pallas_call x13, Pallas kernels, call(): pl.pallas_call(kernel, out_shape=tuple((pinned.get(kind, jax.ShapeDtypeSt...  25.9 us
    ppermute x13, starting transfers between devices, rank_swap(): lax.ppermute(values, 'dp', [(rank, rank ^ step) for rank in range(count)])  18.8 us
    all_to_all x1, starting transfers between devices, body(): lax.all_to_all(jnp.broadcast_to(cond[None], (dp_count,) + cond.shape), 'd...  10.3 us
    ppermute x13, waiting for transfers between devices, rank_swap(): lax.ppermute(values, 'dp', [(rank, rank ^ step) for rank in range(count)])  6.32 us
    ppermute x7, starting transfers between devices, swap_cores(): return lax.ppermute(values, 'seq', CORE_SWAP)  1.79 us
  transfers between devices with their start and end apart: 21, of which 6 were waited for; matrix products, arithmetic and copies ran while one was open for 2% of the time, Pallas kernels for 22%

profile of v4, /device:TPU:0, one launch (start us, length us, event | category | flops | bytes accessed | tf_op | source)
XLA Modules:
  0.0 66.3 jit_solution(5893794289309646815)
XLA Ops:
  0.6 0.5 collective-permute-start
  1.2 0.1 collective-permute-start.1
  1.2 1.3 %broadcast_in_dim.2 = bf16[16,2,384]{2,1,0:T(2,128)(2,1)} broadcast(bf16[2,384]{1,0:T(2,128)(2,1)} %own_cond_ref.1), dimensions={1,2} | broadcast | bytes 26112 | tf_op jit(solution)/shard_map/broadcast_in_dim | solution.py:1065
  2.5 10.3 %all-to-all-start = ((bf16[16,2,384]{2,1,0:T(2,128)(2,1)}), bf16[16,2,384]{2,1,0:T(2,128)(2,1)S(1)}, u32[]{:S(2)}, u32[]{:S(2)}) async-start(bf16[16,2,384]{2,1,0:T(2,128)(2,1)} %broadcast_in_dim.2), calls=%async_computation | async-start | bytes 49152 | tf_op jit(solution)/shard_map/all_to_all | solution.py:1064
  13.5 0.0 collective-permute-done.tokens_far_ref
  13.5 1.7 %load.1 = (bf16[2,256,384]{2,1,0:T(8,128)(2,1)S(1)}, f32[8,256]{1,0:T(8,128)S(1)}, bf16[8,128]{1,0:T(8,128)(2,1)S(1)}, f32[8,384]{1,0:T(8,128)S(1)}, f32[1,1152]...) custom-call(bf16[4,128,384]{2,1,0:T(8,128)(2,1)} %tokens_hbm.1, ...), custom_call_target="tpu_custom_call" | custom-call | flops 1 | bytes 1 | tf_op jit(solution)/shard_map/load/pallas_call | solution.py:925
  15.2 0.1 all-to-all-done.cond_ref
  15.3 9.7 %forward_and_ffn_grads.1 = (bf16[512,1152]{1,0:T(8,128)(2,1)S(1)}, bf16[512,384]{1,0:T(8,128)(2,1)S(1)}, f32[512,384]{1,0:T(8,128)S(1)}, f32[512,128]{1,0:T(8,12...) custom-call(bf16[16,2,384]{2,1,0:T(2,128)(2,1)S(1)} %all-to-all-done, ...), custom_call_target="tpu_custom_call" | custom-call | flops 1 | bytes 1 | tf_op jit(solution)/shard_map/forward_and_ffn_grads/pallas_call | solution.py:925
  25.0 0.1 collective-permute-start.2
  25.1 3.0 %norm_back.1 = (bf16[2,256,384]{2,1,0:T(8,128)(2,1)S(1)}, bf16[512,384]{1,0:T(8,128)(2,1)S(1)}, f32[512,384]{1,0:T(8,128)S(1)}, f32[192,384]{1,0:T(8,128)S(1)}, ...) custom-call(bf16[8,2304]{1,0:T(8,128)(2,1)S(1)} %get-tuple-element.115.mod_ref, ...), custom_call_target="tpu_custom_call" | custom-call | flops 1 | bytes 1 | tf_op jit(solution)/shard_map/norm_back/pallas_call | solution.py:925
  28.1 0.6 collective-permute-start.5
  28.7 0.2 split_plane.1
  28.9 1.5 %collective-permute-start.3 = (bf16[392,384]{1,0:T(8,128)(2,1)S(1)}, bf16[392,384]{1,0:T(8,128)(2,1)S(1)}, u32[]{:S(2)}, u32[]{:S(2)}) collective-permute-start(bf16[392,384]{1,0:T(8,128)(2,1)S(1)} %get-tuple-element.107.after_ref), channel_id=1, source_target_pairs={{0,2},{2,0},{4,6},{6,4},{8,10},{10,8},{12,14},{14,12},{16,18},{18,... | collective-permute-start | bytes 903176 | tf_op jit(solution)/shard_map/ppermute | solution.py:942
  30.4 1.5 %collective-permute-start.4 = (bf16[384,384]{1,0:T(8,128)(2,1)S(1)}, bf16[384,384]{1,0:T(8,128)(2,1)S(1)}, u32[]{:S(2)}, u32[]{:S(2)}) collective-permute-start(bf16[384,384]{1,0:T(8,128)(2,1)S(1)} %get-tuple-element.108.after_too_ref), channel_id=1, source_target_pairs={{0,4},{2,6},{4,0},{6,2},{8,12},{10,14},{12,8},{14,10},{16,20},{18,... | collective-permute-start | bytes 884744 | tf_op jit(solution)/shard_map/ppermute | solution.py:942
  31.9 5.8 %attention_back.1 = (bf16[2,256,384]{2,1,0:T(8,128)(2,1)S(1)}, f32[576,384]{1,0:T(8,128)S(1)}, bf16[416,384]{1,0:T(8,128)(2,1)S(1)}, bf16[424,384]{1,0:T(8,128)(2,1)S(1)}, f32[8,384]{1,0:T(8,128)S(1)}) custom-call(f32[512,384]{1,0:T(8,128)S(1)} %get-tuple-element.109.normed_ref, f32[512,128]{1,0:T(8,128)S(1)} %get-tuple-element.110.inverse_ref, ...), custom_call_target="tpu_custom_call" | custom-call | flops 1 | bytes 1 | tf_op jit(solution)/shard_map/attention_back/pallas_call | solution.py:925
  37.7 0.1 collective-permute-start.9
  37.8 0.5 collective-permute-start.8
  38.3 0.8 %collective-permute-done.4.recv_down_ref = bf16[384,384]{1,0:T(8,128)(2,1)S(1)} collective-permute-done((bf16[384,384]{1,0:T(8,128)(2,1)S(1)}, bf16[384,384]{1,0:T(8,128)(2,1)S(1)}, u32[]{:S(2)}, u32[]{:S(2)}) %collective-permute-start.4) | collective-permute-done | bytes 294944 | tf_op jit(solution)/shard_map/ppermute | solution.py:942
  39.1 0.0 collective-permute-done.3.recv_up_ref
  39.1 0.1 cross_plane.1
  39.2 1.5 %collective-permute-start.6 = (bf16[208,384]{1,0:T(8,128)(2,1)S(1)}, bf16[208,384]{1,0:T(8,128)(2,1)S(1)}, u32[]{:S(2)}, u32[]{:S(2)}) collective-permute-start(bf16[208,384]{1,0:T(8,128)(2,1)S(1)} %get-tuple-element.133.refs_0_), channel_id=1, source_target_pairs={{0,4},{2,6},{4,0},{6,2},{8,12},{10,14},{12,8},{14,10},{16,20},{18,... | collective-permute-start | bytes 479240 | tf_op jit(solution)/shard_map/ppermute | solution.py:942
  40.8 0.5 collective-permute-start.7
  41.3 0.0 collective-permute-done.8.recv_ref.recv_two_ref
  41.3 0.0 collective-permute-done.9.other_ref.recv_other_ref
  41.3 0.2 split_qkv_plane.1
  41.6 1.5 %collective-permute-start.13 = (bf16[216,384]{1,0:T(8,128)(2,1)S(1)}, bf16[216,384]{1,0:T(8,128)(2,1)S(1)}, u32[]{:S(2)}, u32[]{:S(2)}) collective-permute-start(bf16[216,384]{1,0:T(8,128)(2,1)S(1)} %get-tuple-element.152), channel_id=1, source_target_pairs={{0,2},{2,0},{4,6},{6,4},{8,10},{10,8},{12,14},{14,12},{16,18},{18,... | collective-permute-start | bytes 497672 | tf_op jit(solution)/shard_map/ppermute | solution.py:942
  43.1 0.6 collective-permute-start.14
  43.7 1.4 %collective-permute-start.15 = (bf16[216,384]{1,0:T(8,128)(2,1)S(1)}, bf16[216,384]{1,0:T(8,128)(2,1)S(1)}, u32[]{:S(2)}, u32[]{:S(2)}) collective-permute-start(bf16[216,384]{1,0:T(8,128)(2,1)S(1)} %get-tuple-element.140.refs_3_), channel_id=1, source_target_pairs={{0,6},{2,4},{4,2},{6,0},{8,14},{10,12},{12,10},{14,8},{16,22},{18,... | collective-permute-start | bytes 497672 | tf_op jit(solution)/shard_map/ppermute | solution.py:942
  45.1 2.4 %collective-permute-done.7.refs_2_ = bf16[192,384]{1,0:T(8,128)(2,1)S(1)} collective-permute-done((bf16[192,384]{1,0:T(8,128)(2,1)S(1)}, bf16[192,384]{1,0:T(8,128)(2,1)S(1)}, u32[]{:S(2)}, u32[]{:S(2)}) %collective-permute-start.7) | collective-permute-done | bytes 147488 | tf_op jit(solution)/shard_map/ppermute | solution.py:942
  47.6 0.3 fold_plane.1
  47.9 1.5 %collective-permute-start.10 = (bf16[104,384]{1,0:T(8,128)(2,1)S(1)}, bf16[104,384]{1,0:T(8,128)(2,1)S(1)}, u32[]{:S(2)}, u32[]{:S(2)}) collective-permute-start(bf16[104,384]{1,0:T(8,128)(2,1)S(1)} %get-tuple-element.143), channel_id=1, source_target_pairs={{0,8},{2,10},{4,12},{6,14},{8,0},{10,2},{12,4},{14,6},{16,24},{18,... | collective-permute-start | bytes 239624 | tf_op jit(solution)/shard_map/ppermute | solution.py:942
  49.4 2.3 %collective-permute-start.11 = (bf16[104,384]{1,0:T(8,128)(2,1)S(1)}, bf16[104,384]{1,0:T(8,128)(2,1)S(1)}, u32[]{:S(2)}, u32[]{:S(2)}) collective-permute-start(bf16[104,384]{1,0:T(8,128)(2,1)S(1)} %get-tuple-element.144), channel_id=1, source_target_pairs={{0,16},{2,18},{4,20},{6,22},{8,24},{10,26},{12,28},{14,30},{16,0},... | collective-permute-start | bytes 239624 | tf_op jit(solution)/shard_map/ppermute | solution.py:942
  51.7 0.0 collective-permute-done.13.refs_1_
  51.7 1.9 %collective-permute-start.12 = (bf16[104,384]{1,0:T(8,128)(2,1)S(1)}, bf16[104,384]{1,0:T(8,128)(2,1)S(1)}, u32[]{:S(2)}, u32[]{:S(2)}) collective-permute-start(bf16[104,384]{1,0:T(8,128)(2,1)S(1)} %get-tuple-element.145), channel_id=1, source_target_pairs={{0,24},{2,26},{4,28},{6,30},{8,16},{10,18},{12,20},{14,22},{16,8},... | collective-permute-start | bytes 239624 | tf_op jit(solution)/shard_map/ppermute | solution.py:942
  53.6 0.3 fold_qkv_plane.1
  53.9 0.5 collective-permute-start.16
  54.4 2.3 %collective-permute-start.17 = (bf16[104,384]{1,0:T(8,128)(2,1)S(1)}, bf16[104,384]{1,0:T(8,128)(2,1)S(1)}, u32[]{:S(2)}, u32[]{:S(2)}) collective-permute-start(bf16[104,384]{1,0:T(8,128)(2,1)S(1)} %get-tuple-element.156), channel_id=1, source_target_pairs={{0,16},{2,18},{4,20},{6,22},{8,24},{10,26},{12,28},{14,30},{16,0},... | collective-permute-start | bytes 239624 | tf_op jit(solution)/shard_map/ppermute | solution.py:942
  56.7 0.0 collective-permute-done.10.one_ref
  56.7 1.6 %collective-permute-start.18 = (bf16[104,384]{1,0:T(8,128)(2,1)S(1)}, bf16[104,384]{1,0:T(8,128)(2,1)S(1)}, u32[]{:S(2)}, u32[]{:S(2)}) collective-permute-start(bf16[104,384]{1,0:T(8,128)(2,1)S(1)} %get-tuple-element.157), channel_id=1, source_target_pairs={{0,24},{2,26},{4,28},{6,30},{8,16},{10,18},{12,20},{14,22},{16,8},... | collective-permute-start | bytes 239624 | tf_op jit(solution)/shard_map/ppermute | solution.py:942
  58.4 0.0 collective-permute-done.11.two_ref
  58.4 0.0 collective-permute-done.12.three_ref
  58.4 1.8 %finish_line.1 = (bf16[4,128,384]{2,1,0:T(8,128)(2,1)}, bf16[4,128,384]{2,1,0:T(8,128)(2,1)}, f32[24,768]{1,0:T(8,128)}, f32[96,192]{1,0:T(8,128)}, bf16[24,192]{1,0:T(8,128)(2,1)S(1)}, /*index=5*/s32[1,192]{1,0:T(1,128)S(1)}) custom-call(f32[96,384]{1,0:T(8,128)S(1)} %get-tuple-element.141.own_ref, bf16[8,384]{1,0:T(8,128)(2,1)S(1)} %get-tuple-element.142.own_small_ref, ...), custom_call_target="tpu_custom_call" | custom-call | flops 1 | bytes 1 | tf_op jit(solution)/shard_map/finish_line/pallas_call | solution.py:925
  60.2 0.1 collective-permute-done.16.one_ref
  60.3 3.0 %collective-permute-done.17.two_ref = bf16[104,384]{1,0:T(8,128)(2,1)S(1)} collective-permute-done((bf16[104,384]{1,0:T(8,128)(2,1)S(1)}, bf16[104,384]{1,0:T(8,128)(2,1)S(1)}, u32[]{:S(2)}, u32[]{:S(2)}) %collective-permute-start.17) | collective-permute-done | bytes 79904 | tf_op jit(solution)/shard_map/ppermute | solution.py:942
  63.3 1.1 %late_groups.1 = (bf16[4,48,384]{2,1,0:T(8,128)(2,1)S(1)}, f32[8,384]{1,0:T(8,128)S(1)}, f32[8,384]{1,0:T(8,128)S(1)}, f32[384]{0:T(512)}, f32[1536]{0:T(1024)}, /*index=5*/f32[384]{0:T(512)}, f32[2,384]{1,0:T(2,128)}) custom-call(bf16[56,384]{1,0:T(8,128)(2,1)S(1)} %get-tuple-element.154.own_small_ref, ...), custom_call_target="tpu_custom_call" | custom-call | flops 1 | bytes 1 | tf_op jit(solution)/shard_map/late_groups/pallas_call | solution.py:925
  64.4 0.9 %rest_sums.1 = (f32[24,192]{1,0:T(8,128)}, f32[24,576]{1,0:T(8,128)}, f32[24,1152]{1,0:T(8,128)}) custom-call(f32[48,384]{1,0:T(8,128)S(1)} %get-tuple-element.162.own_ref, bf16[104,384]{1,0:T(8,128)(2,1)S(1)} %collective-permute-done.16.one_ref, bf16[104,384]{1,0:T(8,128)(2,1)S(1)} %collective-permute-done.17.two_ref, ...), custom_call_target="tpu_custom_call" | custom-call | flops 1 | bytes 1 | tf_op jit(solution)/shard_map/rest_sums/pallas_call | solution.py:925
  65.3 0.3 collective-permute-done.19.recv_ref
  65.6 0.7 %final_groups.1 = (f32[2,192]{1,0:T(2,128)}, f32[2304]{0:T(1024)}) custom-call(f32[8,384]{1,0:T(8,128)S(1)} %get-tuple-element.159.own_ref, f32[8,384]{1,0:T(8,128)S(1)} %collective-permute-done.19.recv_ref, bf16[2,384]{1,0:T(2,128)(2,1)S(1)} %copy-done), custom_call_target="tpu_custom_call" | custom-call | flops 1 | bytes 1 | tf_op jit(solution)/shard_map/final_groups/pallas_call | solution.py:925
  (10 shorter events, 0.0 us)
Async XLA Ops:
  0.6 12.8 %collective-permute-start = (bf16[4,128,384]{2,1,0:T(8,128)(2,1)}, bf16[4,128,384]{2,1,0:T(8,128)(2,1)S(1)}, u32[]{:S(2)}, u32[]{:S(2)}) collective-permute-start(bf16[4,128,384]{2,1,0:T(8,128)(2,1)} %tokens_hbm.1), channel_id=1, source_target_pairs={{0,1},{1,0},{2,3},{3,2},{4,5},{5,4},{6,7},{7,6},{8,9},{9,8},{10,11... | collective-permute-start | bytes 1179656 | tf_op jit(solution)/shard_map/ppermute | solution.py:895
  1.2 14.2 %collective-permute-start.1 = (bf16[4,128,384]{2,1,0:T(8,128)(2,1)}, bf16[4,128,384]{2,1,0:T(8,128)(2,1)S(1)}, u32[]{:S(2)}, u32[]{:S(2)}) collective-permute-start(bf16[4,128,384]{2,1,0:T(8,128)(2,1)} %cot_hbm.1), channel_id=1, source_target_pairs={{0,1},{1,0},{2,3},{3,2},{4,5},{5,4},{6,7},{7,6},{8,9},{9,8},{10,11... | collective-permute-start | bytes 1179656 | tf_op jit(solution)/shard_map/ppermute | solution.py:895
  2.5 12.8 %all-to-all-start = ((bf16[16,2,384]{2,1,0:T(2,128)(2,1)}), bf16[16,2,384]{2,1,0:T(2,128)(2,1)S(1)}, u32[]{:S(2)}, u32[]{:S(2)}) async-start(bf16[16,2,384]{2,1,0:T(2,128)(2,1)} %broadcast_in_dim.2), calls=%async_computation | async-start | bytes 49152 | tf_op jit(solution)/shard_map/all_to_all | solution.py:1064
  25.0 3.6 %collective-permute-start.2 = (bf16[1536,384]{1,0:T(8,128)(2,1)S(1)}, bf16[1536,384]{1,0:T(8,128)(2,1)S(1)}, u32[]{:S(2)}, u32[]{:S(2)}) collective-permute-start(bf16[1536,384]{1,0:T(8,128)(2,1)S(1)} %get-tuple-element.103), channel_id=1, source_target_pairs={{0,1},{1,0},{2,3},{3,2},{4,5},{5,4},{6,7},{7,6},{8,9},{9,8},{10,11... | collective-permute-start | bytes 3538952 | tf_op jit(solution)/shard_map/ppermute | solution.py:895
  28.1 3.8 %collective-permute-start.5 = (bf16[464,384]{1,0:T(8,128)(2,1)S(1)}, bf16[464,384]{1,0:T(8,128)(2,1)S(1)}, u32[]{:S(2)}, u32[]{:S(2)}) collective-permute-start(bf16[464,384]{1,0:T(8,128)(2,1)S(1)} %get-tuple-element.130), channel_id=1, source_target_pairs={{0,1},{1,0},{2,3},{3,2},{4,5},{5,4},{6,7},{7,6},{8,9},{9,8},{10,11... | collective-permute-start | bytes 1069064 | tf_op jit(solution)/shard_map/ppermute | solution.py:895
  28.9 10.2 %collective-permute-start.3 = (bf16[392,384]{1,0:T(8,128)(2,1)S(1)}, bf16[392,384]{1,0:T(8,128)(2,1)S(1)}, u32[]{:S(2)}, u32[]{:S(2)}) collective-permute-start(bf16[392,384]{1,0:T(8,128)(2,1)S(1)} %get-tuple-element.107.after_ref), channel_id=1, source_target_pairs={{0,2},{2,0},{4,6},{6,4},{8,10},{10,8},{12,14},{14,12},{16,18},{18,... | collective-permute-start | bytes 903176 | tf_op jit(solution)/shard_map/ppermute | solution.py:942
  30.4 8.7 %collective-permute-start.4 = (bf16[384,384]{1,0:T(8,128)(2,1)S(1)}, bf16[384,384]{1,0:T(8,128)(2,1)S(1)}, u32[]{:S(2)}, u32[]{:S(2)}) collective-permute-start(bf16[384,384]{1,0:T(8,128)(2,1)S(1)} %get-tuple-element.108.after_too_ref), channel_id=1, source_target_pairs={{0,4},{2,6},{4,0},{6,2},{8,12},{10,14},{12,8},{14,10},{16,20},{18,... | collective-permute-start | bytes 884744 | tf_op jit(solution)/shard_map/ppermute | solution.py:942
  37.7 3.6 %collective-permute-start.9 = (bf16[424,384]{1,0:T(8,128)(2,1)S(1)}, bf16[424,384]{1,0:T(8,128)(2,1)S(1)}, u32[]{:S(2)}, u32[]{:S(2)}) collective-permute-start(bf16[424,384]{1,0:T(8,128)(2,1)S(1)} %get-tuple-element.137), channel_id=1, source_target_pairs={{0,1},{1,0},{2,3},{3,2},{4,5},{5,4},{6,7},{7,6},{8,9},{9,8},{10,11... | collective-permute-start | bytes 976904 | tf_op jit(solution)/shard_map/ppermute | solution.py:895
  37.8 3.5 %collective-permute-start.8 = (bf16[416,384]{1,0:T(8,128)(2,1)S(1)}, bf16[416,384]{1,0:T(8,128)(2,1)S(1)}, u32[]{:S(2)}, u32[]{:S(2)}) collective-permute-start(bf16[416,384]{1,0:T(8,128)(2,1)S(1)} %get-tuple-element.136), channel_id=1, source_target_pairs={{0,1},{1,0},{2,3},{3,2},{4,5},{5,4},{6,7},{7,6},{8,9},{9,8},{10,11... | collective-permute-start | bytes 958472 | tf_op jit(solution)/shard_map/ppermute | solution.py:895
  39.2 8.3 %collective-permute-start.6 = (bf16[208,384]{1,0:T(8,128)(2,1)S(1)}, bf16[208,384]{1,0:T(8,128)(2,1)S(1)}, u32[]{:S(2)}, u32[]{:S(2)}) collective-permute-start(bf16[208,384]{1,0:T(8,128)(2,1)S(1)} %get-tuple-element.133.refs_0_), channel_id=1, source_target_pairs={{0,4},{2,6},{4,0},{6,2},{8,12},{10,14},{12,8},{14,10},{16,20},{18,... | collective-permute-start | bytes 479240 | tf_op jit(solution)/shard_map/ppermute | solution.py:942
  40.8 6.8 %collective-permute-start.7 = (bf16[192,384]{1,0:T(8,128)(2,1)S(1)}, bf16[192,384]{1,0:T(8,128)(2,1)S(1)}, u32[]{:S(2)}, u32[]{:S(2)}) collective-permute-start(bf16[192,384]{1,0:T(8,128)(2,1)S(1)} %get-tuple-element.134), channel_id=1, source_target_pairs={{0,2},{2,0},{4,6},{6,4},{8,10},{10,8},{12,14},{14,12},{16,18},{18,... | collective-permute-start | bytes 442376 | tf_op jit(solution)/shard_map/ppermute | solution.py:942
  41.6 10.1 %collective-permute-start.13 = (bf16[216,384]{1,0:T(8,128)(2,1)S(1)}, bf16[216,384]{1,0:T(8,128)(2,1)S(1)}, u32[]{:S(2)}, u32[]{:S(2)}) collective-permute-start(bf16[216,384]{1,0:T(8,128)(2,1)S(1)} %get-tuple-element.152), channel_id=1, source_target_pairs={{0,2},{2,0},{4,6},{6,4},{8,10},{10,8},{12,14},{14,12},{16,18},{18,... | collective-permute-start | bytes 497672 | tf_op jit(solution)/shard_map/ppermute | solution.py:942
  43.1 10.5 %collective-permute-start.14 = (bf16[216,384]{1,0:T(8,128)(2,1)S(1)}, bf16[216,384]{1,0:T(8,128)(2,1)S(1)}, u32[]{:S(2)}, u32[]{:S(2)}) collective-permute-start(bf16[216,384]{1,0:T(8,128)(2,1)S(1)} %get-tuple-element.153), channel_id=1, source_target_pairs={{0,4},{2,6},{4,0},{6,2},{8,12},{10,14},{12,8},{14,10},{16,20},{18,... | collective-permute-start | bytes 497672 | tf_op jit(solution)/shard_map/ppermute | solution.py:942
  43.7 10.0 %collective-permute-start.15 = (bf16[216,384]{1,0:T(8,128)(2,1)S(1)}, bf16[216,384]{1,0:T(8,128)(2,1)S(1)}, u32[]{:S(2)}, u32[]{:S(2)}) collective-permute-start(bf16[216,384]{1,0:T(8,128)(2,1)S(1)} %get-tuple-element.140.refs_3_), channel_id=1, source_target_pairs={{0,6},{2,4},{4,2},{6,0},{8,14},{10,12},{12,10},{14,8},{16,22},{18,... | collective-permute-start | bytes 497672 | tf_op jit(solution)/shard_map/ppermute | solution.py:942
  47.9 8.9 %collective-permute-start.10 = (bf16[104,384]{1,0:T(8,128)(2,1)S(1)}, bf16[104,384]{1,0:T(8,128)(2,1)S(1)}, u32[]{:S(2)}, u32[]{:S(2)}) collective-permute-start(bf16[104,384]{1,0:T(8,128)(2,1)S(1)} %get-tuple-element.143), channel_id=1, source_target_pairs={{0,8},{2,10},{4,12},{6,14},{8,0},{10,2},{12,4},{14,6},{16,24},{18,... | collective-permute-start | bytes 239624 | tf_op jit(solution)/shard_map/ppermute | solution.py:942
  49.4 9.0 %collective-permute-start.11 = (bf16[104,384]{1,0:T(8,128)(2,1)S(1)}, bf16[104,384]{1,0:T(8,128)(2,1)S(1)}, u32[]{:S(2)}, u32[]{:S(2)}) collective-permute-start(bf16[104,384]{1,0:T(8,128)(2,1)S(1)} %get-tuple-element.144), channel_id=1, source_target_pairs={{0,16},{2,18},{4,20},{6,22},{8,24},{10,26},{12,28},{14,30},{16,0},... | collective-permute-start | bytes 239624 | tf_op jit(solution)/shard_map/ppermute | solution.py:942
  51.7 6.7 %collective-permute-start.12 = (bf16[104,384]{1,0:T(8,128)(2,1)S(1)}, bf16[104,384]{1,0:T(8,128)(2,1)S(1)}, u32[]{:S(2)}, u32[]{:S(2)}) collective-permute-start(bf16[104,384]{1,0:T(8,128)(2,1)S(1)} %get-tuple-element.145), channel_id=1, source_target_pairs={{0,24},{2,26},{4,28},{6,30},{8,16},{10,18},{12,20},{14,22},{16,8},... | collective-permute-start | bytes 239624 | tf_op jit(solution)/shard_map/ppermute | solution.py:942
  53.9 6.3 %collective-permute-start.16 = (bf16[104,384]{1,0:T(8,128)(2,1)S(1)}, bf16[104,384]{1,0:T(8,128)(2,1)S(1)}, u32[]{:S(2)}, u32[]{:S(2)}) collective-permute-start(bf16[104,384]{1,0:T(8,128)(2,1)S(1)} %get-tuple-element.155), channel_id=1, source_target_pairs={{0,8},{2,10},{4,12},{6,14},{8,0},{10,2},{12,4},{14,6},{16,24},{18,... | collective-permute-start | bytes 239624 | tf_op jit(solution)/shard_map/ppermute | solution.py:942
  54.4 8.8 %collective-permute-start.17 = (bf16[104,384]{1,0:T(8,128)(2,1)S(1)}, bf16[104,384]{1,0:T(8,128)(2,1)S(1)}, u32[]{:S(2)}, u32[]{:S(2)}) collective-permute-start(bf16[104,384]{1,0:T(8,128)(2,1)S(1)} %get-tuple-element.156), channel_id=1, source_target_pairs={{0,16},{2,18},{4,20},{6,22},{8,24},{10,26},{12,28},{14,30},{16,0},... | collective-permute-start | bytes 239624 | tf_op jit(solution)/shard_map/ppermute | solution.py:942
  56.7 6.5 %collective-permute-start.18 = (bf16[104,384]{1,0:T(8,128)(2,1)S(1)}, bf16[104,384]{1,0:T(8,128)(2,1)S(1)}, u32[]{:S(2)}, u32[]{:S(2)}) collective-permute-start(bf16[104,384]{1,0:T(8,128)(2,1)S(1)} %get-tuple-element.157), channel_id=1, source_target_pairs={{0,24},{2,26},{4,28},{6,30},{8,16},{10,18},{12,20},{14,22},{16,8},... | collective-permute-start | bytes 239624 | tf_op jit(solution)/shard_map/ppermute | solution.py:942
  63.3 2.3 %copy-start = (bf16[2,384]{1,0:T(2,128)(2,1)S(1)}, bf16[2,384]{1,0:T(2,128)(2,1)}, u32[]{:S(2)}) copy-start(bf16[2,384]{1,0:T(2,128)(2,1)} %own_cond_ref.1) | copy-start | bytes 4612
  64.4 1.2 %collective-permute-start.19 = (f32[8,384]{1,0:T(8,128)S(1)}, f32[8,384]{1,0:T(8,128)S(1)}, u32[]{:S(2)}, u32[]{:S(2)}) collective-permute-start(f32[8,384]{1,0:T(8,128)S(1)} %get-tuple-element.160.after_ref), channel_id=1, source_target_pairs={{0,1},{1,0},{2,3},{3,2},{4,5},{5,4},{6,7},{7,6},{8,9},{9,8},{10,11... | collective-permute-start | bytes 36872 | tf_op jit(solution)/shard_map/ppermute | solution.py:895

commit v5 on v4

--- a/solution.py
+++ b/solution.py
@@ -16,6 +16,8 @@
 GROUPS_PER_RANK = 2
 GENERAL = False
 PIECE_ROWS = 288
+PLANE_STEPS = (3, 1, 2)
+LINE_STEPS = (2, 3, 1)
 F32 = jnp.float32
 LOW = jnp.bfloat16
 
@@ -621,7 +623,7 @@
     total_ref[:cut, :] = keep_ref[:cut, :] + recv_ref[:cut, :].astype(F32)
     total_ref[cut : width + half, :] = keep_ref[cut:, :] + other_ref[:start, :].astype(F32)
     total_ref[width + half :, :] = keep_out_ref[...] + recv_out_ref[:half, :].astype(F32)
-    for step, target in enumerate(refs[-5:-1]):
+    for step, target in zip((0,) + PLANE_STEPS, refs[-5:-1]):
         who = (lax.axis_index("dp") & 3) ^ step
         for z in range(8):
             begin = piece * (4 * z + who)
@@ -657,7 +659,7 @@
     ids = [group_ref[q, 0:1] for q in range(4)] + [jnp.zeros((4, width), F32)]
     small = jnp.concatenate(ids, axis=0).astype(LOW)
     rest_small_ref[...] = small
-    for step, target in enumerate((rest_ref,) + tuple(sends)):
+    for step, target in zip((0,) + LINE_STEPS, (rest_ref,) + tuple(sends)):
         who = (lax.axis_index("dp") >> 2) ^ step
         rows = pl.ds(pl.multiple_of(2 * piece * who, 8), 2 * piece)
         target[: 2 * piece, :] = total_ref[rows, :].astype(target.dtype)
@@ -679,13 +681,13 @@
     piece = width // 16
     half = width // 2
     total_ref[...] = summed(parts, slice(0, 8 * piece))
-    for step, part in enumerate(parts):
+    for step, part in zip((0,) + PLANE_STEPS, parts):
         late_ref[(lax.axis_index("dp") & 3) ^ step] = part[8 * piece :, :].astype(F32)
     rows = [late_ref[q, :12] for q in range(4)]
     rows.append(late_ref[0, 12:20] + late_ref[1, 12:20] + late_ref[2, 12:20] + late_ref[3, 12:20])
     small = jnp.concatenate(rows, axis=0).astype(LOW)
     rest_small_ref[...] = small
-    for step, target in enumerate((rest_ref,) + tuple(sends)):
+    for step, target in zip((0,) + LINE_STEPS, (rest_ref,) + tuple(sends)):
         who = (lax.axis_index("dp") >> 2) ^ step
 
         def side(start):
@@ -771,7 +773,7 @@
     down_ref[...] = jnp.concatenate([down[:, :half], down[:, half:]], axis=0)
     line = lax.axis_index("dp") >> 2
     smalls = (own_small_ref[...],) + tuple(part[4 * piece :, :] for part in parts[1:])
-    for step, small in enumerate(smalls):
+    for step, small in zip((0,) + LINE_STEPS, smalls):
         stack_ref[line ^ step] = small[:, :LANES].astype(F32)
     stack = stack_ref[...].reshape(32, LANES).astype(LOW)
     count = 192
@@ -812,7 +814,7 @@
     smalls = (own_small_ref[...],) + tuple(
         part[2 * piece :, :] for part in (one_ref, two_ref, three_ref)
     )
-    for step, small in enumerate(smalls):
+    for step, small in zip((0,) + LINE_STEPS, smalls):
         stack_out_ref[line ^ step] = small[:48]
         bias_ref[line ^ step] = small[48:].astype(F32)
     stack = stack_out_ref[...].reshape(192, width)
@@ -1332,7 +1334,7 @@
         small_one,
         cross_up,
     )
-    near_qkv = [rank_swap(item, step + 1, 16) for step, item in enumerate(sent_qkv)]
+    near_qkv = [rank_swap(item, step, 16) for step, item in zip(PLANE_STEPS, sent_qkv)]
     line_rows = 4 * piece + 8
     rest, rest_ids, *lines = call(
         fold_kernel,
@@ -1346,7 +1348,7 @@
         near_down,
         sent_qkv[2],
     )
-    lines = [rank_swap(item, 4 * (step + 1), 16) for step, item in enumerate(lines)]
+    lines = [rank_swap(item, 4 * step, 16) for step, item in zip(LINE_STEPS, lines)]
     line_rows = 2 * piece + 56
     rest_qkv, rest_small, *lines_qkv = call(
         fold_qkv_kernel,
@@ -1358,7 +1360,7 @@
         own_qkv,
         *near_qkv,
     )
-    lines_qkv = [rank_swap(item, 4 * (step + 1), 16) for step, item in enumerate(lines_qkv)]
+    lines_qkv = [rank_swap(item, 4 * step, 16) for step, item in zip(LINE_STEPS, lines_qkv)]
     output, grad_tokens, up_sum, down_sum, silu_rows, all_ids = call(
         finish_kernel,
         "finish_line",

time: 66.5 us -> 65.7 us (0.988)
  starting transfers between devices: 30.9 us -> 29 us
  waiting for transfers between devices: 6.75 us -> 7.82 us
    ppermute x13, starting transfers between devices: 18.8 us -> 16.9 us  [rank_swap(): lax.ppermute(values, 'dp', [(rank, rank ^ step) for rank in range(count)])]
    ppermute x13, waiting for transfers between devices: 6.32 us -> 7.39 us  [rank_swap(): lax.ppermute(values, 'dp', [(rank, rank ^ step) for rank in range(count)])]
  transfers between devices with their start and end apart: 21 -> 21, of which waited for: 6 -> 7; matrix products, arithmetic and copies ran while one was open for 2% -> 2% of each run, Pallas kernels for 22% -> 22%
where the time goes in v5:
time: 65.7 us; the launch traced here: 65.4 us
  starting transfers between devices  29 us (44%)
  Pallas kernels  25.9 us (39%)
  waiting for transfers between devices  7.82 us (12%)
  between operations  1.41 us (2%)
  local copies, waits for them, and re-layouts  1.31 us (2%)
    pallas_call x13, Pallas kernels, call(): pl.pallas_call(kernel, out_shape=tuple((pinned.get(kind, jax.ShapeDtypeSt...  25.9 us
    ppermute x13, starting transfers between devices, rank_swap(): lax.ppermute(values, 'dp', [(rank, rank ^ step) for rank in range(count)])  16.9 us
    all_to_all x1, starting transfers between devices, body(): lax.all_to_all(jnp.broadcast_to(cond[None], (dp_count,) + cond.shape), 'd...  10.3 us
    ppermute x13, waiting for transfers between devices, rank_swap(): lax.ppermute(values, 'dp', [(rank, rank ^ step) for rank in range(count)])  7.39 us
    ppermute x7, starting transfers between devices, swap_cores(): return lax.ppermute(values, 'seq', CORE_SWAP)  1.79 us
  transfers between devices with their start and end apart: 21, of which 7 were waited for; matrix products, arithmetic and copies ran while one was open for 2% of the time, Pallas kernels for 22%

profile of v5, /device:TPU:0, one launch (start us, length us, event | category | flops | bytes accessed | tf_op | source)
XLA Modules:
  0.0 65.4 jit_solution(7532788437666683689)
XLA Ops:
  0.6 0.5 collective-permute-start
  1.2 0.1 collective-permute-start.1
  1.2 1.3 %broadcast_in_dim.2 = bf16[16,2,384]{2,1,0:T(2,128)(2,1)} broadcast(bf16[2,384]{1,0:T(2,128)(2,1)} %own_cond_ref.1), dimensions={1,2} | broadcast | bytes 26112 | tf_op jit(solution)/shard_map/broadcast_in_dim | solution.py:1067
  2.5 10.3 %all-to-all-start = ((bf16[16,2,384]{2,1,0:T(2,128)(2,1)}), bf16[16,2,384]{2,1,0:T(2,128)(2,1)S(1)}, u32[]{:S(2)}, u32[]{:S(2)}) async-start(bf16[16,2,384]{2,1,0:T(2,128)(2,1)} %broadcast_in_dim.2), calls=%async_computation | async-start | bytes 49152 | tf_op jit(solution)/shard_map/all_to_all | solution.py:1066
  13.5 0.0 collective-permute-done.tokens_far_ref
  13.5 1.7 %load.1 = (bf16[2,256,384]{2,1,0:T(8,128)(2,1)S(1)}, f32[8,256]{1,0:T(8,128)S(1)}, bf16[8,128]{1,0:T(8,128)(2,1)S(1)}, f32[8,384]{1,0:T(8,128)S(1)}, f32[1,1152]...) custom-call(bf16[4,128,384]{2,1,0:T(8,128)(2,1)} %tokens_hbm.1, ...), custom_call_target="tpu_custom_call" | custom-call | flops 1 | bytes 1 | tf_op jit(solution)/shard_map/load/pallas_call | solution.py:927
  15.2 0.1 all-to-all-done.cond_ref
  15.3 9.7 %forward_and_ffn_grads.1 = (bf16[512,1152]{1,0:T(8,128)(2,1)S(1)}, bf16[512,384]{1,0:T(8,128)(2,1)S(1)}, f32[512,384]{1,0:T(8,128)S(1)}, f32[512,128]{1,0:T(8,12...) custom-call(bf16[16,2,384]{2,1,0:T(2,128)(2,1)S(1)} %all-to-all-done, ...), custom_call_target="tpu_custom_call" | custom-call | flops 1 | bytes 1 | tf_op jit(solution)/shard_map/forward_and_ffn_grads/pallas_call | solution.py:927
  25.0 0.1 collective-permute-start.2
  25.1 3.0 %norm_back.1 = (bf16[2,256,384]{2,1,0:T(8,128)(2,1)S(1)}, bf16[512,384]{1,0:T(8,128)(2,1)S(1)}, f32[512,384]{1,0:T(8,128)S(1)}, f32[192,384]{1,0:T(8,128)S(1)}, ...) custom-call(bf16[8,2304]{1,0:T(8,128)(2,1)S(1)} %get-tuple-element.115.mod_ref, ...), custom_call_target="tpu_custom_call" | custom-call | flops 1 | bytes 1 | tf_op jit(solution)/shard_map/norm_back/pallas_call | solution.py:927
  28.1 0.6 collective-permute-start.5
  28.7 0.0 collective-permute-done.2.recv_ref
  28.7 0.2 split_plane.1
  28.9 1.5 %collective-permute-start.3 = (bf16[392,384]{1,0:T(8,128)(2,1)S(1)}, bf16[392,384]{1,0:T(8,128)(2,1)S(1)}, u32[]{:S(2)}, u32[]{:S(2)}) collective-permute-start(bf16[392,384]{1,0:T(8,128)(2,1)S(1)} %get-tuple-element.107.after_ref), channel_id=1, source_target_pairs={{0,2},{2,0},{4,6},{6,4},{8,10},{10,8},{12,14},{14,12},{16,18},{18,... | collective-permute-start | bytes 903176 | tf_op jit(solution)/shard_map/ppermute | solution.py:944
  30.4 1.5 %collective-permute-start.4 = (bf16[384,384]{1,0:T(8,128)(2,1)S(1)}, bf16[384,384]{1,0:T(8,128)(2,1)S(1)}, u32[]{:S(2)}, u32[]{:S(2)}) collective-permute-start(bf16[384,384]{1,0:T(8,128)(2,1)S(1)} %get-tuple-element.108.after_too_ref), channel_id=1, source_target_pairs={{0,4},{2,6},{4,0},{6,2},{8,12},{10,14},{12,8},{14,10},{16,20},{18,... | collective-permute-start | bytes 884744 | tf_op jit(solution)/shard_map/ppermute | solution.py:944
  31.9 5.8 %attention_back.1 = (bf16[2,256,384]{2,1,0:T(8,128)(2,1)S(1)}, f32[576,384]{1,0:T(8,128)S(1)}, bf16[416,384]{1,0:T(8,128)(2,1)S(1)}, bf16[424,384]{1,0:T(8,128)(2,1)S(1)}, f32[8,384]{1,0:T(8,128)S(1)}) custom-call(f32[512,384]{1,0:T(8,128)S(1)} %get-tuple-element.109.normed_ref, f32[512,128]{1,0:T(8,128)S(1)} %get-tuple-element.110.inverse_ref, ...), custom_call_target="tpu_custom_call" | custom-call | flops 1 | bytes 1 | tf_op jit(solution)/shard_map/attention_back/pallas_call | solution.py:927
  37.7 0.1 collective-permute-start.9
  37.8 0.5 collective-permute-start.8
  38.3 0.8 %collective-permute-done.4.recv_down_ref = bf16[384,384]{1,0:T(8,128)(2,1)S(1)} collective-permute-done((bf16[384,384]{1,0:T(8,128)(2,1)S(1)}, bf16[384,384]{1,0:T(8,128)(2,1)S(1)}, u32[]{:S(2)}, u32[]{:S(2)}) %collective-permute-start.4) | collective-permute-done | bytes 294944 | tf_op jit(solution)/shard_map/ppermute | solution.py:944
  39.1 0.1 cross_plane.1
  39.2 1.5 %collective-permute-start.6 = (bf16[208,384]{1,0:T(8,128)(2,1)S(1)}, bf16[208,384]{1,0:T(8,128)(2,1)S(1)}, u32[]{:S(2)}, u32[]{:S(2)}) collective-permute-start(bf16[208,384]{1,0:T(8,128)(2,1)S(1)} %get-tuple-element.133.refs_0_), channel_id=1, source_target_pairs={{0,4},{2,6},{4,0},{6,2},{8,12},{10,14},{12,8},{14,10},{16,20},{18,... | collective-permute-start | bytes 479240 | tf_op jit(solution)/shard_map/ppermute | solution.py:944
  40.8 0.5 collective-permute-start.7
  41.3 0.0 collective-permute-done.8.recv_ref.recv_two_ref
  41.3 0.0 collective-permute-done.9.other_ref.recv_other_ref
  41.3 0.2 split_qkv_plane.1
  41.6 1.6 %collective-permute-start.13 = (bf16[216,384]{1,0:T(8,128)(2,1)S(1)}, bf16[216,384]{1,0:T(8,128)(2,1)S(1)}, u32[]{:S(2)}, u32[]{:S(2)}) collective-permute-start(bf16[216,384]{1,0:T(8,128)(2,1)S(1)} %get-tuple-element.152), channel_id=1, source_target_pairs={{0,6},{2,4},{4,2},{6,0},{8,14},{10,12},{12,10},{14,8},{16,22},{18,... | collective-permute-start | bytes 497672 | tf_op jit(solution)/shard_map/ppermute | solution.py:944
  43.1 0.6 collective-permute-start.14
  43.7 1.4 %collective-permute-start.15 = (bf16[216,384]{1,0:T(8,128)(2,1)S(1)}, bf16[216,384]{1,0:T(8,128)(2,1)S(1)}, u32[]{:S(2)}, u32[]{:S(2)}) collective-permute-start(bf16[216,384]{1,0:T(8,128)(2,1)S(1)} %get-tuple-element.140.refs_3_), channel_id=1, source_target_pairs={{0,4},{2,6},{4,0},{6,2},{8,12},{10,14},{12,8},{14,10},{16,20},{18,... | collective-permute-start | bytes 497672 | tf_op jit(solution)/shard_map/ppermute | solution.py:944
  45.1 2.4 %collective-permute-done.7.refs_2_ = bf16[192,384]{1,0:T(8,128)(2,1)S(1)} collective-permute-done((bf16[192,384]{1,0:T(8,128)(2,1)S(1)}, bf16[192,384]{1,0:T(8,128)(2,1)S(1)}, u32[]{:S(2)}, u32[]{:S(2)}) %collective-permute-start.7) | collective-permute-done | bytes 147488 | tf_op jit(solution)/shard_map/ppermute | solution.py:944
  47.6 0.3 fold_plane.1
  47.9 2.4 %collective-permute-start.10 = (bf16[104,384]{1,0:T(8,128)(2,1)S(1)}, bf16[104,384]{1,0:T(8,128)(2,1)S(1)}, u32[]{:S(2)}, u32[]{:S(2)}) collective-permute-start(bf16[104,384]{1,0:T(8,128)(2,1)S(1)} %get-tuple-element.143), channel_id=1, source_target_pairs={{0,16},{2,18},{4,20},{6,22},{8,24},{10,26},{12,28},{14,30},{16,0},... | collective-permute-start | bytes 239624 | tf_op jit(solution)/shard_map/ppermute | solution.py:944
  50.2 1.5 %collective-permute-start.11 = (bf16[104,384]{1,0:T(8,128)(2,1)S(1)}, bf16[104,384]{1,0:T(8,128)(2,1)S(1)}, u32[]{:S(2)}, u32[]{:S(2)}) collective-permute-start(bf16[104,384]{1,0:T(8,128)(2,1)S(1)} %get-tuple-element.144), channel_id=1, source_target_pairs={{0,24},{2,26},{4,28},{6,30},{8,16},{10,18},{12,20},{14,22},{16,8},... | collective-permute-start | bytes 239624 | tf_op jit(solution)/shard_map/ppermute | solution.py:944
  51.7 0.0 collective-permute-done.13.refs_1_
  51.7 0.7 %collective-permute-start.12 = (bf16[104,384]{1,0:T(8,128)(2,1)S(1)}, bf16[104,384]{1,0:T(8,128)(2,1)S(1)}, u32[]{:S(2)}, u32[]{:S(2)}) collective-permute-start(bf16[104,384]{1,0:T(8,128)(2,1)S(1)} %get-tuple-element.145), channel_id=1, source_target_pairs={{0,8},{2,10},{4,12},{6,14},{8,0},{10,2},{12,4},{14,6},{16,24},{18,... | collective-permute-start | bytes 239624 | tf_op jit(solution)/shard_map/ppermute | solution.py:944
  52.4 0.0 collective-permute-done.14.refs_2_
  52.4 0.0 collective-permute-done.15.refs_3_
  52.4 0.3 fold_qkv_plane.1
  52.7 2.4 %collective-permute-start.16 = (bf16[104,384]{1,0:T(8,128)(2,1)S(1)}, bf16[104,384]{1,0:T(8,128)(2,1)S(1)}, u32[]{:S(2)}, u32[]{:S(2)}) collective-permute-start(bf16[104,384]{1,0:T(8,128)(2,1)S(1)} %get-tuple-element.155), channel_id=1, source_target_pairs={{0,16},{2,18},{4,20},{6,22},{8,24},{10,26},{12,28},{14,30},{16,0},... | collective-permute-start | bytes 239624 | tf_op jit(solution)/shard_map/ppermute | solution.py:944
  55.1 1.4 %collective-permute-start.17 = (bf16[104,384]{1,0:T(8,128)(2,1)S(1)}, bf16[104,384]{1,0:T(8,128)(2,1)S(1)}, u32[]{:S(2)}, u32[]{:S(2)}) collective-permute-start(bf16[104,384]{1,0:T(8,128)(2,1)S(1)} %get-tuple-element.156), channel_id=1, source_target_pairs={{0,24},{2,26},{4,28},{6,30},{8,16},{10,18},{12,20},{14,22},{16,8},... | collective-permute-start | bytes 239624 | tf_op jit(solution)/shard_map/ppermute | solution.py:944
  56.5 0.0 collective-permute-done.10.one_ref
  56.5 0.8 %collective-permute-done.11.two_ref = bf16[104,384]{1,0:T(8,128)(2,1)S(1)} collective-permute-done((bf16[104,384]{1,0:T(8,128)(2,1)S(1)}, bf16[104,384]{1,0:T(8,128)(2,1)S(1)}, u32[]{:S(2)}, u32[]{:S(2)}) %collective-permute-start.11) | collective-permute-done | bytes 79904 | tf_op jit(solution)/shard_map/ppermute | solution.py:944
  57.3 1.8 %finish_line.1 = (bf16[4,128,384]{2,1,0:T(8,128)(2,1)}, bf16[4,128,384]{2,1,0:T(8,128)(2,1)}, f32[24,768]{1,0:T(8,128)}, f32[96,192]{1,0:T(8,128)}, bf16[24,192]{1,0:T(8,128)(2,1)S(1)}, /*index=5*/s32[1,192]{1,0:T(1,128)S(1)}) custom-call(f32[96,384]{1,0:T(8,128)S(1)} %get-tuple-element.141.own_ref, bf16[8,384]{1,0:T(8,128)(2,1)S(1)} %get-tuple-element.142.own_small_ref, ...), custom_call_target="tpu_custom_call" | custom-call | flops 1 | bytes 1 | tf_op jit(solution)/shard_map/finish_line/pallas_call | solution.py:927
  59.1 3.1 %collective-permute-done.16.one_ref = bf16[104,384]{1,0:T(8,128)(2,1)S(1)} collective-permute-done((bf16[104,384]{1,0:T(8,128)(2,1)S(1)}, bf16[104,384]{1,0:T(8,128)(2,1)S(1)}, u32[]{:S(2)}, u32[]{:S(2)}) %collective-permute-start.16) | collective-permute-done | bytes 79904 | tf_op jit(solution)/shard_map/ppermute | solution.py:944
  62.2 0.3 collective-permute-done.18.three_ref
  62.5 1.1 %late_groups.1 = (bf16[4,48,384]{2,1,0:T(8,128)(2,1)S(1)}, f32[8,384]{1,0:T(8,128)S(1)}, f32[8,384]{1,0:T(8,128)S(1)}, f32[384]{0:T(512)}, f32[1536]{0:T(1024)}, /*index=5*/f32[384]{0:T(512)}, f32[2,384]{1,0:T(2,128)}) custom-call(bf16[56,384]{1,0:T(8,128)(2,1)S(1)} %get-tuple-element.154.own_small_ref, ...), custom_call_target="tpu_custom_call" | custom-call | flops 1 | bytes 1 | tf_op jit(solution)/shard_map/late_groups/pallas_call | solution.py:927
  63.6 0.9 %rest_sums.1 = (f32[24,192]{1,0:T(8,128)}, f32[24,576]{1,0:T(8,128)}, f32[24,1152]{1,0:T(8,128)}) custom-call(f32[48,384]{1,0:T(8,128)S(1)} %get-tuple-element.162.own_ref, bf16[104,384]{1,0:T(8,128)(2,1)S(1)} %collective-permute-done.16.one_ref, bf16[104,384]{1,0:T(8,128)(2,1)S(1)} %collective-permute-done.17.two_ref, ...), custom_call_target="tpu_custom_call" | custom-call | flops 1 | bytes 1 | tf_op jit(solution)/shard_map/rest_sums/pallas_call | solution.py:927
  64.5 0.3 collective-permute-done.19.recv_ref
  64.8 0.7 %final_groups.1 = (f32[2,192]{1,0:T(2,128)}, f32[2304]{0:T(1024)}) custom-call(f32[8,384]{1,0:T(8,128)S(1)} %get-tuple-element.159.own_ref, f32[8,384]{1,0:T(8,128)S(1)} %collective-permute-done.19.recv_ref, bf16[2,384]{1,0:T(2,128)(2,1)S(1)} %copy-done), custom_call_target="tpu_custom_call" | custom-call | flops 1 | bytes 1 | tf_op jit(solution)/shard_map/final_groups/pallas_call | solution.py:927
  (10 shorter events, 0.0 us)
Async XLA Ops:
  0.6 12.8 %collective-permute-start = (bf16[4,128,384]{2,1,0:T(8,128)(2,1)}, bf16[4,128,384]{2,1,0:T(8,128)(2,1)S(1)}, u32[]{:S(2)}, u32[]{:S(2)}) collective-permute-start(bf16[4,128,384]{2,1,0:T(8,128)(2,1)} %tokens_hbm.1), channel_id=1, source_target_pairs={{0,1},{1,0},{2,3},{3,2},{4,5},{5,4},{6,7},{7,6},{8,9},{9,8},{10,11... | collective-permute-start | bytes 1179656 | tf_op jit(solution)/shard_map/ppermute | solution.py:897
  1.2 14.2 %collective-permute-start.1 = (bf16[4,128,384]{2,1,0:T(8,128)(2,1)}, bf16[4,128,384]{2,1,0:T(8,128)(2,1)S(1)}, u32[]{:S(2)}, u32[]{:S(2)}) collective-permute-start(bf16[4,128,384]{2,1,0:T(8,128)(2,1)} %cot_hbm.1), channel_id=1, source_target_pairs={{0,1},{1,0},{2,3},{3,2},{4,5},{5,4},{6,7},{7,6},{8,9},{9,8},{10,11... | collective-permute-start | bytes 1179656 | tf_op jit(solution)/shard_map/ppermute | solution.py:897
  2.5 12.8 %all-to-all-start = ((bf16[16,2,384]{2,1,0:T(2,128)(2,1)}), bf16[16,2,384]{2,1,0:T(2,128)(2,1)S(1)}, u32[]{:S(2)}, u32[]{:S(2)}) async-start(bf16[16,2,384]{2,1,0:T(2,128)(2,1)} %broadcast_in_dim.2), calls=%async_computation | async-start | bytes 49152 | tf_op jit(solution)/shard_map/all_to_all | solution.py:1066
  25.0 3.6 %collective-permute-start.2 = (bf16[1536,384]{1,0:T(8,128)(2,1)S(1)}, bf16[1536,384]{1,0:T(8,128)(2,1)S(1)}, u32[]{:S(2)}, u32[]{:S(2)}) collective-permute-start(bf16[1536,384]{1,0:T(8,128)(2,1)S(1)} %get-tuple-element.103), channel_id=1, source_target_pairs={{0,1},{1,0},{2,3},{3,2},{4,5},{5,4},{6,7},{7,6},{8,9},{9,8},{10,11... | collective-permute-start | bytes 3538952 | tf_op jit(solution)/shard_map/ppermute | solution.py:897
  28.1 3.8 %collective-permute-start.5 = (bf16[464,384]{1,0:T(8,128)(2,1)S(1)}, bf16[464,384]{1,0:T(8,128)(2,1)S(1)}, u32[]{:S(2)}, u32[]{:S(2)}) collective-permute-start(bf16[464,384]{1,0:T(8,128)(2,1)S(1)} %get-tuple-element.130), channel_id=1, source_target_pairs={{0,1},{1,0},{2,3},{3,2},{4,5},{5,4},{6,7},{7,6},{8,9},{9,8},{10,11... | collective-permute-start | bytes 1069064 | tf_op jit(solution)/shard_map/ppermute | solution.py:897
  28.9 10.2 %collective-permute-start.3 = (bf16[392,384]{1,0:T(8,128)(2,1)S(1)}, bf16[392,384]{1,0:T(8,128)(2,1)S(1)}, u32[]{:S(2)}, u32[]{:S(2)}) collective-permute-start(bf16[392,384]{1,0:T(8,128)(2,1)S(1)} %get-tuple-element.107.after_ref), channel_id=1, source_target_pairs={{0,2},{2,0},{4,6},{6,4},{8,10},{10,8},{12,14},{14,12},{16,18},{18,... | collective-permute-start | bytes 903176 | tf_op jit(solution)/shard_map/ppermute | solution.py:944
  30.4 8.7 %collective-permute-start.4 = (bf16[384,384]{1,0:T(8,128)(2,1)S(1)}, bf16[384,384]{1,0:T(8,128)(2,1)S(1)}, u32[]{:S(2)}, u32[]{:S(2)}) collective-permute-start(bf16[384,384]{1,0:T(8,128)(2,1)S(1)} %get-tuple-element.108.after_too_ref), channel_id=1, source_target_pairs={{0,4},{2,6},{4,0},{6,2},{8,12},{10,14},{12,8},{14,10},{16,20},{18,... | collective-permute-start | bytes 884744 | tf_op jit(solution)/shard_map/ppermute | solution.py:944
  37.7 3.6 %collective-permute-start.9 = (bf16[424,384]{1,0:T(8,128)(2,1)S(1)}, bf16[424,384]{1,0:T(8,128)(2,1)S(1)}, u32[]{:S(2)}, u32[]{:S(2)}) collective-permute-start(bf16[424,384]{1,0:T(8,128)(2,1)S(1)} %get-tuple-element.137), channel_id=1, source_target_pairs={{0,1},{1,0},{2,3},{3,2},{4,5},{5,4},{6,7},{7,6},{8,9},{9,8},{10,11... | collective-permute-start | bytes 976904 | tf_op jit(solution)/shard_map/ppermute | solution.py:897
  37.8 3.5 %collective-permute-start.8 = (bf16[416,384]{1,0:T(8,128)(2,1)S(1)}, bf16[416,384]{1,0:T(8,128)(2,1)S(1)}, u32[]{:S(2)}, u32[]{:S(2)}) collective-permute-start(bf16[416,384]{1,0:T(8,128)(2,1)S(1)} %get-tuple-element.136), channel_id=1, source_target_pairs={{0,1},{1,0},{2,3},{3,2},{4,5},{5,4},{6,7},{7,6},{8,9},{9,8},{10,11... | collective-permute-start | bytes 958472 | tf_op jit(solution)/shard_map/ppermute | solution.py:897
  39.2 8.3 %collective-permute-start.6 = (bf16[208,384]{1,0:T(8,128)(2,1)S(1)}, bf16[208,384]{1,0:T(8,128)(2,1)S(1)}, u32[]{:S(2)}, u32[]{:S(2)}) collective-permute-start(bf16[208,384]{1,0:T(8,128)(2,1)S(1)} %get-tuple-element.133.refs_0_), channel_id=1, source_target_pairs={{0,4},{2,6},{4,0},{6,2},{8,12},{10,14},{12,8},{14,10},{16,20},{18,... | collective-permute-start | bytes 479240 | tf_op jit(solution)/shard_map/ppermute | solution.py:944
  40.8 6.8 %collective-permute-start.7 = (bf16[192,384]{1,0:T(8,128)(2,1)S(1)}, bf16[192,384]{1,0:T(8,128)(2,1)S(1)}, u32[]{:S(2)}, u32[]{:S(2)}) collective-permute-start(bf16[192,384]{1,0:T(8,128)(2,1)S(1)} %get-tuple-element.134), channel_id=1, source_target_pairs={{0,2},{2,0},{4,6},{6,4},{8,10},{10,8},{12,14},{14,12},{16,18},{18,... | collective-permute-start | bytes 442376 | tf_op jit(solution)/shard_map/ppermute | solution.py:944
  41.6 10.2 %collective-permute-start.13 = (bf16[216,384]{1,0:T(8,128)(2,1)S(1)}, bf16[216,384]{1,0:T(8,128)(2,1)S(1)}, u32[]{:S(2)}, u32[]{:S(2)}) collective-permute-start(bf16[216,384]{1,0:T(8,128)(2,1)S(1)} %get-tuple-element.152), channel_id=1, source_target_pairs={{0,6},{2,4},{4,2},{6,0},{8,14},{10,12},{12,10},{14,8},{16,22},{18,... | collective-permute-start | bytes 497672 | tf_op jit(solution)/shard_map/ppermute | solution.py:944
  43.1 9.3 %collective-permute-start.14 = (bf16[216,384]{1,0:T(8,128)(2,1)S(1)}, bf16[216,384]{1,0:T(8,128)(2,1)S(1)}, u32[]{:S(2)}, u32[]{:S(2)}) collective-permute-start(bf16[216,384]{1,0:T(8,128)(2,1)S(1)} %get-tuple-element.153), channel_id=1, source_target_pairs={{0,2},{2,0},{4,6},{6,4},{8,10},{10,8},{12,14},{14,12},{16,18},{18,... | collective-permute-start | bytes 497672 | tf_op jit(solution)/shard_map/ppermute | solution.py:944
  43.7 8.8 %collective-permute-start.15 = (bf16[216,384]{1,0:T(8,128)(2,1)S(1)}, bf16[216,384]{1,0:T(8,128)(2,1)S(1)}, u32[]{:S(2)}, u32[]{:S(2)}) collective-permute-start(bf16[216,384]{1,0:T(8,128)(2,1)S(1)} %get-tuple-element.140.refs_3_), channel_id=1, source_target_pairs={{0,4},{2,6},{4,0},{6,2},{8,12},{10,14},{12,8},{14,10},{16,20},{18,... | collective-permute-start | bytes 497672 | tf_op jit(solution)/shard_map/ppermute | solution.py:944
  47.9 8.6 %collective-permute-start.10 = (bf16[104,384]{1,0:T(8,128)(2,1)S(1)}, bf16[104,384]{1,0:T(8,128)(2,1)S(1)}, u32[]{:S(2)}, u32[]{:S(2)}) collective-permute-start(bf16[104,384]{1,0:T(8,128)(2,1)S(1)} %get-tuple-element.143), channel_id=1, source_target_pairs={{0,16},{2,18},{4,20},{6,22},{8,24},{10,26},{12,28},{14,30},{16,0},... | collective-permute-start | bytes 239624 | tf_op jit(solution)/shard_map/ppermute | solution.py:944
  50.2 7.0 %collective-permute-start.11 = (bf16[104,384]{1,0:T(8,128)(2,1)S(1)}, bf16[104,384]{1,0:T(8,128)(2,1)S(1)}, u32[]{:S(2)}, u32[]{:S(2)}) collective-permute-start(bf16[104,384]{1,0:T(8,128)(2,1)S(1)} %get-tuple-element.144), channel_id=1, source_target_pairs={{0,24},{2,26},{4,28},{6,30},{8,16},{10,18},{12,20},{14,22},{16,8},... | collective-permute-start | bytes 239624 | tf_op jit(solution)/shard_map/ppermute | solution.py:944
  51.7 5.5 %collective-permute-start.12 = (bf16[104,384]{1,0:T(8,128)(2,1)S(1)}, bf16[104,384]{1,0:T(8,128)(2,1)S(1)}, u32[]{:S(2)}, u32[]{:S(2)}) collective-permute-start(bf16[104,384]{1,0:T(8,128)(2,1)S(1)} %get-tuple-element.145), channel_id=1, source_target_pairs={{0,8},{2,10},{4,12},{6,14},{8,0},{10,2},{12,4},{14,6},{16,24},{18,... | collective-permute-start | bytes 239624 | tf_op jit(solution)/shard_map/ppermute | solution.py:944
  52.7 9.5 %collective-permute-start.16 = (bf16[104,384]{1,0:T(8,128)(2,1)S(1)}, bf16[104,384]{1,0:T(8,128)(2,1)S(1)}, u32[]{:S(2)}, u32[]{:S(2)}) collective-permute-start(bf16[104,384]{1,0:T(8,128)(2,1)S(1)} %get-tuple-element.155), channel_id=1, source_target_pairs={{0,16},{2,18},{4,20},{6,22},{8,24},{10,26},{12,28},{14,30},{16,0},... | collective-permute-start | bytes 239624 | tf_op jit(solution)/shard_map/ppermute | solution.py:944
  55.1 7.1 %collective-permute-start.17 = (bf16[104,384]{1,0:T(8,128)(2,1)S(1)}, bf16[104,384]{1,0:T(8,128)(2,1)S(1)}, u32[]{:S(2)}, u32[]{:S(2)}) collective-permute-start(bf16[104,384]{1,0:T(8,128)(2,1)S(1)} %get-tuple-element.156), channel_id=1, source_target_pairs={{0,24},{2,26},{4,28},{6,30},{8,16},{10,18},{12,20},{14,22},{16,8},... | collective-permute-start | bytes 239624 | tf_op jit(solution)/shard_map/ppermute | solution.py:944
  56.5 6.0 %collective-permute-start.18 = (bf16[104,384]{1,0:T(8,128)(2,1)S(1)}, bf16[104,384]{1,0:T(8,128)(2,1)S(1)}, u32[]{:S(2)}, u32[]{:S(2)}) collective-permute-start(bf16[104,384]{1,0:T(8,128)(2,1)S(1)} %get-tuple-element.157), channel_id=1, source_target_pairs={{0,8},{2,10},{4,12},{6,14},{8,0},{10,2},{12,4},{14,6},{16,24},{18,... | collective-permute-start | bytes 239624 | tf_op jit(solution)/shard_map/ppermute | solution.py:944
  62.5 2.3 %copy-start = (bf16[2,384]{1,0:T(2,128)(2,1)S(1)}, bf16[2,384]{1,0:T(2,128)(2,1)}, u32[]{:S(2)}) copy-start(bf16[2,384]{1,0:T(2,128)(2,1)} %own_cond_ref.1) | copy-start | bytes 4612
  63.6 1.2 %collective-permute-start.19 = (f32[8,384]{1,0:T(8,128)S(1)}, f32[8,384]{1,0:T(8,128)S(1)}, u32[]{:S(2)}, u32[]{:S(2)}) collective-permute-start(f32[8,384]{1,0:T(8,128)S(1)} %get-tuple-element.160.after_ref), channel_id=1, source_target_pairs={{0,1},{1,0},{2,3},{3,2},{4,5},{5,4},{6,7},{7,6},{8,9},{9,8},{10,11... | collective-permute-start | bytes 36872 | tf_op jit(solution)/shard_map/ppermute | solution.py:897

commit v6 on v5

--- a/solution.py
+++ b/solution.py
@@ -403,6 +403,7 @@
     keep_ref,
     send_ref,
     small_ref,
+    far_ref,
     gattn_ref,
 ):
     core = lax.axis_index("seq")
@@ -440,10 +441,9 @@
     out_second = jnp.concatenate([out_term[:half, half:], out_term[half:, half:]], axis=1)
     keep_ref[...] = jnp.where(core == 0, out_first, out_second)
     send_ref[:half, :] = jnp.where(core == 0, out_second, out_first).astype(LOW)
-    send_ref[half : half + 16, :] = small_ref[...].astype(LOW)
+    send_ref[half:, :] = small_ref[...].astype(LOW)
     for image in range(image_count):
-        start = half + 16 + image * half_len
-        send_ref[start : start + half_len, :] = output_ref[image, half_len:, :]
+        far_ref[image] = output_ref[image, half_len:, :]
 
 
 def backward_kernel(
@@ -524,13 +524,13 @@
     keep_ref[width:, :] = jnp.where(core == 0, low_unit, high_unit)
     cut = send_ref.shape[0] - half_len
     send_ref[:cut, :] = pair[:cut]
-    send_ref[cut:, :] = grad_tokens_ref[0, half_len:, :]
     start = width - cut
     other_ref[:start, :] = pair[cut:]
     other_ref[start : start + half, :] = jnp.where(core == 0, high_unit, low_unit).astype(LOW)
     start += half
     other_ref[start : start + 8, :] = small_ref[...].astype(LOW)
-    other_ref[start + 8 :, :] = grad_tokens_ref[1, half_len:, :]
+    for index, (target, start) in enumerate(((send_ref, cut), (other_ref, start + 8))):
+        target[start:, :] = grad_tokens_ref[index, half_len:, :]
 
 
 def by_core(core, near, far):
@@ -538,8 +538,17 @@
 
 
 def split_kernel(
-    keep_ref, recv_ref, marks_ref, own_up_ref, own_down_ref, send_up_ref, send_down_ref
+    keep_ref,
+    recv_ref,
+    marks_ref,
+    out_ref,
+    own_up_ref,
+    own_down_ref,
+    send_up_ref,
+    send_down_ref,
+    send_out_ref,
 ):
+    send_out_ref[...] = out_ref[...]
     width = keep_ref.shape[1]
     piece = width // 16
     long = 4 * piece
@@ -734,7 +743,7 @@
     two_ref,
     three_ref,
     lead_ref,
-    recv_out_ref,
+    recv_far_ref,
     recv_two_ref,
     recv_other_ref,
     output_ref,
@@ -757,9 +766,8 @@
     pairs = []
     for index in range(count):
         slot = (1 - core) * count + index
-        start = recv_out_ref.shape[0] - (count - index) * half_len
-        pairs.append((recv_out_ref.at[pl.ds(start, half_len)], output_to.at[slot]))
         source = (recv_two_ref, recv_other_ref)[index]
+        pairs.append((recv_far_ref.at[index], output_to.at[slot]))
         start = source.shape[0] - half_len
         pairs.append((source.at[pl.ds(start, half_len)], grad_tokens_to.at[slot]))
         slot = core * count + index
@@ -956,7 +964,8 @@
     width, mod_width = ada_weight.shape
     half = width // 2
     (keep_one, send_one), (keep_out, send_out), (keep_two, send_two, send_other) = sides
-    output, grad_tokens = heads
+    output, output_far, grad_tokens = heads
+    output_far = swap_cores(output_far)
     small_one, small_two = smalls
     half_len = output.shape[1] // 2
     recv_out = swap_cores(send_out)
@@ -971,7 +980,6 @@
     second_sum = keep_two + jnp.concatenate(
         [recv_two[:PIECE_ROWS], recv_other[: keep_two.shape[0] - PIECE_ROWS]], axis=0
     ).astype(F32)
-    output_far = recv_out[half + 16 :].reshape(-1, half_len, width)
     grad_far = jnp.stack([item[-half_len:] for item in (recv_two, recv_other)])
     ff_half = first_sum.shape[0] - 2 * width - half
     up = jnp.concatenate([first_sum[:width], first_sum[width : 2 * width]], axis=1)
@@ -1200,7 +1208,7 @@
         up_weight,
         down_weight,
     )
-    output, grad_att, grad_mid, keep_out, send_out, small_one = call(
+    output, grad_att, grad_mid, keep_out, send_out, small_one, output_far = call(
         finish_forward_kernel,
         "norm_back",
         (
@@ -1208,12 +1216,13 @@
             ((row_count, width), LOW),
             ((row_count, width), F32),
             ((half, width), F32),
-            ((half + 16 + row_count // 2, width), LOW),
+            ((half + 16, width), LOW),
             ((16, width), F32),
+            (half_shape, LOW),
         ),
         [vmem((row_count, width), LOW)],
         16,
-        ("V" * 13, "V" * 6),
+        ("V" * 13, "V" * 7),
         image_mod,
         att,
         middle,
@@ -1267,7 +1276,7 @@
             dp_rank,
             ((keep_one, send_one), (keep_out, send_out), (keep_two, send_two, send_other)),
             (small_one, small_two),
-            (output, grad_tokens),
+            (output, output_far, grad_tokens),
             cond_blocks[::-1].reshape(-1, width),
             cond,
             own_ids,
@@ -1275,9 +1284,8 @@
         )
 
     recv_one = swap_cores(send_one)
-    recv_out = swap_cores(send_out)
     block_rows = 8 * piece
-    own_up, own_down, sent_up, sent_down = call(
+    own_up, own_down, sent_up, sent_down, sent_out = call(
         split_kernel,
         "split_plane",
         (
@@ -1285,14 +1293,17 @@
             ((2 * block_rows, width), F32),
             ((2 * block_rows + 8, width), LOW),
             ((2 * block_rows, width), LOW),
+            ((half + 16, width), LOW),
         ),
         [],
         16,
-        ("VVV", "VVVV"),
+        ("VVVV", "VVVVV"),
         keep_one,
         recv_one,
         marks,
-    )
+        send_out,
+    )
+    recv_out = swap_cores(sent_out)
     near_up, near_down = rank_swap(sent_up, 1, 16), rank_swap(sent_down, 2, 16)
     grad_tokens, keep_two, send_two, send_other, small_two = attention_back(
         sent_up, sent_down, recv_out
@@ -1317,6 +1328,7 @@
     )
     near_up, near_down = rank_swap(cross_up, 2, 16), rank_swap(cross_down, 1, 16)
     recv_two, recv_other = swap_cores(send_two), swap_cores(send_other)
+    recv_far = swap_cores(output_far)
     split_rows = 8 * piece + 24
     own_qkv, *sent_qkv = call(
         split_qkv_kernel,
@@ -1324,7 +1336,7 @@
         (((split_rows, width), F32),) + (((split_rows, width), LOW),) * 3,
         [vmem((2 * width, width), F32)],
         16,
-        ("VVVVVVVa", "VVVV"),
+        ("VVVVVVVaa", "VVVV"),
         keep_two,
         recv_two,
         recv_other,
@@ -1333,6 +1345,7 @@
         recv_out,
         small_one,
         cross_up,
+        recv_far,
     )
     near_qkv = [rank_swap(item, step, 16) for step, item in zip(PLANE_STEPS, sent_qkv)]
     line_rows = 4 * piece + 8
@@ -1379,7 +1392,7 @@
         rest_ids,
         *lines,
         lead,
-        recv_out,
+        recv_far,
         recv_two,
         recv_other,
         output,

time: 65.7 us -> 65.5 us (level)
    ppermute x7 -> x8, starting transfers between devices: 1.79 us -> 1.87 us  [swap_cores(): return lax.ppermute(values, 'seq', CORE_SWAP)]
  transfers between devices with their start and end apart: 21 -> 22, of which waited for: 7 -> 8; matrix products, arithmetic and copies ran while one was open for 2% -> 2% of each run, Pallas kernels for 22% -> 22%
where the time goes in v6:
time: 65.5 us; the launch traced here: 65.3 us
  starting transfers between devices  29 us (44%)
  Pallas kernels  25.9 us (40%)
  waiting for transfers between devices  7.69 us (12%)
  between operations  1.42 us (2%)
  local copies, waits for them, and re-layouts  1.31 us (2%)
    pallas_call x13, Pallas kernels, call(): pl.pallas_call(kernel, out_shape=tuple((pinned.get(kind, jax.ShapeDtypeSt...  25.9 us
    ppermute x13, starting transfers between devices, rank_swap(): lax.ppermute(values, 'dp', [(rank, rank ^ step) for rank in range(count)])  16.9 us
    all_to_all x1, starting transfers between devices, body(): lax.all_to_all(jnp.broadcast_to(cond[None], (dp_count,) + cond.shape), 'd...  10.3 us
    ppermute x13, waiting for transfers between devices, rank_swap(): lax.ppermute(values, 'dp', [(rank, rank ^ step) for rank in range(count)])  7.26 us
    ppermute x8, starting transfers between devices, swap_cores(): return lax.ppermute(values, 'seq', CORE_SWAP)  1.87 us
  transfers between devices with their start and end apart: 22, of which 8 were waited for; matrix products, arithmetic and copies ran while one was open for 2% of the time, Pallas kernels for 22%

profile of v6, /device:TPU:0, one launch (start us, length us, event | category | flops | bytes accessed | tf_op | source)
XLA Modules:
  0.0 65.3 jit_solution(13656770256012859418)
XLA Ops:
  0.6 0.5 collective-permute-start
  1.2 0.1 collective-permute-start.1
  1.2 1.3 %broadcast_in_dim.2 = bf16[16,2,384]{2,1,0:T(2,128)(2,1)} broadcast(bf16[2,384]{1,0:T(2,128)(2,1)} %own_cond_ref.1), dimensions={1,2} | broadcast | bytes 26112 | tf_op jit(solution)/shard_map/broadcast_in_dim | solution.py:1075
  2.5 10.3 %all-to-all-start = ((bf16[16,2,384]{2,1,0:T(2,128)(2,1)}), bf16[16,2,384]{2,1,0:T(2,128)(2,1)S(1)}, u32[]{:S(2)}, u32[]{:S(2)}) async-start(bf16[16,2,384]{2,1,0:T(2,128)(2,1)} %broadcast_in_dim.2), calls=%async_computation | async-start | bytes 49152 | tf_op jit(solution)/shard_map/all_to_all | solution.py:1074
  13.5 0.0 collective-permute-done.tokens_far_ref
  13.5 1.7 %load.1 = (bf16[2,256,384]{2,1,0:T(8,128)(2,1)S(1)}, f32[8,256]{1,0:T(8,128)S(1)}, bf16[8,128]{1,0:T(8,128)(2,1)S(1)}, f32[8,384]{1,0:T(8,128)S(1)}, f32[1,1152]...) custom-call(bf16[4,128,384]{2,1,0:T(8,128)(2,1)} %tokens_hbm.1, ...), custom_call_target="tpu_custom_call" | custom-call | flops 1 | bytes 1 | tf_op jit(solution)/shard_map/load/pallas_call | solution.py:935
  15.2 0.1 all-to-all-done.cond_ref
  15.3 0.0 collective-permute-done.1.cot_far_ref
  15.3 9.7 %forward_and_ffn_grads.1 = (bf16[512,1152]{1,0:T(8,128)(2,1)S(1)}, bf16[512,384]{1,0:T(8,128)(2,1)S(1)}, f32[512,384]{1,0:T(8,128)S(1)}, f32[512,128]{1,0:T(8,12...) custom-call(bf16[16,2,384]{2,1,0:T(2,128)(2,1)S(1)} %all-to-all-done, ...), custom_call_target="tpu_custom_call" | custom-call | flops 1 | bytes 1 | tf_op jit(solution)/shard_map/forward_and_ffn_grads/pallas_call | solution.py:935
  25.0 0.1 collective-permute-start.2
  25.1 2.9 %norm_back.1 = (bf16[2,256,384]{2,1,0:T(8,128)(2,1)S(1)}, bf16[512,384]{1,0:T(8,128)(2,1)S(1)}, f32[512,384]{1,0:T(8,128)S(1)}, f32[192,384]{1,0:T(8,128)S(1)}, ...) custom-call(bf16[8,2304]{1,0:T(8,128)(2,1)S(1)} %get-tuple-element.107.mod_ref, ...), custom_call_target="tpu_custom_call" | custom-call | flops 1 | bytes 1 | tf_op jit(solution)/shard_map/norm_back/pallas_call | solution.py:935
  28.0 0.3 split_plane.1
  28.3 0.6 collective-permute-start.5
  28.9 1.5 %collective-permute-start.3 = (bf16[392,384]{1,0:T(8,128)(2,1)S(1)}, bf16[392,384]{1,0:T(8,128)(2,1)S(1)}, u32[]{:S(2)}, u32[]{:S(2)}) collective-permute-start(bf16[392,384]{1,0:T(8,128)(2,1)S(1)} %get-tuple-element.123.after_ref), channel_id=1, source_target_pairs={{0,2},{2,0},{4,6},{6,4},{8,10},{10,8},{12,14},{14,12},{16,18},{18,... | collective-permute-start | bytes 903176 | tf_op jit(solution)/shard_map/ppermute | solution.py:952
  30.3 1.4 %collective-permute-start.4 = (bf16[384,384]{1,0:T(8,128)(2,1)S(1)}, bf16[384,384]{1,0:T(8,128)(2,1)S(1)}, u32[]{:S(2)}, u32[]{:S(2)}) collective-permute-start(bf16[384,384]{1,0:T(8,128)(2,1)S(1)} %get-tuple-element.124.after_too_ref), channel_id=1, source_target_pairs={{0,4},{2,6},{4,0},{6,2},{8,12},{10,14},{12,8},{14,10},{16,20},{18,... | collective-permute-start | bytes 884744 | tf_op jit(solution)/shard_map/ppermute | solution.py:952
  31.8 0.0 collective-permute-done.5.after_all_ref.recv_out_ref
  31.8 5.8 %attention_back.1 = (bf16[2,256,384]{2,1,0:T(8,128)(2,1)S(1)}, f32[576,384]{1,0:T(8,128)S(1)}, bf16[416,384]{1,0:T(8,128)(2,1)S(1)}, bf16[424,384]{1,0:T(8,128)(2,1)S(1)}, f32[8,384]{1,0:T(8,128)S(1)}) custom-call(f32[512,384]{1,0:T(8,128)S(1)} %get-tuple-element.125.normed_ref, f32[512,128]{1,0:T(8,128)S(1)} %get-tuple-element.126.inverse_ref, ...), custom_call_target="tpu_custom_call" | custom-call | flops 1 | bytes 1 | tf_op jit(solution)/shard_map/attention_back/pallas_call | solution.py:935
  37.6 0.1 collective-permute-start.9
  37.7 0.5 collective-permute-start.8
  38.2 0.1 collective-permute-start.10
  38.3 0.8 %collective-permute-done.4.recv_down_ref = bf16[384,384]{1,0:T(8,128)(2,1)S(1)} collective-permute-done((bf16[384,384]{1,0:T(8,128)(2,1)S(1)}, bf16[384,384]{1,0:T(8,128)(2,1)S(1)}, u32[]{:S(2)}, u32[]{:S(2)}) %collective-permute-start.4) | collective-permute-done | bytes 294944 | tf_op jit(solution)/shard_map/ppermute | solution.py:952
  39.1 0.0 collective-permute-done.3.recv_up_ref
  39.1 0.1 cross_plane.1
  39.2 1.5 %collective-permute-start.6 = (bf16[208,384]{1,0:T(8,128)(2,1)S(1)}, bf16[208,384]{1,0:T(8,128)(2,1)S(1)}, u32[]{:S(2)}, u32[]{:S(2)}) collective-permute-start(bf16[208,384]{1,0:T(8,128)(2,1)S(1)} %get-tuple-element.136.refs_0_), channel_id=1, source_target_pairs={{0,4},{2,6},{4,0},{6,2},{8,12},{10,14},{12,8},{14,10},{16,20},{18,... | collective-permute-start | bytes 479240 | tf_op jit(solution)/shard_map/ppermute | solution.py:952
  40.7 0.6 collective-permute-start.7
  41.3 0.2 split_qkv_plane.1
  41.5 1.6 %collective-permute-start.14 = (bf16[216,384]{1,0:T(8,128)(2,1)S(1)}, bf16[216,384]{1,0:T(8,128)(2,1)S(1)}, u32[]{:S(2)}, u32[]{:S(2)}) collective-permute-start(bf16[216,384]{1,0:T(8,128)(2,1)S(1)} %get-tuple-element.156), channel_id=1, source_target_pairs={{0,6},{2,4},{4,2},{6,0},{8,14},{10,12},{12,10},{14,8},{16,22},{18,... | collective-permute-start | bytes 497672 | tf_op jit(solution)/shard_map/ppermute | solution.py:952
  43.1 0.6 collective-permute-start.15
  43.6 1.4 %collective-permute-start.16 = (bf16[216,384]{1,0:T(8,128)(2,1)S(1)}, bf16[216,384]{1,0:T(8,128)(2,1)S(1)}, u32[]{:S(2)}, u32[]{:S(2)}) collective-permute-start(bf16[216,384]{1,0:T(8,128)(2,1)S(1)} %get-tuple-element.144.refs_3_), channel_id=1, source_target_pairs={{0,4},{2,6},{4,0},{6,2},{8,12},{10,14},{12,8},{14,10},{16,20},{18,... | collective-permute-start | bytes 497672 | tf_op jit(solution)/shard_map/ppermute | solution.py:952
  45.1 2.4 %collective-permute-done.7.refs_2_ = bf16[192,384]{1,0:T(8,128)(2,1)S(1)} collective-permute-done((bf16[192,384]{1,0:T(8,128)(2,1)S(1)}, bf16[192,384]{1,0:T(8,128)(2,1)S(1)}, u32[]{:S(2)}, u32[]{:S(2)}) %collective-permute-start.7) | collective-permute-done | bytes 147488 | tf_op jit(solution)/shard_map/ppermute | solution.py:952
  47.5 0.0 collective-permute-done.6.refs_1_
  47.5 0.3 fold_plane.1
  47.8 2.4 %collective-permute-start.11 = (bf16[104,384]{1,0:T(8,128)(2,1)S(1)}, bf16[104,384]{1,0:T(8,128)(2,1)S(1)}, u32[]{:S(2)}, u32[]{:S(2)}) collective-permute-start(bf16[104,384]{1,0:T(8,128)(2,1)S(1)} %get-tuple-element.147), channel_id=1, source_target_pairs={{0,16},{2,18},{4,20},{6,22},{8,24},{10,26},{12,28},{14,30},{16,0},... | collective-permute-start | bytes 239624 | tf_op jit(solution)/shard_map/ppermute | solution.py:952
  50.2 1.5 %collective-permute-start.12 = (bf16[104,384]{1,0:T(8,128)(2,1)S(1)}, bf16[104,384]{1,0:T(8,128)(2,1)S(1)}, u32[]{:S(2)}, u32[]{:S(2)}) collective-permute-start(bf16[104,384]{1,0:T(8,128)(2,1)S(1)} %get-tuple-element.148), channel_id=1, source_target_pairs={{0,24},{2,26},{4,28},{6,30},{8,16},{10,18},{12,20},{14,22},{16,8},... | collective-permute-start | bytes 239624 | tf_op jit(solution)/shard_map/ppermute | solution.py:952
  51.7 0.8 %collective-permute-start.13 = (bf16[104,384]{1,0:T(8,128)(2,1)S(1)}, bf16[104,384]{1,0:T(8,128)(2,1)S(1)}, u32[]{:S(2)}, u32[]{:S(2)}) collective-permute-start(bf16[104,384]{1,0:T(8,128)(2,1)S(1)} %get-tuple-element.149), channel_id=1, source_target_pairs={{0,8},{2,10},{4,12},{6,14},{8,0},{10,2},{12,4},{14,6},{16,24},{18,... | collective-permute-start | bytes 239624 | tf_op jit(solution)/shard_map/ppermute | solution.py:952
  52.5 0.0 collective-permute-done.16.refs_3_
  52.5 0.3 fold_qkv_plane.1
  52.8 2.4 %collective-permute-start.17 = (bf16[104,384]{1,0:T(8,128)(2,1)S(1)}, bf16[104,384]{1,0:T(8,128)(2,1)S(1)}, u32[]{:S(2)}, u32[]{:S(2)}) collective-permute-start(bf16[104,384]{1,0:T(8,128)(2,1)S(1)} %get-tuple-element.159), channel_id=1, source_target_pairs={{0,16},{2,18},{4,20},{6,22},{8,24},{10,26},{12,28},{14,30},{16,0},... | collective-permute-start | bytes 239624 | tf_op jit(solution)/shard_map/ppermute | solution.py:952
  55.2 1.2 %collective-permute-start.18 = (bf16[104,384]{1,0:T(8,128)(2,1)S(1)}, bf16[104,384]{1,0:T(8,128)(2,1)S(1)}, u32[]{:S(2)}, u32[]{:S(2)}) collective-permute-start(bf16[104,384]{1,0:T(8,128)(2,1)S(1)} %get-tuple-element.160), channel_id=1, source_target_pairs={{0,24},{2,26},{4,28},{6,30},{8,16},{10,18},{12,20},{14,22},{16,8},... | collective-permute-start | bytes 239624 | tf_op jit(solution)/shard_map/ppermute | solution.py:952
  56.4 0.4 collective-permute-done.12.two_ref
  56.9 0.4 collective-permute-done.13.three_ref
  57.2 1.8 %finish_line.1 = (bf16[4,128,384]{2,1,0:T(8,128)(2,1)}, bf16[4,128,384]{2,1,0:T(8,128)(2,1)}, f32[24,768]{1,0:T(8,128)}, f32[96,192]{1,0:T(8,128)}, bf16[24,192]{1,0:T(8,128)(2,1)S(1)}, /*index=5*/s32[1,192]{1,0:T(1,128)S(1)}) custom-call(f32[96,384]{1,0:T(8,128)S(1)} %get-tuple-element.145.own_ref, bf16[8,384]{1,0:T(8,128)(2,1)S(1)} %get-tuple-element.146.own_small_ref, ...), custom_call_target="tpu_custom_call" | custom-call | flops 1 | bytes 1 | tf_op jit(solution)/shard_map/finish_line/pallas_call | solution.py:935
  59.1 2.8 %collective-permute-done.17.one_ref = bf16[104,384]{1,0:T(8,128)(2,1)S(1)} collective-permute-done((bf16[104,384]{1,0:T(8,128)(2,1)S(1)}, bf16[104,384]{1,0:T(8,128)(2,1)S(1)}, u32[]{:S(2)}, u32[]{:S(2)}) %collective-permute-start.17) | collective-permute-done | bytes 79904 | tf_op jit(solution)/shard_map/ppermute | solution.py:952
  61.9 0.4 collective-permute-done.19.three_ref
  62.3 1.1 %late_groups.1 = (bf16[4,48,384]{2,1,0:T(8,128)(2,1)S(1)}, f32[8,384]{1,0:T(8,128)S(1)}, f32[8,384]{1,0:T(8,128)S(1)}, f32[384]{0:T(512)}, f32[1536]{0:T(1024)}, /*index=5*/f32[384]{0:T(512)}, f32[2,384]{1,0:T(2,128)}) custom-call(bf16[56,384]{1,0:T(8,128)(2,1)S(1)} %get-tuple-element.158.own_small_ref, ...), custom_call_target="tpu_custom_call" | custom-call | flops 1 | bytes 1 | tf_op jit(solution)/shard_map/late_groups/pallas_call | solution.py:935
  63.4 0.9 %rest_sums.1 = (f32[24,192]{1,0:T(8,128)}, f32[24,576]{1,0:T(8,128)}, f32[24,1152]{1,0:T(8,128)}) custom-call(f32[48,384]{1,0:T(8,128)S(1)} %get-tuple-element.166.own_ref, bf16[104,384]{1,0:T(8,128)(2,1)S(1)} %collective-permute-done.17.one_ref, bf16[104,384]{1,0:T(8,128)(2,1)S(1)} %collective-permute-done.18.two_ref, ...), custom_call_target="tpu_custom_call" | custom-call | flops 1 | bytes 1 | tf_op jit(solution)/shard_map/rest_sums/pallas_call | solution.py:935
  64.3 0.3 collective-permute-done.20.recv_ref
  64.6 0.7 %final_groups.1 = (f32[2,192]{1,0:T(2,128)}, f32[2304]{0:T(1024)}) custom-call(f32[8,384]{1,0:T(8,128)S(1)} %get-tuple-element.163.own_ref, f32[8,384]{1,0:T(8,128)S(1)} %collective-permute-done.20.recv_ref, bf16[2,384]{1,0:T(2,128)(2,1)S(1)} %copy-done), custom_call_target="tpu_custom_call" | custom-call | flops 1 | bytes 1 | tf_op jit(solution)/shard_map/final_groups/pallas_call | solution.py:935
  (12 shorter events, 0.0 us)
Async XLA Ops:
  0.6 12.8 %collective-permute-start = (bf16[4,128,384]{2,1,0:T(8,128)(2,1)}, bf16[4,128,384]{2,1,0:T(8,128)(2,1)S(1)}, u32[]{:S(2)}, u32[]{:S(2)}) collective-permute-start(bf16[4,128,384]{2,1,0:T(8,128)(2,1)} %tokens_hbm.1), channel_id=1, source_target_pairs={{0,1},{1,0},{2,3},{3,2},{4,5},{5,4},{6,7},{7,6},{8,9},{9,8},{10,11... | collective-permute-start | bytes 1179656 | tf_op jit(solution)/shard_map/ppermute | solution.py:905
  1.2 14.2 %collective-permute-start.1 = (bf16[4,128,384]{2,1,0:T(8,128)(2,1)}, bf16[4,128,384]{2,1,0:T(8,128)(2,1)S(1)}, u32[]{:S(2)}, u32[]{:S(2)}) collective-permute-start(bf16[4,128,384]{2,1,0:T(8,128)(2,1)} %cot_hbm.1), channel_id=1, source_target_pairs={{0,1},{1,0},{2,3},{3,2},{4,5},{5,4},{6,7},{7,6},{8,9},{9,8},{10,11... | collective-permute-start | bytes 1179656 | tf_op jit(solution)/shard_map/ppermute | solution.py:905
  2.5 12.8 %all-to-all-start = ((bf16[16,2,384]{2,1,0:T(2,128)(2,1)}), bf16[16,2,384]{2,1,0:T(2,128)(2,1)S(1)}, u32[]{:S(2)}, u32[]{:S(2)}) async-start(bf16[16,2,384]{2,1,0:T(2,128)(2,1)} %broadcast_in_dim.2), calls=%async_computation | async-start | bytes 49152 | tf_op jit(solution)/shard_map/all_to_all | solution.py:1074
  25.0 3.0 %collective-permute-start.2 = (bf16[1536,384]{1,0:T(8,128)(2,1)S(1)}, bf16[1536,384]{1,0:T(8,128)(2,1)S(1)}, u32[]{:S(2)}, u32[]{:S(2)}) collective-permute-start(bf16[1536,384]{1,0:T(8,128)(2,1)S(1)} %get-tuple-element.105), channel_id=1, source_target_pairs={{0,1},{1,0},{2,3},{3,2},{4,5},{5,4},{6,7},{7,6},{8,9},{9,8},{10,11... | collective-permute-start | bytes 3538952 | tf_op jit(solution)/shard_map/ppermute | solution.py:905
  28.3 3.5 %collective-permute-start.5 = (bf16[208,384]{1,0:T(8,128)(2,1)S(1)}, bf16[208,384]{1,0:T(8,128)(2,1)S(1)}, u32[]{:S(2)}, u32[]{:S(2)}) collective-permute-start(bf16[208,384]{1,0:T(8,128)(2,1)S(1)} %get-tuple-element.133), channel_id=1, source_target_pairs={{0,1},{1,0},{2,3},{3,2},{4,5},{5,4},{6,7},{7,6},{8,9},{9,8},{10,11... | collective-permute-start | bytes 479240 | tf_op jit(solution)/shard_map/ppermute | solution.py:905
  28.9 10.2 %collective-permute-start.3 = (bf16[392,384]{1,0:T(8,128)(2,1)S(1)}, bf16[392,384]{1,0:T(8,128)(2,1)S(1)}, u32[]{:S(2)}, u32[]{:S(2)}) collective-permute-start(bf16[392,384]{1,0:T(8,128)(2,1)S(1)} %get-tuple-element.123.after_ref), channel_id=1, source_target_pairs={{0,2},{2,0},{4,6},{6,4},{8,10},{10,8},{12,14},{14,12},{16,18},{18,... | collective-permute-start | bytes 903176 | tf_op jit(solution)/shard_map/ppermute | solution.py:952
  30.3 8.7 %collective-permute-start.4 = (bf16[384,384]{1,0:T(8,128)(2,1)S(1)}, bf16[384,384]{1,0:T(8,128)(2,1)S(1)}, u32[]{:S(2)}, u32[]{:S(2)}) collective-permute-start(bf16[384,384]{1,0:T(8,128)(2,1)S(1)} %get-tuple-element.124.after_too_ref), channel_id=1, source_target_pairs={{0,4},{2,6},{4,0},{6,2},{8,12},{10,14},{12,8},{14,10},{16,20},{18,... | collective-permute-start | bytes 884744 | tf_op jit(solution)/shard_map/ppermute | solution.py:952
  37.6 3.7 %collective-permute-start.9 = (bf16[424,384]{1,0:T(8,128)(2,1)S(1)}, bf16[424,384]{1,0:T(8,128)(2,1)S(1)}, u32[]{:S(2)}, u32[]{:S(2)}) collective-permute-start(bf16[424,384]{1,0:T(8,128)(2,1)S(1)} %get-tuple-element.140), channel_id=1, source_target_pairs={{0,1},{1,0},{2,3},{3,2},{4,5},{5,4},{6,7},{7,6},{8,9},{9,8},{10,11... | collective-permute-start | bytes 976904 | tf_op jit(solution)/shard_map/ppermute | solution.py:905
  37.7 3.6 %collective-permute-start.8 = (bf16[416,384]{1,0:T(8,128)(2,1)S(1)}, bf16[416,384]{1,0:T(8,128)(2,1)S(1)}, u32[]{:S(2)}, u32[]{:S(2)}) collective-permute-start(bf16[416,384]{1,0:T(8,128)(2,1)S(1)} %get-tuple-element.139), channel_id=1, source_target_pairs={{0,1},{1,0},{2,3},{3,2},{4,5},{5,4},{6,7},{7,6},{8,9},{9,8},{10,11... | collective-permute-start | bytes 958472 | tf_op jit(solution)/shard_map/ppermute | solution.py:905
  38.2 3.1 %collective-permute-start.10 = (bf16[2,128,384]{2,1,0:T(8,128)(2,1)S(1)}, bf16[2,128,384]{2,1,0:T(8,128)(2,1)S(1)}, u32[]{:S(2)}, u32[]{:S(2)}) collective-permute-start(bf16[2,128,384]{2,1,0:T(8,128)(2,1)S(1)} %get-tuple-element.143), channel_id=1, source_target_pairs={{0,1},{1,0},{2,3},{3,2},{4,5},{5,4},{6,7},{7,6},{8,9},{9,8},{10,11... | collective-permute-start | bytes 589832 | tf_op jit(solution)/shard_map/ppermute | solution.py:905
  39.2 8.3 %collective-permute-start.6 = (bf16[208,384]{1,0:T(8,128)(2,1)S(1)}, bf16[208,384]{1,0:T(8,128)(2,1)S(1)}, u32[]{:S(2)}, u32[]{:S(2)}) collective-permute-start(bf16[208,384]{1,0:T(8,128)(2,1)S(1)} %get-tuple-element.136.refs_0_), channel_id=1, source_target_pairs={{0,4},{2,6},{4,0},{6,2},{8,12},{10,14},{12,8},{14,10},{16,20},{18,... | collective-permute-start | bytes 479240 | tf_op jit(solution)/shard_map/ppermute | solution.py:952
  40.7 6.8 %collective-permute-start.7 = (bf16[192,384]{1,0:T(8,128)(2,1)S(1)}, bf16[192,384]{1,0:T(8,128)(2,1)S(1)}, u32[]{:S(2)}, u32[]{:S(2)}) collective-permute-start(bf16[192,384]{1,0:T(8,128)(2,1)S(1)} %get-tuple-element.137), channel_id=1, source_target_pairs={{0,2},{2,0},{4,6},{6,4},{8,10},{10,8},{12,14},{14,12},{16,18},{18,... | collective-permute-start | bytes 442376 | tf_op jit(solution)/shard_map/ppermute | solution.py:952
  41.5 10.2 %collective-permute-start.14 = (bf16[216,384]{1,0:T(8,128)(2,1)S(1)}, bf16[216,384]{1,0:T(8,128)(2,1)S(1)}, u32[]{:S(2)}, u32[]{:S(2)}) collective-permute-start(bf16[216,384]{1,0:T(8,128)(2,1)S(1)} %get-tuple-element.156), channel_id=1, source_target_pairs={{0,6},{2,4},{4,2},{6,0},{8,14},{10,12},{12,10},{14,8},{16,22},{18,... | collective-permute-start | bytes 497672 | tf_op jit(solution)/shard_map/ppermute | solution.py:952
  43.1 9.5 %collective-permute-start.15 = (bf16[216,384]{1,0:T(8,128)(2,1)S(1)}, bf16[216,384]{1,0:T(8,128)(2,1)S(1)}, u32[]{:S(2)}, u32[]{:S(2)}) collective-permute-start(bf16[216,384]{1,0:T(8,128)(2,1)S(1)} %get-tuple-element.157), channel_id=1, source_target_pairs={{0,2},{2,0},{4,6},{6,4},{8,10},{10,8},{12,14},{14,12},{16,18},{18,... | collective-permute-start | bytes 497672 | tf_op jit(solution)/shard_map/ppermute | solution.py:952
  43.6 8.9 %collective-permute-start.16 = (bf16[216,384]{1,0:T(8,128)(2,1)S(1)}, bf16[216,384]{1,0:T(8,128)(2,1)S(1)}, u32[]{:S(2)}, u32[]{:S(2)}) collective-permute-start(bf16[216,384]{1,0:T(8,128)(2,1)S(1)} %get-tuple-element.144.refs_3_), channel_id=1, source_target_pairs={{0,4},{2,6},{4,0},{6,2},{8,12},{10,14},{12,8},{14,10},{16,20},{18,... | collective-permute-start | bytes 497672 | tf_op jit(solution)/shard_map/ppermute | solution.py:952
  47.8 8.6 %collective-permute-start.11 = (bf16[104,384]{1,0:T(8,128)(2,1)S(1)}, bf16[104,384]{1,0:T(8,128)(2,1)S(1)}, u32[]{:S(2)}, u32[]{:S(2)}) collective-permute-start(bf16[104,384]{1,0:T(8,128)(2,1)S(1)} %get-tuple-element.147), channel_id=1, source_target_pairs={{0,16},{2,18},{4,20},{6,22},{8,24},{10,26},{12,28},{14,30},{16,0},... | collective-permute-start | bytes 239624 | tf_op jit(solution)/shard_map/ppermute | solution.py:952
  50.2 6.7 %collective-permute-start.12 = (bf16[104,384]{1,0:T(8,128)(2,1)S(1)}, bf16[104,384]{1,0:T(8,128)(2,1)S(1)}, u32[]{:S(2)}, u32[]{:S(2)}) collective-permute-start(bf16[104,384]{1,0:T(8,128)(2,1)S(1)} %get-tuple-element.148), channel_id=1, source_target_pairs={{0,24},{2,26},{4,28},{6,30},{8,16},{10,18},{12,20},{14,22},{16,8},... | collective-permute-start | bytes 239624 | tf_op jit(solution)/shard_map/ppermute | solution.py:952
  51.7 5.6 %collective-permute-start.13 = (bf16[104,384]{1,0:T(8,128)(2,1)S(1)}, bf16[104,384]{1,0:T(8,128)(2,1)S(1)}, u32[]{:S(2)}, u32[]{:S(2)}) collective-permute-start(bf16[104,384]{1,0:T(8,128)(2,1)S(1)} %get-tuple-element.149), channel_id=1, source_target_pairs={{0,8},{2,10},{4,12},{6,14},{8,0},{10,2},{12,4},{14,6},{16,24},{18,... | collective-permute-start | bytes 239624 | tf_op jit(solution)/shard_map/ppermute | solution.py:952
  52.8 9.1 %collective-permute-start.17 = (bf16[104,384]{1,0:T(8,128)(2,1)S(1)}, bf16[104,384]{1,0:T(8,128)(2,1)S(1)}, u32[]{:S(2)}, u32[]{:S(2)}) collective-permute-start(bf16[104,384]{1,0:T(8,128)(2,1)S(1)} %get-tuple-element.159), channel_id=1, source_target_pairs={{0,16},{2,18},{4,20},{6,22},{8,24},{10,26},{12,28},{14,30},{16,0},... | collective-permute-start | bytes 239624 | tf_op jit(solution)/shard_map/ppermute | solution.py:952
  55.2 6.7 %collective-permute-start.18 = (bf16[104,384]{1,0:T(8,128)(2,1)S(1)}, bf16[104,384]{1,0:T(8,128)(2,1)S(1)}, u32[]{:S(2)}, u32[]{:S(2)}) collective-permute-start(bf16[104,384]{1,0:T(8,128)(2,1)S(1)} %get-tuple-element.160), channel_id=1, source_target_pairs={{0,24},{2,26},{4,28},{6,30},{8,16},{10,18},{12,20},{14,22},{16,8},... | collective-permute-start | bytes 239624 | tf_op jit(solution)/shard_map/ppermute | solution.py:952
  56.4 5.9 %collective-permute-start.19 = (bf16[104,384]{1,0:T(8,128)(2,1)S(1)}, bf16[104,384]{1,0:T(8,128)(2,1)S(1)}, u32[]{:S(2)}, u32[]{:S(2)}) collective-permute-start(bf16[104,384]{1,0:T(8,128)(2,1)S(1)} %get-tuple-element.161), channel_id=1, source_target_pairs={{0,8},{2,10},{4,12},{6,14},{8,0},{10,2},{12,4},{14,6},{16,24},{18,... | collective-permute-start | bytes 239624 | tf_op jit(solution)/shard_map/ppermute | solution.py:952
  62.3 2.3 %copy-start = (bf16[2,384]{1,0:T(2,128)(2,1)S(1)}, bf16[2,384]{1,0:T(2,128)(2,1)}, u32[]{:S(2)}) copy-start(bf16[2,384]{1,0:T(2,128)(2,1)} %own_cond_ref.1) | copy-start | bytes 4612
  63.4 1.2 %collective-permute-start.20 = (f32[8,384]{1,0:T(8,128)S(1)}, f32[8,384]{1,0:T(8,128)S(1)}, u32[]{:S(2)}, u32[]{:S(2)}) collective-permute-start(f32[8,384]{1,0:T(8,128)S(1)} %get-tuple-element.164.after_ref), channel_id=1, source_target_pairs={{0,1},{1,0},{2,3},{3,2},{4,5},{5,4},{6,7},{7,6},{8,9},{9,8},{10,11... | collective-permute-start | bytes 36872 | tf_op jit(solution)/shard_map/ppermute | solution.py:905
